TPU v7x, 128 devices: a whole 4x4x4 slice. The times are simulated.
128 devices in a mesh: shot: 4 (over z), row: 8 (over x, y_lo), col: 4 (over y_hi, core).
Axes of the slice: x: 4, y: 4 (y_hi: 2, y_lo: 2; y = y_hi * 2 + y_lo), z: 4, core: 2. Of those that a mesh axis runs over, the one named last changes fastest.
Arguments:
- velocity: float32 [256, 256, 384], P(('row', 'shot'), 'col'), may hold values from 1.5 to 4.5
- momentum: float32 [256, 256, 384], P(('row', 'shot'), 'col'), may hold values from -6 to 6
- mass_diag: float32 [256, 256, 384], P(('row', 'shot'), 'col'), may hold values from 0.5 to 2
- u_prev: float32 [4, 256, 256, 384], P('shot', 'row', 'col'), may hold values from -6 to 6
- u_cur: float32 [4, 256, 256, 384], P('shot', 'row', 'col'), may hold values from -6 to 6
- adj_next: float32 [4, 256, 256, 384], P('shot', 'row', 'col'), may hold values from -6 to 6
- adj_cur: float32 [4, 256, 256, 384], P('shot', 'row', 'col'), may hold values from -6 to 6
- observed: float32 [4, 2, 256, 256], P('shot', None, 'row', 'col'), may hold values from -6 to 6
- rec_depth: int32 [4, 256, 256], P('shot', 'row', 'col'), may hold values from 0 to 383
- src_cell: int32 [4, 3], P('shot'), may hold values from 0 to 255
- wavelet: float32 [4, 2], P('shot'), may hold values from -60 to 60
Outputs:
- v_new: float32 [256, 256, 384], P(('row', 'shot'), 'col')
- p_half: float32 [256, 256, 384], P(('row', 'shot'), 'col')
All inputs are finite; a program needn't handle non-finite values.
Results may differ from a plain program's by a relative error of at most 0.0001.
Values sent between devices are 32-bit elements; how exact they have to be, the bound alone decides.
A program may use at most 128 MiB of HBM per device.

v0:
```python
import jax
import jax.numpy as jnp
from jax import lax
from jax.sharding import PartitionSpec as P

STENCIL = (-205.0 / 72.0, 8.0 / 5.0, -1.0 / 5.0, 8.0 / 315.0, -1.0 / 560.0)
squared_courant = 0.012
leap_step = 0.2


def extended(block, sides, width):
    for axis, dim in sides:
        count = lax.axis_size(axis)
        forward = [(i, i + 1) for i in range(count - 1)]
        backward = [(target, source) for source, target in forward]
        low = lax.ppermute(
            lax.slice_in_dim(block, block.shape[dim] - width, None, axis=dim), axis, forward
        )
        high = lax.ppermute(lax.slice_in_dim(block, 0, width, axis=dim), axis, backward)
        block = jnp.concatenate([low, block, high], axis=dim)
    return block


def laplace(padded):
    row_count = padded.shape[0] - 8
    col_count = padded.shape[1] - 8
    depth_cells = padded.shape[2]
    center = padded[4 : 4 + row_count, 4 : 4 + col_count]
    z_padded = jnp.pad(center, ((0, 0), (0, 0), (4, 4)))
    result = 3.0 * STENCIL[0] * center
    for offset in range(1, 5):
        along = (
            padded[4 + offset : 4 + offset + row_count, 4 : 4 + col_count]
            + padded[4 - offset : 4 - offset + row_count, 4 : 4 + col_count]
        )
        along = (
            along
            + padded[4 : 4 + row_count, 4 + offset : 4 + offset + col_count]
            + padded[4 : 4 + row_count, 4 - offset : 4 - offset + col_count]
        )
        along = (
            along
            + z_padded[:, :, 4 + offset : 4 + offset + depth_cells]
            + z_padded[:, :, 4 - offset : 4 - offset + depth_cells]
        )
        result = result + STENCIL[offset] * along
    return result


def with_faces(field):
    return extended(field, (("row", 0), ("col", 1)), 4)


def on_device(
    velocity,
    momentum,
    mass_diag,
    u_prev,
    u_cur,
    adj_next,
    adj_cur,
    observed,
    rec_depth,
    src_cell,
    wavelet,
):
    full_velocity = lax.all_gather(velocity, "shot", axis=0, tiled=True)
    stiffness = squared_courant * full_velocity * full_velocity
    row_count, col_count, depth_cells = full_velocity.shape
    oldest = u_prev[0]
    present = u_cur[0]
    adj_later = adj_next[0]
    adj_now = adj_cur[0]
    padded_wave = extended(present, (("row", 0), ("col", 1)), 4)
    padded_adjoint = extended(adj_now, (("row", 0), ("col", 1)), 4)
    x_index = lax.iota(jnp.int32, row_count) + lax.axis_index("row") * row_count
    y_index = lax.iota(jnp.int32, col_count) + lax.axis_index("col") * col_count
    z_index = lax.iota(jnp.int32, depth_cells)
    cell = src_cell[0]
    source_mask = (
        (x_index == cell[0])[:, None, None]
        & (y_index == cell[1])[None, :, None]
        & (z_index == cell[2])[None, None, :]
    ).astype(jnp.float32)
    advanced = (
        2.0 * present - oldest + stiffness * laplace(padded_wave) + wavelet[0, 0] * source_mask
    )
    farthest = (
        2.0 * advanced
        - present
        + stiffness * laplace(with_faces(advanced))
        + wavelet[0, 1] * source_mask
    )
    receiver_mask = (z_index[None, None, :] == rec_depth[0][:, :, None]).astype(jnp.float32)
    misfit_late = jnp.sum(farthest * receiver_mask, axis=2) - observed[0, 1]
    misfit_early = jnp.sum(advanced * receiver_mask, axis=2) - observed[0, 0]
    adj_two = (
        2.0 * adj_now
        - adj_later
        + stiffness * laplace(padded_adjoint)
        + misfit_late[:, :, None] * receiver_mask
    )
    adj_one = (
        2.0 * adj_two
        - adj_now
        + stiffness * laplace(with_faces(adj_two))
        + misfit_early[:, :, None] * receiver_mask
    )
    imaging = adj_two * (farthest - 2.0 * advanced + present) + adj_one * (
        advanced - 2.0 * present + oldest
    )
    share_rows = velocity.shape[0]
    full_sum = lax.psum(imaging, "shot")
    summed = lax.dynamic_slice_in_dim(full_sum, lax.axis_index("shot") * share_rows, share_rows, 0)
    gradient = 2.0 / velocity * summed
    p_half = momentum - 0.5 * leap_step * gradient
    v_new = velocity + leap_step * p_half / mass_diag
    return (v_new, p_half)


def solution(mesh):
    return jax.shard_map(
        on_device,
        mesh=mesh,
        in_specs=(
            P(("row", "shot"), "col", None),
            P(("row", "shot"), "col", None),
            P(("row", "shot"), "col", None),
            P("shot", "row", "col", None),
            P("shot", "row", "col", None),
            P("shot", "row", "col", None),
            P("shot", "row", "col", None),
            P("shot", None, "row", "col"),
            P("shot", "row", "col"),
            P("shot", None),
            P("shot", None),
        ),
        out_specs=(P(("row", "shot"), "col", None), P(("row", "shot"), "col", None)),
        check_vma=False,
    )
```

profile of v0, /device:TPU:1, one launch (start us, length us, event | category | flops | bytes accessed | tf_op | source)
XLA Modules:
  0.0 376.6 jit_solution(13717517673409891883)
XLA Ops:
  7.2 0.0 copy-start
  7.2 0.0 all-gather.2.cloned.1.call-start
  7.2 0.7 all-gather.2.cloned.1.call-update
  7.9 0.0 all-reduce.6.cloned.1.call-start
  8.0 2.2 slice_bitcast_fusion.3
  10.2 1.3 collective-permute-start
  11.5 5.4 %collective-permute-start.1 = (f32[4,64,384]{2,1,0:T(8,128)}, f32[4,64,384]{2,1,0:T(8,128)}, u32[]{:S(2)}, u32[]{:S(2)}) collective-permute-start(f32[4,64,384]{2,1,0:T(8,128)} %get-tuple-element.30), channel_id=1, source_target_pairs={{0,4},{4,8},{8,12},{12,16},{16,20},{20,24},{24,28},{1,5},{5,9},{9,... | collective-permute-start | bytes 1179656 | tf_op jit(solution)/shard_map/ppermute | solution.py:16
  16.9 2.1 slice_bitcast_fusion.1
  19.0 1.3 collective-permute-start.4
  20.3 4.9 %collective-permute-start.5 = (f32[4,64,384]{2,1,0:T(8,128)}, f32[4,64,384]{2,1,0:T(8,128)}, u32[]{:S(2)}, u32[]{:S(2)}) collective-permute-start(f32[4,64,384]{2,1,0:T(8,128)} %get-tuple-element.28), channel_id=1, source_target_pairs={{0,4},{4,8},{8,12},{12,16},{16,20},{20,24},{24,28},{1,5},{5,9},{9,... | collective-permute-start | bytes 1179656 | tf_op jit(solution)/shard_map/ppermute | solution.py:16
  25.2 0.7 fusion.146
  25.9 0.6 iota_compare_fusion.1
  26.5 0.6 add_compare_fusion.1
  27.1 0.6 fusion.145
  27.7 3.3 collective-permute-done.4
  31.0 18.5 %collective-permute-done.5 = f32[4,64,384]{2,1,0:T(8,128)} collective-permute-done((f32[4,64,384]{2,1,0:T(8,128)}, f32[4,64,384]{2,1,0:T(8,128)}, u32[]{:S(2)}, u32[]{:S(2)}) %collective-permute-start.5) | collective-permute-done | bytes 393248 | tf_op jit(solution)/shard_map/ppermute | solution.py:16
  49.5 1.0 pad_maximum_fusion.20
  50.5 2.4 collective-permute-start.6
  52.9 4.7 %collective-permute-start.7 = (f32[40,4,384]{2,1,0:T(4,128)S(1)}, f32[40,4,384]{2,1,0:T(4,128)S(1)}, u32[]{:S(2)}, u32[]{:S(2)}) collective-permute-start(f32[40,4,384]{2,1,0:T(4,128)S(1)} %get-tuple-element.18), channel_id=1, source_target_pairs={{0,1},{1,2},{2,3},{4,5},{5,6},{6,7},{8,9},{9,10},{10,11},{12,13},{... | collective-permute-start | bytes 737288 | tf_op jit(solution)/shard_map/ppermute | solution.py:16
  57.6 0.7 add_compare_fusion
  58.3 0.1 broadcast_and_fusion
  58.3 1.2 collective-permute-done.6
  59.5 1.2 collective-permute-done.7
  60.7 5.9 %pad_maximum_fusion.1 = (f32[40,68,384]{2,1,0:T(8,128)}, f32[40,68,384]{2,1,0:T(8,128)}) fusion(f32[40,4,384]{2,1,0:T(4,128)S(1)} %collective-permute-done.6, f32[4,64,384]{2,1,0:T(8,128)} %collective-permute-done.4, f32[32,64,384]{2,1,0:T(8,128)S(1)} %bitcast.36, f32[4,64,384]{2,1,0:T(8,128)} %collective-permute-done.5, ...), kind=kLoop, calls=%fused_computation.59 | loop fusion | flops 6266880 | bytes 12779520 | tf_op jit(solution)/shard_map/concatenate | solution.py:20
  66.6 23.5 %fusion.75 = f32[32,64,384]{2,1,0:T(8,128)} fusion(f32[32,64,384]{2,1,0:T(8,128)S(1)} %bitcast.37, f32[4,64,384]{2,1,0:T(8,128)} %collective-permute-done.5, f32[4,64,384]{2,1,0:T(8,128)} %collective-permute-done.4, f32[40,68,384]{2,1,0:T(8,128)} %get-tuple-element.16, f32[40,68,384]{2,1,0:T(8,128)} %get-tuple-element.15, f32[1,32,64,384]{3,2,1,0:T(8,128)} %param.14, ...), kind=kLoop, calls=%fused_computation.166 | loop fusion | flops 36175872 | bytes 38537604 | tf_op jit(solution)/shard_map/add | solution.py:86
  90.1 1.3 fusion.144
  91.5 4.1 %collective-permute-start.9 = (f32[4,64,384]{2,1,0:T(8,128)S(1)}, f32[4,64,384]{2,1,0:T(8,128)S(1)}, u32[]{:S(2)}, u32[]{:S(2)}) collective-permute-start(f32[4,64,384]{2,1,0:T(8,128)S(1)} %get-tuple-element.25), channel_id=1, source_target_pairs={{0,4},{4,8},{8,12},{12,16},{16,20},{20,24},{24,28},{1,5},{5,9},{9,... | collective-permute-start | bytes 1179656 | tf_op jit(solution)/shard_map/ppermute | solution.py:16
  95.6 1.3 collective-permute-start.8
  96.9 0.0 collective-permute-done
  96.9 0.0 collective-permute-done.1
  96.9 1.2 pad_maximum_fusion.23
  98.1 0.0 copy-start.3
  98.2 2.2 collective-permute-start.2
  100.3 6.8 %collective-permute-start.3 = (f32[40,4,384]{2,1,0:T(4,128)S(1)}, f32[40,4,384]{2,1,0:T(4,128)S(1)}, u32[]{:S(2)}, u32[]{:S(2)}) collective-permute-start(f32[40,4,384]{2,1,0:T(4,128)S(1)} %get-tuple-element.22), channel_id=1, source_target_pairs={{0,1},{1,2},{2,3},{4,5},{5,6},{6,7},{8,9},{9,10},{10,11},{12,13},{... | collective-permute-start | bytes 737288 | tf_op jit(solution)/shard_map/ppermute | solution.py:16
  107.1 2.0 collective-permute-done.9
  109.1 0.0 collective-permute-done.8
  109.2 0.1 pad_maximum_fusion.17
  109.2 1.9 collective-permute-start.10
  111.2 5.3 %collective-permute-start.11 = (f32[40,4,384]{2,1,0:T(4,128)S(1)}, f32[40,4,384]{2,1,0:T(4,128)S(1)}, u32[]{:S(2)}, u32[]{:S(2)}) collective-permute-start(f32[40,4,384]{2,1,0:T(4,128)S(1)} %get-tuple-element.14), channel_id=1, source_target_pairs={{0,1},{1,2},{2,3},{4,5},{5,6},{6,7},{8,9},{9,10},{10,11},{12,13},{... | collective-permute-start | bytes 737288 | tf_op jit(solution)/shard_map/ppermute | solution.py:16
  116.5 5.8 %pad_maximum_fusion = (f32[40,68,384]{2,1,0:T(8,128)}, f32[40,68,384]{2,1,0:T(8,128)}) fusion(f32[40,4,384]{2,1,0:T(4,128)S(1)} %collective-permute-done.2, f32[4,64,384]{2,1,0:T(8,128)S(1)} %collective-permute-done, f32[32,64,384]{2,1,0:T(8,128)S(1)} %bitcast.40, f32[4,64,384]{2,1,0:T(8,128)} %collective-permute-done.1, ...), kind=kLoop, calls=%fused_computation.57 | loop fusion | flops 6266880 | bytes 12779520 | tf_op jit(solution)/shard_map/concatenate | solution.py:20
  122.3 0.0 collective-permute-done.11
  122.4 4.7 %pad_maximum_fusion.2 = (f32[40,68,384]{2,1,0:T(8,128)}, f32[40,68,384]{2,1,0:T(8,128)}) fusion(f32[40,4,384]{2,1,0:T(4,128)S(1)} %collective-permute-done.10, f32[4,64,384]{2,1,0:T(8,128)S(1)} %collective-permute-done.8, f32[32,64,384]{2,1,0:T(8,128)S(1)} %copy-done.1, f32[4,64,384]{2,1,0:T(8,128)S(1)} %collective-permute-done.9, ...), kind=kLoop, calls=%fused_computation.61 | loop fusion | flops 6266880 | bytes 12779520 | tf_op jit(solution)/shard_map/concatenate | solution.py:20
  127.0 45.6 %select_reduce_fusion = (f32[32,64]{1,0:T(8,128)}, f32[32,64]{1,0:T(8,128)}, f32[32,64,384]{2,1,0:T(8,128)}) fusion(f32[32,64,384]{2,1,0:T(8,128)} %fusion.75, s32[32,64]{1,0:T(8,128)S(1)} %bitcast.41, f32[]{:T(128)} %bitcast.13, pred[384]{0:T(512)(128)(4,1)} %copy-done.15, pred[32,64]{1,0:T(8,128)(4,1)} %copy-done.13, ...), kind=kLoop, calls=%fused_computation.252 | loop fusion | flops 40103936 | bytes 38562180 | tf_op jit(solution)/shard_map/reduce_sum | solution.py:96
  172.6 1.4 bitcast_subtract_fusion.2
  174.0 43.2 %fusion.106 = f32[32,64,384]{2,1,0:T(8,128)} fusion(f32[32,64,384]{2,1,0:T(8,128)} %bitcast.39, f32[4,64,384]{2,1,0:T(8,128)} %collective-permute-done.1, f32[4,64,384]{2,1,0:T(8,128)S(1)} %collective-permute-done, f32[40,68,384]{2,1,0:T(8,128)} %get-tuple-element.20, f32[40,68,384]{2,1,0:T(8,128)} %get-tuple-element.19, f32[1,32,64,384]{3,2,1,0:T(8,128)} %param.16, ...), kind=kLoop, calls=%fused_computation.197 | loop fusion | flops 36175872 | bytes 38551552 | tf_op jit(solution)/shard_map/add | solution.py:98
  217.2 1.3 fusion.143
  218.5 1.3 collective-permute-start.12
  219.8 4.5 %collective-permute-start.13 = (f32[4,64,384]{2,1,0:T(8,128)S(1)}, f32[4,64,384]{2,1,0:T(8,128)S(1)}, u32[]{:S(2)}, u32[]{:S(2)}) collective-permute-start(f32[4,64,384]{2,1,0:T(8,128)S(1)} %get-tuple-element.24), channel_id=1, source_target_pairs={{0,4},{4,8},{8,12},{12,16},{16,20},{20,24},{24,28},{1,5},{5,9},{9,... | collective-permute-start | bytes 1179656 | tf_op jit(solution)/shard_map/ppermute | solution.py:16
  224.3 4.9 %collective-permute-done.12 = f32[4,64,384]{2,1,0:T(8,128)S(1)} collective-permute-done((f32[4,64,384]{2,1,0:T(8,128)S(1)}, f32[4,64,384]{2,1,0:T(8,128)S(1)}, u32[]{:S(2)}, u32[]{:S(2)}) %collective-permute-start.12) | collective-permute-done | bytes 393248 | tf_op jit(solution)/shard_map/ppermute | solution.py:19
  229.2 9.2 %collective-permute-done.13 = f32[4,64,384]{2,1,0:T(8,128)S(1)} collective-permute-done((f32[4,64,384]{2,1,0:T(8,128)S(1)}, f32[4,64,384]{2,1,0:T(8,128)S(1)}, u32[]{:S(2)}, u32[]{:S(2)}) %collective-permute-start.13) | collective-permute-done | bytes 393248 | tf_op jit(solution)/shard_map/ppermute | solution.py:16
  238.5 1.3 pad_maximum_fusion.14
  239.8 2.1 collective-permute-start.14
  241.9 0.0 copy-start.12
  241.9 5.4 %collective-permute-start.15 = (f32[40,4,384]{2,1,0:T(4,128)S(1)}, f32[40,4,384]{2,1,0:T(4,128)S(1)}, u32[]{:S(2)}, u32[]{:S(2)}) collective-permute-start(f32[40,4,384]{2,1,0:T(4,128)S(1)} %get-tuple-element.10), channel_id=1, source_target_pairs={{0,1},{1,2},{2,3},{4,5},{5,6},{6,7},{8,9},{9,10},{10,11},{12,13},{... | collective-permute-start | bytes 737288 | tf_op jit(solution)/shard_map/ppermute | solution.py:16
  247.4 1.4 collective-permute-done.14
  248.8 1.5 collective-permute-done.15
  250.3 3.7 pad_maximum_fusion.3
  254.0 32.6 %fusion.13 = f32[32,64,384]{2,1,0:T(8,128)} fusion(f32[32,64,384]{2,1,0:T(8,128)} %fusion.106, f32[4,64,384]{2,1,0:T(8,128)} %copy-done.7, f32[4,64,384]{2,1,0:T(8,128)S(1)} %collective-permute-done.12, f32[40,68,384]{2,1,0:T(8,128)} %get-tuple-element.8, f32[40,68,384]{2,1,0:T(8,128)S(1)} %get-tuple-element.7, f32[1,32,64,384]{3,2,1,0:T(8,128)} %param.14, ...), kind=kLoop, calls=%fused_computation.104 | loop fusion | flops 43253760 | bytes 51134464 | tf_op jit(solution)/shard_map/add | solution.py:109
  286.6 0.0 copy-start.8
  286.6 0.0 copy-start.9
  286.6 0.0 copy-start.10
  286.6 0.0 all-reduce.6.cloned.1.call-update
  286.6 80.5 %all-reduce.6.cloned.1.call-done = f32[32,64,384]{2,1,0:T(8,128)} async-done(((f32[32,64,384]{2,1,0:T(8,128)}), f32[32,64,384]{2,1,0:T(8,128)}) %all-reduce.6.cloned.1.call-update) | async-done | bytes 3145744 | tf_op jit(solution)/shard_map/psum | solution.py:113
  367.2 2.6 divide_add_fusion
  (32 shorter events, 0.1 us)
Async XLA Ops:
  7.2 42.4 %copy-start = (f32[1,32,64,384]{3,2,1,0:T(8,128)S(1)}, f32[1,32,64,384]{3,2,1,0:T(8,128)}, u32[]{:S(2)}) copy-start(f32[1,32,64,384]{3,2,1,0:T(8,128)} %param.15) | copy-start | bytes 9437188
  7.2 18.1 %copy-start.14 = (s32[1,3]{1,0:T(1,128)S(1)}, s32[1,3]{1,0:T(1,128)}, u32[]{:S(2)}) copy-start(s32[1,3]{1,0:T(1,128)} %param.20) | copy-start | bytes 40
  7.2 19.9 %copy-start.16 = (f32[1,2]{1,0:T(1,128)S(1)}, f32[1,2]{1,0:T(1,128)}, u32[]{:S(2)}) copy-start(f32[1,2]{1,0:T(1,128)} %param.21) | copy-start | bytes 28
  7.2 59.4 %all-gather.2.cloned.1.call-start = ((), (), s32[]{:S(2)}) async-start(), calls=%async_computation | async-start | bytes 3932160 | tf_op jit(solution)/shard_map/all_gather | solution.py:67
  7.9 359.2 %all-reduce.6.cloned.1.call-start = ((), (), s32[]{:S(2)}) async-start(), calls=%async_computation.1 | async-start | bytes 6291456 | tf_op jit(solution)/shard_map/psum | solution.py:113
  10.2 86.7 %collective-permute-start = (f32[4,64,384]{2,1,0:T(8,128)}, f32[4,64,384]{2,1,0:T(8,128)S(1)}, u32[]{:S(2)}, u32[]{:S(2)}) collective-permute-start(f32[4,64,384]{2,1,0:T(8,128)} %get-tuple-element.29), channel_id=1, source_target_pairs={{4,0},{8,4},{12,8},{16,12},{20,16},{24,20},{28,24},{5,1},{9,5},{13... | collective-permute-start | bytes 1179656 | tf_op jit(solution)/shard_map/ppermute | solution.py:19
  11.5 85.4 %collective-permute-start.1 = (f32[4,64,384]{2,1,0:T(8,128)}, f32[4,64,384]{2,1,0:T(8,128)}, u32[]{:S(2)}, u32[]{:S(2)}) collective-permute-start(f32[4,64,384]{2,1,0:T(8,128)} %get-tuple-element.30), channel_id=1, source_target_pairs={{0,4},{4,8},{8,12},{12,16},{16,20},{20,24},{24,28},{1,5},{5,9},{9,... | collective-permute-start | bytes 1179656 | tf_op jit(solution)/shard_map/ppermute | solution.py:16
  19.0 12.0 %collective-permute-start.4 = (f32[4,64,384]{2,1,0:T(8,128)}, f32[4,64,384]{2,1,0:T(8,128)}, u32[]{:S(2)}, u32[]{:S(2)}) collective-permute-start(f32[4,64,384]{2,1,0:T(8,128)} %get-tuple-element.27), channel_id=1, source_target_pairs={{4,0},{8,4},{12,8},{16,12},{20,16},{24,20},{28,24},{5,1},{9,5},{13... | collective-permute-start | bytes 1179656 | tf_op jit(solution)/shard_map/ppermute | solution.py:19
  20.3 29.2 %collective-permute-start.5 = (f32[4,64,384]{2,1,0:T(8,128)}, f32[4,64,384]{2,1,0:T(8,128)}, u32[]{:S(2)}, u32[]{:S(2)}) collective-permute-start(f32[4,64,384]{2,1,0:T(8,128)} %get-tuple-element.28), channel_id=1, source_target_pairs={{0,4},{4,8},{8,12},{12,16},{16,20},{20,24},{24,28},{1,5},{5,9},{9,... | collective-permute-start | bytes 1179656 | tf_op jit(solution)/shard_map/ppermute | solution.py:16
  26.5 40.2 %copy-start.15 = (pred[384]{0:T(512)(128)(4,1)}, pred[384]{0:T(512)(128)(4,1)S(1)}, u32[]{:S(2)}) copy-start(pred[384]{0:T(512)(128)(4,1)S(1)} %iota_compare_fusion.1) | copy-start | bytes 1156
  50.5 9.0 %collective-permute-start.6 = (f32[40,4,384]{2,1,0:T(4,128)S(1)}, f32[40,4,384]{2,1,0:T(4,128)S(1)}, u32[]{:S(2)}, u32[]{:S(2)}) collective-permute-start(f32[40,4,384]{2,1,0:T(4,128)S(1)} %get-tuple-element.17), channel_id=1, source_target_pairs={{1,0},{2,1},{3,2},{5,4},{6,5},{7,6},{9,8},{10,9},{11,10},{13,12},{... | collective-permute-start | bytes 737288 | tf_op jit(solution)/shard_map/ppermute | solution.py:19
  52.9 7.8 %collective-permute-start.7 = (f32[40,4,384]{2,1,0:T(4,128)S(1)}, f32[40,4,384]{2,1,0:T(4,128)S(1)}, u32[]{:S(2)}, u32[]{:S(2)}) collective-permute-start(f32[40,4,384]{2,1,0:T(4,128)S(1)} %get-tuple-element.18), channel_id=1, source_target_pairs={{0,1},{1,2},{2,3},{4,5},{5,6},{6,7},{8,9},{9,10},{10,11},{12,13},{... | collective-permute-start | bytes 737288 | tf_op jit(solution)/shard_map/ppermute | solution.py:16
  58.3 8.3 %copy-start.13 = (pred[32,64]{1,0:T(8,128)(4,1)}, pred[32,64]{1,0:T(8,128)(4,1)S(1)}, u32[]{:S(2)}) copy-start(pred[32,64]{1,0:T(8,128)(4,1)S(1)} %broadcast_and_fusion) | copy-start | bytes 6148
  90.1 19.0 %copy-start.1 = (f32[32,64,384]{2,1,0:T(8,128)S(1)}, f32[32,64,384]{2,1,0:T(8,128)}, u32[]{:S(2)}) copy-start(f32[32,64,384]{2,1,0:T(8,128)} %fusion.75) | copy-start | bytes 9437188
  91.5 17.7 %collective-permute-start.9 = (f32[4,64,384]{2,1,0:T(8,128)S(1)}, f32[4,64,384]{2,1,0:T(8,128)S(1)}, u32[]{:S(2)}, u32[]{:S(2)}) collective-permute-start(f32[4,64,384]{2,1,0:T(8,128)S(1)} %get-tuple-element.25), channel_id=1, source_target_pairs={{0,4},{4,8},{8,12},{12,16},{16,20},{20,24},{24,28},{1,5},{5,9},{9,... | collective-permute-start | bytes 1179656 | tf_op jit(solution)/shard_map/ppermute | solution.py:16
  95.6 13.5 %collective-permute-start.8 = (f32[4,64,384]{2,1,0:T(8,128)S(1)}, f32[4,64,384]{2,1,0:T(8,128)S(1)}, u32[]{:S(2)}, u32[]{:S(2)}) collective-permute-start(f32[4,64,384]{2,1,0:T(8,128)S(1)} %get-tuple-element.26), channel_id=1, source_target_pairs={{4,0},{8,4},{12,8},{16,12},{20,16},{24,20},{28,24},{5,1},{9,5},{13... | collective-permute-start | bytes 1179656 | tf_op jit(solution)/shard_map/ppermute | solution.py:19
  98.1 18.4 %copy-start.3 = (f32[1,32,64,384]{3,2,1,0:T(8,128)S(1)}, f32[1,32,64,384]{3,2,1,0:T(8,128)}, u32[]{:S(2)}) copy-start(f32[1,32,64,384]{3,2,1,0:T(8,128)} %param.17) | copy-start | bytes 9437188
  98.2 18.4 %collective-permute-start.2 = (f32[40,4,384]{2,1,0:T(4,128)S(1)}, f32[40,4,384]{2,1,0:T(4,128)S(1)}, u32[]{:S(2)}, u32[]{:S(2)}) collective-permute-start(f32[40,4,384]{2,1,0:T(4,128)S(1)} %get-tuple-element.21), channel_id=1, source_target_pairs={{1,0},{2,1},{3,2},{5,4},{6,5},{7,6},{9,8},{10,9},{11,10},{13,12},{... | collective-permute-start | bytes 737288 | tf_op jit(solution)/shard_map/ppermute | solution.py:19
  100.3 16.2 %collective-permute-start.3 = (f32[40,4,384]{2,1,0:T(4,128)S(1)}, f32[40,4,384]{2,1,0:T(4,128)S(1)}, u32[]{:S(2)}, u32[]{:S(2)}) collective-permute-start(f32[40,4,384]{2,1,0:T(4,128)S(1)} %get-tuple-element.22), channel_id=1, source_target_pairs={{0,1},{1,2},{2,3},{4,5},{5,6},{6,7},{8,9},{9,10},{10,11},{12,13},{... | collective-permute-start | bytes 737288 | tf_op jit(solution)/shard_map/ppermute | solution.py:16
  109.1 13.2 %copy-start.5 = (f32[4,64,384]{2,1,0:T(8,128)}, f32[4,64,384]{2,1,0:T(8,128)S(1)}, u32[]{:S(2)}) copy-start(f32[4,64,384]{2,1,0:T(8,128)S(1)} %collective-permute-done.9) | copy-start | bytes 1179652
  109.1 13.2 %copy-start.6 = (f32[4,64,384]{2,1,0:T(8,128)}, f32[4,64,384]{2,1,0:T(8,128)S(1)}, u32[]{:S(2)}) copy-start(f32[4,64,384]{2,1,0:T(8,128)S(1)} %collective-permute-done.8) | copy-start | bytes 1179652
  109.2 13.1 %collective-permute-start.10 = (f32[40,4,384]{2,1,0:T(4,128)S(1)}, f32[40,4,384]{2,1,0:T(4,128)S(1)}, u32[]{:S(2)}, u32[]{:S(2)}) collective-permute-start(f32[40,4,384]{2,1,0:T(4,128)S(1)} %get-tuple-element.13), channel_id=1, source_target_pairs={{1,0},{2,1},{3,2},{5,4},{6,5},{7,6},{9,8},{10,9},{11,10},{13,12},{... | collective-permute-start | bytes 737288 | tf_op jit(solution)/shard_map/ppermute | solution.py:19
  111.2 11.2 %collective-permute-start.11 = (f32[40,4,384]{2,1,0:T(4,128)S(1)}, f32[40,4,384]{2,1,0:T(4,128)S(1)}, u32[]{:S(2)}, u32[]{:S(2)}) collective-permute-start(f32[40,4,384]{2,1,0:T(4,128)S(1)} %get-tuple-element.14), channel_id=1, source_target_pairs={{0,1},{1,2},{2,3},{4,5},{5,6},{6,7},{8,9},{9,10},{10,11},{12,13},{... | collective-permute-start | bytes 737288 | tf_op jit(solution)/shard_map/ppermute | solution.py:16
  122.3 4.7 %copy-start.11 = (s32[1,32,64]{2,1,0:T(8,128)S(1)}, s32[1,32,64]{2,1,0:T(8,128)}, u32[]{:S(2)}) copy-start(s32[1,32,64]{2,1,0:T(8,128)} %param.19) | copy-start | bytes 24580
  217.2 33.1 %copy-start.4 = (f32[32,64,384]{2,1,0:T(8,128)S(1)}, f32[32,64,384]{2,1,0:T(8,128)}, u32[]{:S(2)}) copy-start(f32[32,64,384]{2,1,0:T(8,128)} %fusion.106) | copy-start | bytes 9437188
  218.5 10.7 %collective-permute-start.12 = (f32[4,64,384]{2,1,0:T(8,128)S(1)}, f32[4,64,384]{2,1,0:T(8,128)S(1)}, u32[]{:S(2)}, u32[]{:S(2)}) collective-permute-start(f32[4,64,384]{2,1,0:T(8,128)S(1)} %get-tuple-element.23), channel_id=1, source_target_pairs={{4,0},{8,4},{12,8},{16,12},{20,16},{24,20},{28,24},{5,1},{9,5},{13... | collective-permute-start | bytes 1179656 | tf_op jit(solution)/shard_map/ppermute | solution.py:19
  219.8 18.6 %collective-permute-start.13 = (f32[4,64,384]{2,1,0:T(8,128)S(1)}, f32[4,64,384]{2,1,0:T(8,128)S(1)}, u32[]{:S(2)}, u32[]{:S(2)}) collective-permute-start(f32[4,64,384]{2,1,0:T(8,128)S(1)} %get-tuple-element.24), channel_id=1, source_target_pairs={{0,4},{4,8},{8,12},{12,16},{16,20},{20,24},{24,28},{1,5},{5,9},{9,... | collective-permute-start | bytes 1179656 | tf_op jit(solution)/shard_map/ppermute | solution.py:16
  238.5 15.5 %copy-start.7 = (f32[4,64,384]{2,1,0:T(8,128)}, f32[4,64,384]{2,1,0:T(8,128)S(1)}, u32[]{:S(2)}) copy-start(f32[4,64,384]{2,1,0:T(8,128)S(1)} %collective-permute-done.13) | copy-start | bytes 1179652
  239.8 9.0 %collective-permute-start.14 = (f32[40,4,384]{2,1,0:T(4,128)S(1)}, f32[40,4,384]{2,1,0:T(4,128)S(1)}, u32[]{:S(2)}, u32[]{:S(2)}) collective-permute-start(f32[40,4,384]{2,1,0:T(4,128)S(1)} %get-tuple-element.9), channel_id=1, source_target_pairs={{1,0},{2,1},{3,2},{5,4},{6,5},{7,6},{9,8},{10,9},{11,10},{13,12},{... | collective-permute-start | bytes 737288 | tf_op jit(solution)/shard_map/ppermute | solution.py:19
  241.9 12.0 %copy-start.2 = (f32[32,64,384]{2,1,0:T(8,128)S(1)}, f32[32,64,384]{2,1,0:T(8,128)}, u32[]{:S(2)}) copy-start(f32[32,64,384]{2,1,0:T(8,128)} %fusion.75) | copy-start | bytes 9437188
  241.9 12.0 %copy-start.12 = (f32[32,64]{1,0:T(8,128)S(1)}, f32[32,64]{1,0:T(8,128)}, u32[]{:S(2)}) copy-start(f32[32,64]{1,0:T(8,128)} %get-tuple-element.31) | copy-start | bytes 24580
  241.9 8.3 %collective-permute-start.15 = (f32[40,4,384]{2,1,0:T(4,128)S(1)}, f32[40,4,384]{2,1,0:T(4,128)S(1)}, u32[]{:S(2)}, u32[]{:S(2)}) collective-permute-start(f32[40,4,384]{2,1,0:T(4,128)S(1)} %get-tuple-element.10), channel_id=1, source_target_pairs={{0,1},{1,2},{2,3},{4,5},{5,6},{6,7},{8,9},{9,10},{10,11},{12,13},{... | collective-permute-start | bytes 737288 | tf_op jit(solution)/shard_map/ppermute | solution.py:16
  286.6 80.6 %copy-start.8 = (f32[8,64,384]{2,1,0:T(8,128)S(1)}, f32[8,64,384]{2,1,0:T(8,128)}, u32[]{:S(2)}) copy-start(f32[8,64,384]{2,1,0:T(8,128)} %param.11) | copy-start | bytes 2359300
  286.6 80.6 %copy-start.9 = (f32[8,64,384]{2,1,0:T(8,128)S(1)}, f32[8,64,384]{2,1,0:T(8,128)}, u32[]{:S(2)}) copy-start(f32[8,64,384]{2,1,0:T(8,128)} %param.13) | copy-start | bytes 2359300
  286.6 80.6 %copy-start.10 = (f32[8,64,384]{2,1,0:T(8,128)S(1)}, f32[8,64,384]{2,1,0:T(8,128)}, u32[]{:S(2)}) copy-start(f32[8,64,384]{2,1,0:T(8,128)} %param.12) | copy-start | bytes 2359300
Sparse Core Ops, SparseCore 0:
  9.7 42.9 all-gather.1
  286.8 80.3 all-reduce.5
where the time goes:
time: 377 us
  other arithmetic  174 us (46%)
  waiting for transfers between devices  124 us (33%)
  starting transfers between devices  55 us (15%)
  between operations  14.4 us (4%)
  local copies, waits for them, and re-layouts  8.33 us (2%)
    psum x1, waiting for transfers between devices, on_device(): full_sum = lax.psum(imaging, 'shot')  80.5 us
    reduce_sum x1, other arithmetic, on_device(): misfit_early = jnp.sum(advanced * receiver_mask, axis=2) - observed[0, 0]  45.6 us
    add x1, other arithmetic, on_device(): 2.0 * adj_now - adj_later + stiffness * laplace(padded_adjoint)  43.2 us
    ppermute x8, starting transfers between devices, extended(): lax.ppermute(lax.slice_in_dim(block, block.shape[dim] - width, None, axis...  41.2 us
    add x1, other arithmetic, on_device(): adj_two * (farthest - 2.0 * advanced + present)  32.6 us
    ppermute x8, waiting for transfers between devices, extended(): lax.ppermute(lax.slice_in_dim(block, block.shape[dim] - width, None, axis...  32.4 us
    add x1, other arithmetic, on_device(): 2.0 * present - oldest + stiffness * laplace(padded_wave)  23.5 us
    concatenate x4, other arithmetic, extended(): block = jnp.concatenate([low, block, high], axis=dim)  20 us
  transfers between devices with their start and end apart: 18, of which 10 were waited for; matrix products, arithmetic and copies ran while one was open for 12% of the time, Pallas kernels for 0%

commit v1 on v0

v1 whole, which is shorter than its diff:
```python
import functools

import jax
import jax.numpy as jnp
from jax import lax
from jax.experimental import pallas as pl
from jax.experimental.pallas import tpu as pltpu
from jax.sharding import PartitionSpec as P

STENCIL = (-205.0 / 72.0, 8.0 / 5.0, -1.0 / 5.0, 8.0 / 315.0, -1.0 / 560.0)
squared_courant = 0.012
leap_step = 0.2

ROWS_PER_STEP = 8
Y_CHUNK = 8


def halos(block):
    out = []
    for axis, dim in (("row", 0), ("col", 1)):
        count = lax.axis_size(axis)
        forward = [(i, i + 1) for i in range(count - 1)]
        backward = [(target, source) for source, target in forward]
        size = block.shape[dim]
        low = lax.ppermute(lax.slice_in_dim(block, size - 4, None, axis=dim), axis, forward)
        high = lax.ppermute(lax.slice_in_dim(block, 0, 4, axis=dim), axis, backward)
        out += [low, high]
    xlo, xhi, ylo, yhi = out
    ylo = jnp.pad(ylo, ((0, 0), (4, 0), (0, 0)))
    yhi = jnp.pad(yhi, ((0, 0), (0, 4), (0, 0)))
    return xlo, xhi, ylo, yhi


def step_kernel(kind, *refs):
    (f_ref, flo_ref, fhi_ref, xlo_ref, xhi_ref, ylo_ref, yhi_ref, prev_ref, vel_ref, rec_ref) = refs[:10]
    rest = refs[10:]
    if kind in ("wave1", "wave2"):
        src_ref, amp_ref = rest[:2]
        rest = rest[2:]
    else:
        mis_ref = rest[0]
        rest = rest[1:]
    if kind == "adj1":
        dw_ref = rest[0]
        rest = rest[1:]
    elif kind == "adj2":
        dw_ref, part_ref = rest[:2]
        rest = rest[2:]
    outs = rest[:-1]
    pad = rest[-1]

    tb, cols, depth = f_ref.shape
    i = pl.program_id(0)
    n = pl.num_programs(0)

    lo = jnp.where(i == 0, xlo_ref[...], flo_ref[...])
    hi = jnp.where(i == n - 1, xhi_ref[...], fhi_ref[...])
    pad[0:4, 8 : 8 + cols, :] = lo
    pad[4 : 4 + tb, 8 : 8 + cols, :] = f_ref[...]
    pad[4 + tb : 8 + tb, 8 : 8 + cols, :] = hi
    pad[4 : 4 + tb, 0:8, :] = ylo_ref[...]
    pad[4 : 4 + tb, 8 + cols : 16 + cols, :] = yhi_ref[...]

    z_index = lax.broadcasted_iota(jnp.int32, (Y_CHUNK, depth), 1)
    y_index = lax.broadcasted_iota(jnp.int32, (Y_CHUNK, depth), 0)
    if kind in ("wave1", "wave2"):
        src_x = src_ref[0] - i * tb
        src_y = src_ref[1]
        src_z = src_ref[2]
        amp = amp_ref[0]

    def row(r, carry):
        for y0 in range(0, cols, Y_CHUNK):
            ys = pl.ds(8 + y0, Y_CHUNK)
            c = pad[4 + r, ys, :]
            result = (3.0 * STENCIL[0]) * c
            for k in range(1, 5):
                along = pad[4 + r + k, ys, :] + pad[4 + r - k, ys, :]
                along = along + (
                    pad[4 + r, pl.ds(8 + y0 + k, Y_CHUNK), :]
                    + pad[4 + r, pl.ds(8 + y0 - k, Y_CHUNK), :]
                )
                zp = jnp.where(z_index < depth - k, pltpu.roll(c, depth - k, 1), 0.0)
                zm = jnp.where(z_index >= k, pltpu.roll(c, k, 1), 0.0)
                along = along + (zp + zm)
                result = result + STENCIL[k] * along
            v = vel_ref[r, pl.ds(y0, Y_CHUNK), :]
            stiff = squared_courant * v * v
            prev = prev_ref[r, pl.ds(y0, Y_CHUNK), :]
            out = 2.0 * c - prev + stiff * result
            at_rec = z_index == rec_ref[r, pl.ds(y0, Y_CHUNK), :]
            if kind in ("wave1", "wave2"):
                hit = (r == src_x) & (y_index + y0 == src_y) & (z_index == src_z)
                out = out + jnp.where(hit, amp, 0.0)
                picked = jnp.sum(jnp.where(at_rec, out, 0.0), axis=1, keepdims=True)
                outs_now = [(out - 2.0 * c) + prev, picked]
                if kind == "wave1":
                    outs_now = [out] + outs_now
            else:
                out = out + jnp.where(at_rec, mis_ref[r, pl.ds(y0, Y_CHUNK), :], 0.0)
                dw = dw_ref[r, pl.ds(y0, Y_CHUNK), :]
                if kind == "adj1":
                    outs_now = [out, out * dw]
                else:
                    outs_now = [part_ref[r, pl.ds(y0, Y_CHUNK), :] + out * dw]
            for o_ref, val in zip(outs, outs_now):
                o_ref[r, pl.ds(y0, Y_CHUNK), :] = val
        return carry

    lax.fori_loop(0, tb, row, 0)


def leap(kind, f, xlo, xhi, ylo, yhi, prev, vel, rec, *extra):
    rows, cols, depth = f.shape
    tb = ROWS_PER_STEP
    grid = (rows // tb,)
    nq = rows // 4
    block = pl.BlockSpec((tb, cols, depth), lambda i: (i, 0, 0))
    lo_spec = pl.BlockSpec((4, cols, depth), lambda i: (jnp.maximum(2 * i - 1, 0), 0, 0))
    hi_spec = pl.BlockSpec((4, cols, depth), lambda i: (jnp.minimum(2 * i + 2, nq - 1), 0, 0))
    whole4 = pl.BlockSpec((4, cols, depth), lambda i: (0, 0, 0))
    yspec = pl.BlockSpec((tb, 8, depth), lambda i: (i, 0, 0))
    col1 = pl.BlockSpec((tb, cols, 1), lambda i: (i, 0, 0))
    smem = pl.BlockSpec(memory_space=pltpu.SMEM)
    in_specs = [block, lo_spec, hi_spec, whole4, whole4, yspec, yspec, block, block, col1]
    args = [f, f, f, xlo, xhi, ylo, yhi, prev, vel, rec]
    field = jax.ShapeDtypeStruct((rows, cols, depth), jnp.float32)
    picked = jax.ShapeDtypeStruct((rows, cols, 1), jnp.float32)
    if kind in ("wave1", "wave2"):
        src, amp = extra
        in_specs += [smem, smem]
        args += [src, amp]
        if kind == "wave1":
            out_shape = [field, field, picked]
            out_specs = [block, block, col1]
        else:
            out_shape = [field, picked]
            out_specs = [block, col1]
    else:
        mis = extra[0]
        in_specs += [col1] + [block] * (len(extra) - 1)
        args += list(extra)
        if kind == "adj1":
            out_shape = [field, field]
            out_specs = [block, block]
        else:
            out_shape = [field]
            out_specs = [block]
    n_in = len(args)
    cost = pl.CostEstimate(
        flops=60 * rows * cols * depth,
        transcendentals=0,
        bytes_accessed=4 * rows * cols * depth * (n_in - 4 + len(out_shape)),
    )
    return pl.pallas_call(
        functools.partial(step_kernel, kind),
        grid=grid,
        in_specs=in_specs,
        out_specs=out_specs,
        out_shape=out_shape,
        scratch_shapes=[pltpu.VMEM((tb + 8, cols + 16, depth), jnp.float32)],
        compiler_params=pltpu.CompilerParams(vmem_limit_bytes=60 * 1024 * 1024),
        cost_estimate=cost,
        name=f"leap_{kind}",
    )(*args)


def on_device(
    velocity,
    momentum,
    mass_diag,
    u_prev,
    u_cur,
    adj_next,
    adj_cur,
    observed,
    rec_depth,
    src_cell,
    wavelet,
):
    full_velocity = lax.all_gather(velocity, "shot", axis=0, tiled=True)
    row_count, col_count, depth_cells = full_velocity.shape
    oldest = u_prev[0]
    present = u_cur[0]
    adj_later = adj_next[0]
    adj_now = adj_cur[0]
    rec = rec_depth[0][:, :, None]
    cell = src_cell[0]
    src = jnp.stack(
        [
            cell[0] - lax.axis_index("row") * row_count,
            cell[1] - lax.axis_index("col") * col_count,
            cell[2],
        ]
    ).astype(jnp.int32)
    amp = wavelet[0]

    wave_h = halos(present)
    adj_h = halos(adj_now)
    advanced, dw1, pick_adv = leap("wave1", present, *wave_h, oldest, full_velocity, rec, src, amp[0:1])
    dw2, pick_far = leap("wave2", advanced, *halos(advanced), present, full_velocity, rec, src, amp[1:2])
    misfit_late = pick_far - observed[0, 1][:, :, None]
    misfit_early = pick_adv - observed[0, 0][:, :, None]
    adj_two, part = leap("adj1", adj_now, *adj_h, adj_later, full_velocity, rec, misfit_late, dw2)
    (imaging,) = leap("adj2", adj_two, *halos(adj_two), adj_now, full_velocity, rec, misfit_early, dw1, part)
    summed = lax.psum_scatter(imaging, "shot", scatter_dimension=0, tiled=True)
    gradient = 2.0 / velocity * summed
    p_half = momentum - 0.5 * leap_step * gradient
    v_new = velocity + leap_step * p_half / mass_diag
    return (v_new, p_half)


def solution(mesh):
    return jax.shard_map(
        on_device,
        mesh=mesh,
        in_specs=(
            P(("row", "shot"), "col", None),
            P(("row", "shot"), "col", None),
            P(("row", "shot"), "col", None),
            P("shot", "row", "col", None),
            P("shot", "row", "col", None),
            P("shot", "row", "col", None),
            P("shot", "row", "col", None),
            P("shot", None, "row", "col"),
            P("shot", "row", "col"),
            P("shot", None),
            P("shot", None),
        ),
        out_specs=(P(("row", "shot"), "col", None), P(("row", "shot"), "col", None)),
        check_vma=False,
    )
```

time: 377 us -> 266 us (0.71)
  other arithmetic: 174 us -> 7.35 us
  Pallas kernels: 0 us -> 88.9 us
  waiting for transfers between devices: 124 us -> 68.9 us
  local copies, waits for them, and re-layouts: 8.33 us -> 29.4 us
    add x3 -> x0, other arithmetic: 99.3 us -> none  [the longest x1 43.2 us: on_device(): 2.0 * adj_now - adj_later + stiffness * laplace(padded_adjoint)]
    pallas_call x0 -> x4, Pallas kernels: none -> 88.9 us  [leap(): pl.pallas_call(functools.partial(step_kernel, kind), grid=grid, in_specs=...]
    psum x1 -> x0, waiting for transfers between devices: 80.5 us -> none  [on_device(): full_sum = lax.psum(imaging, 'shot')]
    reduce_sum x1 -> x0, other arithmetic: 45.6 us -> none  [on_device(): misfit_early = jnp.sum(advanced * receiver_mask, axis=2) - observed[0, 0]]
    reduce_scatter x0 -> x1, waiting for transfers between devices: none -> 37.1 us  [on_device(): summed = lax.psum_scatter(imaging, 'shot', scatter_dimension=0, tiled=True)]
    ppermute x16, waiting for transfers between devices: 43.2 us -> 17.4 us  [the longest x8 15.6 us: halos(): lax.ppermute(lax.slice_in_dim(block, size - 4, None, axis=dim), axis, for...]
    concatenate x4 -> x0, other arithmetic: 20 us -> none  [extended(): block = jnp.concatenate([low, block, high], axis=dim)]
    all_gather x1, waiting for transfers between devices: 0.01 us -> 13.7 us  [on_device(): full_velocity = lax.all_gather(velocity, 'shot', axis=0, tiled=True)]
  transfers between devices with their start and end apart: 18 -> 18, of which waited for: 10 -> 4; matrix products, arithmetic and copies ran while one was open for 12% -> 11% of each run, Pallas kernels for 0% -> 22%
where the time goes in v1:
time: 266 us; the launch traced here: 265 us
  Pallas kernels  88.9 us (33%)
  waiting for transfers between devices  68.9 us (26%)
  starting transfers between devices  54.7 us (21%)
  local copies, waits for them, and re-layouts  29.4 us (11%)
  between operations  15.6 us (6%)
  other arithmetic  7.35 us (3%)
    pallas_call x4, Pallas kernels, leap(): pl.pallas_call(functools.partial(step_kernel, kind), grid=grid, in_specs=...  88.9 us
    ppermute x8, starting transfers between devices, halos(): lax.ppermute(lax.slice_in_dim(block, size - 4, None, axis=dim), axis, for...  39.7 us
    reduce_scatter x1, waiting for transfers between devices, on_device(): summed = lax.psum_scatter(imaging, 'shot', scatter_dimension=0, tiled=True)  37.1 us
    ppermute x8, waiting for transfers between devices, halos(): lax.ppermute(lax.slice_in_dim(block, size - 4, None, axis=dim), axis, for...  15.6 us
    ppermute x8, starting transfers between devices, halos(): high = lax.ppermute(lax.slice_in_dim(block, 0, 4, axis=dim), axis, backward)  14.9 us
    all_gather x1, waiting for transfers between devices, on_device(): full_velocity = lax.all_gather(velocity, 'shot', axis=0, tiled=True)  13.7 us
    slice x8, local copies, waits for them, and re-layouts, halos(): high = lax.ppermute(lax.slice_in_dim(block, 0, 4, axis=dim), axis, backward)  11.7 us
    pad x4, local copies, waits for them, and re-layouts, halos(): ylo = jnp.pad(ylo, ((0, 0), (4, 0), (0, 0)))  5.96 us
  transfers between devices with their start and end apart: 18, of which 4 were waited for; matrix products, arithmetic and copies ran while one was open for 11% of the time, Pallas kernels for 22%

profile of v1, /device:TPU:1, one launch (start us, length us, event | category | flops | bytes accessed | tf_op | source)
XLA Modules:
  0.0 264.9 jit_solution(3444408323010770740)
XLA Ops:
  7.2 0.0 all-gather.2.cloned.1.call-start
  7.2 0.7 all-gather.2.cloned.1.call-update
  7.9 0.0 reduce-scatter.2.cloned.1.call-start
  8.0 1.2 fusion.4
  9.2 3.3 %collective-permute-start.7 = (f32[32,4,384]{2,1,0:T(4,128)S(1)}, f32[32,4,384]{2,1,0:T(4,128)S(1)}, u32[]{:S(2)}, u32[]{:S(2)}) collective-permute-start(f32[32,4,384]{2,1,0:T(4,128)S(1)} %get-tuple-element.26), channel_id=1, source_target_pairs={{1,0},{2,1},{3,2},{5,4},{6,5},{7,6},{9,8},{10,9},{11,10},{13,12},{... | collective-permute-start | bytes 589832 | tf_op jit(solution)/shard_map/ppermute | solution.py:26
  12.5 4.8 %collective-permute-start.6 = (f32[32,4,384]{2,1,0:T(4,128)S(1)}, f32[32,4,384]{2,1,0:T(4,128)S(1)}, u32[]{:S(2)}, u32[]{:S(2)}) collective-permute-start(f32[32,4,384]{2,1,0:T(4,128)S(1)} %get-tuple-element.27), channel_id=1, source_target_pairs={{0,1},{1,2},{2,3},{4,5},{5,6},{6,7},{8,9},{9,10},{10,11},{12,13},{... | collective-permute-start | bytes 589832 | tf_op jit(solution)/shard_map/ppermute | solution.py:25
  17.3 1.2 slice_bitcast_fusion
  18.5 1.3 collective-permute-start.5
  19.8 4.0 %collective-permute-start.4 = (f32[4,64,384]{2,1,0:T(8,128)S(1)}, f32[4,64,384]{2,1,0:T(8,128)S(1)}, u32[]{:S(2)}, u32[]{:S(2)}) collective-permute-start(f32[4,64,384]{2,1,0:T(8,128)S(1)} %get-tuple-element.29), channel_id=1, source_target_pairs={{0,4},{4,8},{8,12},{12,16},{16,20},{20,24},{24,28},{1,5},{5,9},{9,... | collective-permute-start | bytes 1179656 | tf_op jit(solution)/shard_map/ppermute | solution.py:25
  23.8 1.3 fusion.5
  25.1 1.9 collective-permute-start.3
  27.0 1.4 copy.22.refs_9_
  28.4 0.6 fusion.7
  30.3 1.3 pad_add_fusion.refs_10_
  31.6 0.6 fusion.6
  32.2 0.0 collective-permute-done.7
  32.2 5.1 %collective-permute-start.2 = (f32[32,4,384]{2,1,0:T(4,128)S(1)}, f32[32,4,384]{2,1,0:T(4,128)}, u32[]{:S(2)}, u32[]{:S(2)}) collective-permute-start(f32[32,4,384]{2,1,0:T(4,128)S(1)} %get-tuple-element.31), channel_id=1, source_target_pairs={{0,1},{1,2},{2,3},{4,5},{5,6},{6,7},{8,9},{9,10},{10,11},{12,13},{... | collective-permute-start | bytes 589832 | tf_op jit(solution)/shard_map/ppermute | solution.py:25
  37.3 0.8 pad.29.refs_6_
  38.2 0.8 pad.28.refs_5_
  39.0 0.0 copy-start.7
  39.0 13.7 %all-gather.2.cloned.1.call-done.refs_8_ = f32[32,64,384]{2,1,0:T(8,128)} async-done(((f32[8,64,384]{2,1,0:T(8,128)}), f32[32,64,384]{2,1,0:T(8,128)}) %all-gather.2.cloned.1.call-update) | async-done | bytes 3145744 | tf_op jit(solution)/shard_map/all_gather | solution.py:181
  52.7 29.0 %leap_wave1.1 = (f32[32,64,384]{2,1,0:T(8,128)}, f32[32,64,384]{2,1,0:T(8,128)}, f32[32,64,1]{2,1,0:T(8,128)}) custom-call(f32[32,64,384]{2,1,0:T(8,128)} %bitcast.25, f32[32,64,384]{2,1,0:T(8,128)} %bitcast.26, f32[32,64,384]{2,1,0:T(8,128)} %bitcast.27, f32[4,64,384]{2,1,0:T(8,128)} %copy-done.7, f32[4,64,384]{2,1,0:T(8,128)} %copy-done.6, ...), custom_call_target="tpu_custom_call" | custom-call | flops 47185920 | bytes 34603008 | tf_op jit(solution)/shard_map/leap_wave1/pallas_call | solution.py:155
  81.8 0.0 copy-start.11
  81.8 1.9 fusion.2
  83.6 1.2 fusion.3
  84.8 2.6 collective-permute-start.11
  87.4 1.3 collective-permute-start.9
  88.7 4.7 %collective-permute-start.8 = (f32[4,64,384]{2,1,0:T(8,128)S(1)}, f32[4,64,384]{2,1,0:T(8,128)}, u32[]{:S(2)}, u32[]{:S(2)}) collective-permute-start(f32[4,64,384]{2,1,0:T(8,128)S(1)} %get-tuple-element.25), channel_id=1, source_target_pairs={{0,4},{4,8},{8,12},{12,16},{16,20},{20,24},{24,28},{1,5},{5,9},{9,... | collective-permute-start | bytes 1179656 | tf_op jit(solution)/shard_map/ppermute | solution.py:25
  93.5 1.2 slice_bitcast_fusion.2
  94.6 0.0 copy-start.10
  94.7 1.3 collective-permute-start.1
  96.0 4.7 %collective-permute-start = (f32[4,64,384]{2,1,0:T(8,128)S(1)}, f32[4,64,384]{2,1,0:T(8,128)}, u32[]{:S(2)}, u32[]{:S(2)}) collective-permute-start(f32[4,64,384]{2,1,0:T(8,128)S(1)} %get-tuple-element.33), channel_id=1, source_target_pairs={{0,4},{4,8},{8,12},{12,16},{16,20},{20,24},{24,28},{1,5},{5,9},{9,... | collective-permute-start | bytes 1179656 | tf_op jit(solution)/shard_map/ppermute | solution.py:25
  100.7 5.8 %collective-permute-start.10 = (f32[32,4,384]{2,1,0:T(4,128)}, f32[32,4,384]{2,1,0:T(4,128)}, u32[]{:S(2)}, u32[]{:S(2)}) collective-permute-start(f32[32,4,384]{2,1,0:T(4,128)} %get-tuple-element.23), channel_id=1, source_target_pairs={{0,1},{1,2},{2,3},{4,5},{5,6},{6,7},{8,9},{9,10},{10,11},{12,13},{... | collective-permute-start | bytes 589832 | tf_op jit(solution)/shard_map/ppermute | solution.py:25
  106.6 0.4 copy.21
  107.0 1.7 pad.27.refs_6_
  108.7 1.7 pad.26.refs_5_
  110.4 1.7 pad.31.refs_6_
  112.1 15.6 %collective-permute-done.10 = f32[32,4,384]{2,1,0:T(4,128)} collective-permute-done((f32[32,4,384]{2,1,0:T(4,128)}, f32[32,4,384]{2,1,0:T(4,128)}, u32[]{:S(2)}, u32[]{:S(2)}) %collective-permute-start.10) | collective-permute-done | bytes 196640 | tf_op jit(solution)/shard_map/ppermute | solution.py:25
  127.7 1.7 pad.30.refs_5_
  129.4 0.7 copy-done.9
  130.2 28.8 %leap_wave2.1 = (f32[32,64,384]{2,1,0:T(8,128)}, f32[32,64,1]{2,1,0:T(8,128)}) custom-call(f32[32,64,384]{2,1,0:T(8,128)} %get-tuple-element.9.refs_0_.refs_1_.refs_2_, f32[32,64,384]{2,1,0:T(8,128)} %get-tuple-element.9.refs_0_.refs_1_.refs_2_, f32[32,64,384]{2,1,0:T(8,128)} %get-tuple-element.9.refs_0_.refs_1_.refs_2_, ...), custom_call_target="tpu_custom_call" | custom-call | flops 47185920 | bytes 31457280 | tf_op jit(solution)/shard_map/leap_wave2/pallas_call | solution.py:155
  159.0 2.4 sub.17.refs_10_
  161.4 0.7 copy-done.8
  162.1 15.5 %leap_adj1.1 = (f32[32,64,384]{2,1,0:T(8,128)}, f32[32,64,384]{2,1,0:T(8,128)}) custom-call(f32[32,64,384]{2,1,0:T(8,128)} %bitcast.30, f32[32,64,384]{2,1,0:T(8,128)} %bitcast.31, f32[32,64,384]{2,1,0:T(8,128)} %bitcast.32, f32[4,64,384]{2,1,0:T(8,128)} %collective-permute-done.refs_3_, f32[4,64,384]{2,1,0:T(8,128)} %copy-done.8, ...), custom_call_target="tpu_custom_call" | custom-call | flops 47185920 | bytes 31457280 | tf_op jit(solution)/shard_map/leap_adj1/pallas_call | solution.py:155
  177.6 2.0 fusion.1
  179.6 1.3 collective-permute-start.13
  180.9 4.0 %collective-permute-start.12 = (f32[4,64,384]{2,1,0:T(8,128)S(1)}, f32[4,64,384]{2,1,0:T(8,128)S(1)}, u32[]{:S(2)}, u32[]{:S(2)}) collective-permute-start(f32[4,64,384]{2,1,0:T(8,128)S(1)} %get-tuple-element.21), channel_id=1, source_target_pairs={{0,4},{4,8},{8,12},{12,16},{16,20},{20,24},{24,28},{1,5},{5,9},{9,... | collective-permute-start | bytes 1179656 | tf_op jit(solution)/shard_map/ppermute | solution.py:25
  184.9 1.9 fusion
  186.8 1.9 collective-permute-start.15
  188.7 6.5 %collective-permute-start.14 = (f32[32,4,384]{2,1,0:T(4,128)S(1)}, f32[32,4,384]{2,1,0:T(4,128)}, u32[]{:S(2)}, u32[]{:S(2)}) collective-permute-start(f32[32,4,384]{2,1,0:T(4,128)S(1)} %get-tuple-element.19), channel_id=1, source_target_pairs={{0,1},{1,2},{2,3},{4,5},{5,6},{6,7},{8,9},{9,10},{10,11},{12,13},{... | collective-permute-start | bytes 589832 | tf_op jit(solution)/shard_map/ppermute | solution.py:25
  195.1 0.4 copy.23
  195.6 1.1 sub.18.refs_10_
  196.7 1.8 collective-permute-done.15
  198.5 1.7 pad.33.refs_6_
  200.2 1.7 pad.32.refs_5_
  201.9 0.0 copy-start.5
  201.9 0.7 copy-done.4
  202.7 0.1 copy-done.5
  202.8 15.6 %leap_adj2.1 = f32[32,64,384]{2,1,0:T(8,128)} custom-call(f32[32,64,384]{2,1,0:T(8,128)} %get-tuple-element.12.refs_0_.refs_1_.refs_2_, f32[32,64,384]{2,1,0:T(8,128)} %get-tuple-element.12.refs_0_.refs_1_.refs_2_, f32[32,64,384]{2,1,0:T(8,128)} %get-tuple-element.12.refs_0_.refs_1_.refs_2_, f32[4,64,384]{2,1,0:T(8,128)} %copy-done.5, ...), custom_call_target="tpu_custom_call" | custom-call | flops 47185920 | bytes 31457280 | tf_op jit(solution)/shard_map/leap_adj2/pallas_call | solution.py:155
  218.3 0.0 copy-start.2
  218.4 0.0 copy-start.3
  218.4 0.0 reduce-scatter.2.cloned.1.call-update
  218.4 37.1 %reduce-scatter.2.cloned.1.call-done = f32[8,64,384]{2,1,0:T(8,128)} async-done(((f32[32,64,384]{2,1,0:T(8,128)}), f32[8,64,384]{2,1,0:T(8,128)}) %reduce-scatter.2.cloned.1.call-update) | async-done | bytes 786448 | tf_op jit(solution)/shard_map/reduce_scatter | solution.py:206
  255.5 2.6 divide_add_fusion
  (34 shorter events, 0.1 us)
Async XLA Ops:
  7.2 19.9 %copy-start.12 = (s32[1,32,64]{2,1,0:T(8,128)S(1)}, s32[1,32,64]{2,1,0:T(8,128)}, u32[]{:S(2)}) copy-start(s32[1,32,64]{2,1,0:T(8,128)} %param.19) | copy-start | bytes 24580
  7.2 21.2 %copy-start.13 = (s32[1,3]{1,0:T(1,128)S(1)}, s32[1,3]{1,0:T(1,128)}, u32[]{:S(2)}) copy-start(s32[1,3]{1,0:T(1,128)} %param.20) | copy-start | bytes 40
  7.2 24.4 %copy-start.14 = (f32[1,2]{1,0:T(1,128)S(1)}, f32[1,2]{1,0:T(1,128)}, u32[]{:S(2)}) copy-start(f32[1,2]{1,0:T(1,128)} %param.21) | copy-start | bytes 28
  7.2 45.5 %all-gather.2.cloned.1.call-start = ((), (), s32[]{:S(2)}) async-start(), calls=%async_computation.1 | async-start | bytes 3932160 | tf_op jit(solution)/shard_map/all_gather | solution.py:181
  7.9 247.5 %reduce-scatter.2.cloned.1.call-start = ((), (), s32[]{:S(2)}) async-start(), calls=%async_computation.2 | async-start | bytes 3932160 | tf_op jit(solution)/shard_map/reduce_scatter | solution.py:206
  9.2 23.0 %collective-permute-start.7 = (f32[32,4,384]{2,1,0:T(4,128)S(1)}, f32[32,4,384]{2,1,0:T(4,128)S(1)}, u32[]{:S(2)}, u32[]{:S(2)}) collective-permute-start(f32[32,4,384]{2,1,0:T(4,128)S(1)} %get-tuple-element.26), channel_id=1, source_target_pairs={{1,0},{2,1},{3,2},{5,4},{6,5},{7,6},{9,8},{10,9},{11,10},{13,12},{... | collective-permute-start | bytes 589832 | tf_op jit(solution)/shard_map/ppermute | solution.py:26
  12.5 25.6 %collective-permute-start.6 = (f32[32,4,384]{2,1,0:T(4,128)S(1)}, f32[32,4,384]{2,1,0:T(4,128)S(1)}, u32[]{:S(2)}, u32[]{:S(2)}) collective-permute-start(f32[32,4,384]{2,1,0:T(4,128)S(1)} %get-tuple-element.27), channel_id=1, source_target_pairs={{0,1},{1,2},{2,3},{4,5},{5,6},{6,7},{8,9},{9,10},{10,11},{12,13},{... | collective-permute-start | bytes 589832 | tf_op jit(solution)/shard_map/ppermute | solution.py:25
  18.5 20.5 %collective-permute-start.5 = (f32[4,64,384]{2,1,0:T(8,128)S(1)}, f32[4,64,384]{2,1,0:T(8,128)S(1)}, u32[]{:S(2)}, u32[]{:S(2)}) collective-permute-start(f32[4,64,384]{2,1,0:T(8,128)S(1)} %get-tuple-element.28), channel_id=1, source_target_pairs={{4,0},{8,4},{12,8},{16,12},{20,16},{24,20},{28,24},{5,1},{9,5},{13... | collective-permute-start | bytes 1179656 | tf_op jit(solution)/shard_map/ppermute | solution.py:26
  19.8 19.2 %collective-permute-start.4 = (f32[4,64,384]{2,1,0:T(8,128)S(1)}, f32[4,64,384]{2,1,0:T(8,128)S(1)}, u32[]{:S(2)}, u32[]{:S(2)}) collective-permute-start(f32[4,64,384]{2,1,0:T(8,128)S(1)} %get-tuple-element.29), channel_id=1, source_target_pairs={{0,4},{4,8},{8,12},{12,16},{16,20},{20,24},{24,28},{1,5},{5,9},{9,... | collective-permute-start | bytes 1179656 | tf_op jit(solution)/shard_map/ppermute | solution.py:25
  25.1 69.6 %collective-permute-start.3 = (f32[32,4,384]{2,1,0:T(4,128)S(1)}, f32[32,4,384]{2,1,0:T(4,128)S(1)}, u32[]{:S(2)}, u32[]{:S(2)}) collective-permute-start(f32[32,4,384]{2,1,0:T(4,128)S(1)} %get-tuple-element.30), channel_id=1, source_target_pairs={{1,0},{2,1},{3,2},{5,4},{6,5},{7,6},{9,8},{10,9},{11,10},{13,12},{... | collective-permute-start | bytes 589832 | tf_op jit(solution)/shard_map/ppermute | solution.py:26
  32.2 63.8 %collective-permute-start.2 = (f32[32,4,384]{2,1,0:T(4,128)S(1)}, f32[32,4,384]{2,1,0:T(4,128)}, u32[]{:S(2)}, u32[]{:S(2)}) collective-permute-start(f32[32,4,384]{2,1,0:T(4,128)S(1)} %get-tuple-element.31), channel_id=1, source_target_pairs={{0,1},{1,2},{2,3},{4,5},{5,6},{6,7},{8,9},{9,10},{10,11},{12,13},{... | collective-permute-start | bytes 589832 | tf_op jit(solution)/shard_map/ppermute | solution.py:25
  39.0 13.8 %copy-start.6 = (f32[4,64,384]{2,1,0:T(8,128)}, f32[4,64,384]{2,1,0:T(8,128)S(1)}, u32[]{:S(2)}) copy-start(f32[4,64,384]{2,1,0:T(8,128)S(1)} %collective-permute-done.5.refs_4_) | copy-start | bytes 1179652
  39.0 13.8 %copy-start.7 = (f32[4,64,384]{2,1,0:T(8,128)}, f32[4,64,384]{2,1,0:T(8,128)S(1)}, u32[]{:S(2)}) copy-start(f32[4,64,384]{2,1,0:T(8,128)S(1)} %collective-permute-done.4.refs_3_) | copy-start | bytes 1179652
  81.8 24.8 %copy-start.11 = (f32[1,2,32,64]{3,2,1,0:T(8,128)S(1)}, f32[1,2,32,64]{3,2,1,0:T(8,128)}, u32[]{:S(2)}) copy-start(f32[1,2,32,64]{3,2,1,0:T(8,128)} %param.18) | copy-start | bytes 49156
  84.8 15.9 %collective-permute-start.11 = (f32[32,4,384]{2,1,0:T(4,128)S(1)}, f32[32,4,384]{2,1,0:T(4,128)}, u32[]{:S(2)}, u32[]{:S(2)}) collective-permute-start(f32[32,4,384]{2,1,0:T(4,128)S(1)} %get-tuple-element.22), channel_id=1, source_target_pairs={{1,0},{2,1},{3,2},{5,4},{6,5},{7,6},{9,8},{10,9},{11,10},{13,12},{... | collective-permute-start | bytes 589832 | tf_op jit(solution)/shard_map/ppermute | solution.py:26
  87.4 42.0 %collective-permute-start.9 = (f32[4,64,384]{2,1,0:T(8,128)S(1)}, f32[4,64,384]{2,1,0:T(8,128)S(1)}, u32[]{:S(2)}, u32[]{:S(2)}) collective-permute-start(f32[4,64,384]{2,1,0:T(8,128)S(1)} %get-tuple-element.24), channel_id=1, source_target_pairs={{4,0},{8,4},{12,8},{16,12},{20,16},{24,20},{28,24},{5,1},{9,5},{13... | collective-permute-start | bytes 1179656 | tf_op jit(solution)/shard_map/ppermute | solution.py:26
  88.7 40.7 %collective-permute-start.8 = (f32[4,64,384]{2,1,0:T(8,128)S(1)}, f32[4,64,384]{2,1,0:T(8,128)}, u32[]{:S(2)}, u32[]{:S(2)}) collective-permute-start(f32[4,64,384]{2,1,0:T(8,128)S(1)} %get-tuple-element.25), channel_id=1, source_target_pairs={{0,4},{4,8},{8,12},{12,16},{16,20},{20,24},{24,28},{1,5},{5,9},{9,... | collective-permute-start | bytes 1179656 | tf_op jit(solution)/shard_map/ppermute | solution.py:25
  94.6 11.9 %copy-start.10 = (f32[32,4,384]{2,1,0:T(4,128)}, f32[32,4,384]{2,1,0:T(4,128)S(1)}, u32[]{:S(2)}) copy-start(f32[32,4,384]{2,1,0:T(4,128)S(1)} %collective-permute-done.3) | copy-start | bytes 589828
  94.7 66.7 %collective-permute-start.1 = (f32[4,64,384]{2,1,0:T(8,128)S(1)}, f32[4,64,384]{2,1,0:T(8,128)S(1)}, u32[]{:S(2)}, u32[]{:S(2)}) collective-permute-start(f32[4,64,384]{2,1,0:T(8,128)S(1)} %get-tuple-element.32), channel_id=1, source_target_pairs={{4,0},{8,4},{12,8},{16,12},{20,16},{24,20},{28,24},{5,1},{9,5},{13... | collective-permute-start | bytes 1179656 | tf_op jit(solution)/shard_map/ppermute | solution.py:26
  96.0 65.4 %collective-permute-start = (f32[4,64,384]{2,1,0:T(8,128)S(1)}, f32[4,64,384]{2,1,0:T(8,128)}, u32[]{:S(2)}, u32[]{:S(2)}) collective-permute-start(f32[4,64,384]{2,1,0:T(8,128)S(1)} %get-tuple-element.33), channel_id=1, source_target_pairs={{0,4},{4,8},{8,12},{12,16},{16,20},{20,24},{24,28},{1,5},{5,9},{9,... | collective-permute-start | bytes 1179656 | tf_op jit(solution)/shard_map/ppermute | solution.py:25
  100.7 27.0 %collective-permute-start.10 = (f32[32,4,384]{2,1,0:T(4,128)}, f32[32,4,384]{2,1,0:T(4,128)}, u32[]{:S(2)}, u32[]{:S(2)}) collective-permute-start(f32[32,4,384]{2,1,0:T(4,128)} %get-tuple-element.23), channel_id=1, source_target_pairs={{0,1},{1,2},{2,3},{4,5},{5,6},{6,7},{8,9},{9,10},{10,11},{12,13},{... | collective-permute-start | bytes 589832 | tf_op jit(solution)/shard_map/ppermute | solution.py:25
  129.4 0.7 copy-start.9
  161.4 0.7 copy-start.8
  177.6 18.0 %copy-start.1 = (f32[32,64,1]{2,1,0:T(8,128)S(1)}, f32[32,64,1]{2,1,0:T(8,128)}, u32[]{:S(2)}) copy-start(f32[32,64,1]{2,1,0:T(8,128)} %get-tuple-element.13) | copy-start | bytes 24580
  179.6 22.3 %collective-permute-start.13 = (f32[4,64,384]{2,1,0:T(8,128)}, f32[4,64,384]{2,1,0:T(8,128)S(1)}, u32[]{:S(2)}, u32[]{:S(2)}) collective-permute-start(f32[4,64,384]{2,1,0:T(8,128)} %get-tuple-element.20), channel_id=1, source_target_pairs={{4,0},{8,4},{12,8},{16,12},{20,16},{24,20},{28,24},{5,1},{9,5},{13... | collective-permute-start | bytes 1179656 | tf_op jit(solution)/shard_map/ppermute | solution.py:26
  180.9 21.0 %collective-permute-start.12 = (f32[4,64,384]{2,1,0:T(8,128)S(1)}, f32[4,64,384]{2,1,0:T(8,128)S(1)}, u32[]{:S(2)}, u32[]{:S(2)}) collective-permute-start(f32[4,64,384]{2,1,0:T(8,128)S(1)} %get-tuple-element.21), channel_id=1, source_target_pairs={{0,4},{4,8},{8,12},{12,16},{16,20},{20,24},{24,28},{1,5},{5,9},{9,... | collective-permute-start | bytes 1179656 | tf_op jit(solution)/shard_map/ppermute | solution.py:25
  186.8 11.7 %collective-permute-start.15 = (f32[32,4,384]{2,1,0:T(4,128)}, f32[32,4,384]{2,1,0:T(4,128)}, u32[]{:S(2)}, u32[]{:S(2)}) collective-permute-start(f32[32,4,384]{2,1,0:T(4,128)} %get-tuple-element.18), channel_id=1, source_target_pairs={{1,0},{2,1},{3,2},{5,4},{6,5},{7,6},{9,8},{10,9},{11,10},{13,12},{... | collective-permute-start | bytes 589832 | tf_op jit(solution)/shard_map/ppermute | solution.py:26
  188.7 11.5 %collective-permute-start.14 = (f32[32,4,384]{2,1,0:T(4,128)S(1)}, f32[32,4,384]{2,1,0:T(4,128)}, u32[]{:S(2)}, u32[]{:S(2)}) collective-permute-start(f32[32,4,384]{2,1,0:T(4,128)S(1)} %get-tuple-element.19), channel_id=1, source_target_pairs={{0,1},{1,2},{2,3},{4,5},{5,6},{6,7},{8,9},{9,10},{10,11},{12,13},{... | collective-permute-start | bytes 589832 | tf_op jit(solution)/shard_map/ppermute | solution.py:25
  201.9 0.7 copy-start.4
  201.9 0.9 copy-start.5
  218.3 37.1 %copy-start = (f32[8,64,384]{2,1,0:T(8,128)S(1)}, f32[8,64,384]{2,1,0:T(8,128)}, u32[]{:S(2)}) copy-start(f32[8,64,384]{2,1,0:T(8,128)} %param.11) | copy-start | bytes 2359300
  218.3 37.1 %copy-start.2 = (f32[8,64,384]{2,1,0:T(8,128)S(1)}, f32[8,64,384]{2,1,0:T(8,128)}, u32[]{:S(2)}) copy-start(f32[8,64,384]{2,1,0:T(8,128)} %param.13) | copy-start | bytes 2359300
  218.4 37.1 %copy-start.3 = (f32[8,64,384]{2,1,0:T(8,128)S(1)}, f32[8,64,384]{2,1,0:T(8,128)}, u32[]{:S(2)}) copy-start(f32[8,64,384]{2,1,0:T(8,128)} %param.12) | copy-start | bytes 2359300
Sparse Core Ops, SparseCore 0:
  9.7 42.9 all-gather.1
  218.5 36.8 reduce-scatter.1

commit v2 on v1

--- a/solution.py
+++ b/solution.py
@@ -165,6 +165,80 @@
     )(*args)
 
 
+def kick_kernel(img_ref, vel_ref, mom_ref, mass_ref, v_out, p_out, recv, send_sem, recv_sem, own_sem):
+    me = lax.axis_index("shot")
+    n = lax.axis_size("shot")
+    rows = vel_ref.shape[0]
+    mesh = pl.DeviceIdType.MESH
+
+    barrier = pltpu.get_barrier_semaphore()
+    for d in range(1, n):
+        pl.semaphore_signal(barrier, inc=1, device_id={"shot": lax.rem(me + d, n)}, device_id_type=mesh)
+    pl.semaphore_wait(barrier, n - 1)
+
+    sends = []
+    for d in (1, n - 1) + tuple(range(2, n - 1)):
+        peer = lax.rem(me + d, n)
+        copy = pltpu.make_async_remote_copy(
+            src_ref=img_ref.at[pl.ds(pl.multiple_of(peer * rows, rows), rows)],
+            dst_ref=recv.at[me],
+            send_sem=send_sem.at[d],
+            recv_sem=recv_sem.at[me],
+            device_id={"shot": peer},
+            device_id_type=mesh,
+        )
+        copy.start()
+        sends.append(copy)
+    own = pltpu.make_async_copy(img_ref.at[pl.ds(pl.multiple_of(me * rows, rows), rows)], recv.at[me], own_sem)
+    own.start()
+    for copy in sends:
+        copy.wait_send()
+    own.wait()
+    for d in range(1, n):
+        src = lax.rem(me + d, n)
+        pltpu.make_async_remote_copy(
+            src_ref=img_ref.at[pl.ds(0, rows)],
+            dst_ref=recv.at[src],
+            send_sem=send_sem.at[d],
+            recv_sem=recv_sem.at[src],
+            device_id={"shot": src},
+            device_id_type=mesh,
+        ).wait_recv()
+
+    def row(r, carry):
+        summed = recv[0, r]
+        for s in range(1, n):
+            summed = summed + recv[s, r]
+        v = vel_ref[r]
+        gradient = 2.0 / v * summed
+        p_half = mom_ref[r] - 0.5 * leap_step * gradient
+        p_out[r] = p_half
+        v_out[r] = v + leap_step * p_half / mass_ref[r]
+        return carry
+
+    lax.fori_loop(0, rows, row, 0)
+
+
+def kick(imaging, velocity, momentum, mass_diag):
+    n = lax.axis_size("shot")
+    vmem = pl.BlockSpec(memory_space=pltpu.VMEM)
+    slab = jax.ShapeDtypeStruct(velocity.shape, jnp.float32)
+    return pl.pallas_call(
+        kick_kernel,
+        in_specs=[pl.BlockSpec(memory_space=pl.ANY), vmem, vmem, vmem],
+        out_specs=[vmem, vmem],
+        out_shape=[slab, slab],
+        scratch_shapes=[
+            pltpu.VMEM((n,) + velocity.shape, jnp.float32),
+            pltpu.SemaphoreType.DMA((n,)),
+            pltpu.SemaphoreType.DMA((n,)),
+            pltpu.SemaphoreType.DMA(()),
+        ],
+        compiler_params=pltpu.CompilerParams(collective_id=0, has_side_effects=True, vmem_limit_bytes=48 * 1024 * 1024),
+        name="kick_reduce_scatter",
+    )(imaging, velocity, momentum, mass_diag)
+
+
 def on_device(
     velocity,
     momentum,
@@ -203,10 +277,7 @@
     misfit_early = pick_adv - observed[0, 0][:, :, None]
     adj_two, part = leap("adj1", adj_now, *adj_h, adj_later, full_velocity, rec, misfit_late, dw2)
     (imaging,) = leap("adj2", adj_two, *halos(adj_two), adj_now, full_velocity, rec, misfit_early, dw1, part)
-    summed = lax.psum_scatter(imaging, "shot", scatter_dimension=0, tiled=True)
-    gradient = 2.0 / velocity * summed
-    p_half = momentum - 0.5 * leap_step * gradient
-    v_new = velocity + leap_step * p_half / mass_diag
+    v_new, p_half = kick(imaging, velocity, momentum, mass_diag)
     return (v_new, p_half)
 
 

time: 266 us -> 262 us (0.985)
  waiting for transfers between devices: 68.9 us -> 31.8 us
  Pallas kernels: 88.9 us -> 123 us
    reduce_scatter x1 -> x0, waiting for transfers between devices: 37.1 us -> none  [on_device(): summed = lax.psum_scatter(imaging, 'shot', scatter_dimension=0, tiled=True)]
    pallas_call x0 -> x1, Pallas kernels: none -> 33.7 us  [kick(): pl.pallas_call(kick_kernel, in_specs=[pl.BlockSpec(memory_space=pl.ANY),...]
  transfers between devices with their start and end apart: 18 -> 17, of which waited for: 4 -> 3; matrix products, arithmetic and copies ran while one was open for 11% -> 11% of each run, Pallas kernels for 22% -> 22%
where the time goes in v2:
time: 262 us; the launch traced here: 261 us
  Pallas kernels  123 us (47%)
  starting transfers between devices  54.7 us (21%)
  waiting for transfers between devices  31.8 us (12%)
  local copies, waits for them, and re-layouts  31.2 us (12%)
  between operations  15.6 us (6%)
  other arithmetic  4.8 us (2%)
    pallas_call x4, Pallas kernels, leap(): pl.pallas_call(functools.partial(step_kernel, kind), grid=grid, in_specs=...  89 us
    ppermute x8, starting transfers between devices, halos(): lax.ppermute(lax.slice_in_dim(block, size - 4, None, axis=dim), axis, for...  39.7 us
    pallas_call x1, Pallas kernels, kick(): pl.pallas_call(kick_kernel, in_specs=[pl.BlockSpec(memory_space=pl.ANY),...  33.7 us
    ppermute x8, waiting for transfers between devices, halos(): lax.ppermute(lax.slice_in_dim(block, size - 4, None, axis=dim), axis, for...  15.6 us
    ppermute x8, starting transfers between devices, halos(): high = lax.ppermute(lax.slice_in_dim(block, 0, 4, axis=dim), axis, backward)  14.9 us
    all_gather x1, waiting for transfers between devices, on_device(): full_velocity = lax.all_gather(velocity, 'shot', axis=0, tiled=True)  13.8 us
    slice x8, local copies, waits for them, and re-layouts, halos(): high = lax.ppermute(lax.slice_in_dim(block, 0, 4, axis=dim), axis, backward)  11.7 us
    pad x4, local copies, waits for them, and re-layouts, halos(): ylo = jnp.pad(ylo, ((0, 0), (4, 0), (0, 0)))  5.96 us
  transfers between devices with their start and end apart: 17, of which 3 were waited for; matrix products, arithmetic and copies ran while one was open for 11% of the time, Pallas kernels for 22%

profile of v2, /device:TPU:1, one launch (start us, length us, event | category | flops | bytes accessed | tf_op | source)
XLA Modules:
  0.0 260.8 jit_solution(5923606508582694885)
XLA Ops:
  7.2 0.0 all-gather.2.cloned.1.call-start
  7.2 0.7 all-gather.2.cloned.1.call-update
  7.9 1.2 fusion.4
  9.1 3.3 %collective-permute-start.7 = (f32[32,4,384]{2,1,0:T(4,128)S(1)}, f32[32,4,384]{2,1,0:T(4,128)S(1)}, u32[]{:S(2)}, u32[]{:S(2)}) collective-permute-start(f32[32,4,384]{2,1,0:T(4,128)S(1)} %get-tuple-element.24), channel_id=1, source_target_pairs={{1,0},{2,1},{3,2},{5,4},{6,5},{7,6},{9,8},{10,9},{11,10},{13,12},{... | collective-permute-start | bytes 589832 | tf_op jit(solution)/shard_map/ppermute | solution.py:26
  12.5 4.8 %collective-permute-start.6 = (f32[32,4,384]{2,1,0:T(4,128)S(1)}, f32[32,4,384]{2,1,0:T(4,128)S(1)}, u32[]{:S(2)}, u32[]{:S(2)}) collective-permute-start(f32[32,4,384]{2,1,0:T(4,128)S(1)} %get-tuple-element.25), channel_id=1, source_target_pairs={{0,1},{1,2},{2,3},{4,5},{5,6},{6,7},{8,9},{9,10},{10,11},{12,13},{... | collective-permute-start | bytes 589832 | tf_op jit(solution)/shard_map/ppermute | solution.py:25
  17.3 1.2 slice_bitcast_fusion
  18.4 1.3 collective-permute-start.5
  19.7 4.0 %collective-permute-start.4 = (f32[4,64,384]{2,1,0:T(8,128)S(1)}, f32[4,64,384]{2,1,0:T(8,128)S(1)}, u32[]{:S(2)}, u32[]{:S(2)}) collective-permute-start(f32[4,64,384]{2,1,0:T(8,128)S(1)} %get-tuple-element.27), channel_id=1, source_target_pairs={{0,4},{4,8},{8,12},{12,16},{16,20},{20,24},{24,28},{1,5},{5,9},{9,... | collective-permute-start | bytes 1179656 | tf_op jit(solution)/shard_map/ppermute | solution.py:25
  23.8 1.3 fusion.5
  25.0 1.9 collective-permute-start.3
  27.0 1.4 copy.22.refs_9_
  28.4 0.6 fusion.7
  30.3 1.3 pad_add_fusion.refs_10_
  31.6 0.6 fusion.6
  32.1 0.0 collective-permute-done.7
  32.1 5.1 %collective-permute-start.2 = (f32[32,4,384]{2,1,0:T(4,128)S(1)}, f32[32,4,384]{2,1,0:T(4,128)}, u32[]{:S(2)}, u32[]{:S(2)}) collective-permute-start(f32[32,4,384]{2,1,0:T(4,128)S(1)} %get-tuple-element.29), channel_id=1, source_target_pairs={{0,1},{1,2},{2,3},{4,5},{5,6},{6,7},{8,9},{9,10},{10,11},{12,13},{... | collective-permute-start | bytes 589832 | tf_op jit(solution)/shard_map/ppermute | solution.py:25
  37.3 0.8 pad.29.refs_6_
  38.1 0.8 pad.28.refs_5_
  38.9 0.0 copy-start.7
  38.9 13.8 %all-gather.2.cloned.1.call-done.refs_8_ = f32[32,64,384]{2,1,0:T(8,128)} async-done(((f32[8,64,384]{2,1,0:T(8,128)}), f32[32,64,384]{2,1,0:T(8,128)}) %all-gather.2.cloned.1.call-update) | async-done | bytes 3145744 | tf_op jit(solution)/shard_map/all_gather | solution.py:255
  52.7 29.0 %leap_wave1.1 = (f32[32,64,384]{2,1,0:T(8,128)}, f32[32,64,384]{2,1,0:T(8,128)}, f32[32,64,1]{2,1,0:T(8,128)}) custom-call(f32[32,64,384]{2,1,0:T(8,128)} %bitcast.25, f32[32,64,384]{2,1,0:T(8,128)} %bitcast.26, f32[32,64,384]{2,1,0:T(8,128)} %bitcast.27, f32[4,64,384]{2,1,0:T(8,128)} %copy-done.7, f32[4,64,384]{2,1,0:T(8,128)} %copy-done.6, ...), custom_call_target="tpu_custom_call" | custom-call | flops 47185920 | bytes 34603008 | tf_op jit(solution)/shard_map/leap_wave1/pallas_call | solution.py:155
  81.8 0.0 copy-start.11
  81.8 1.9 fusion.2
  83.6 1.2 fusion.3
  84.8 2.6 collective-permute-start.11
  87.4 1.3 collective-permute-start.9
  88.7 4.7 %collective-permute-start.8 = (f32[4,64,384]{2,1,0:T(8,128)S(1)}, f32[4,64,384]{2,1,0:T(8,128)}, u32[]{:S(2)}, u32[]{:S(2)}) collective-permute-start(f32[4,64,384]{2,1,0:T(8,128)S(1)} %get-tuple-element.23), channel_id=1, source_target_pairs={{0,4},{4,8},{8,12},{12,16},{16,20},{20,24},{24,28},{1,5},{5,9},{9,... | collective-permute-start | bytes 1179656 | tf_op jit(solution)/shard_map/ppermute | solution.py:25
  93.5 1.2 slice_bitcast_fusion.2
  94.6 0.0 copy-start.10
  94.7 1.3 collective-permute-start.1
  96.0 0.0 collective-permute-done.2
  96.0 4.7 %collective-permute-start = (f32[4,64,384]{2,1,0:T(8,128)S(1)}, f32[4,64,384]{2,1,0:T(8,128)}, u32[]{:S(2)}, u32[]{:S(2)}) collective-permute-start(f32[4,64,384]{2,1,0:T(8,128)S(1)} %get-tuple-element.31), channel_id=1, source_target_pairs={{0,4},{4,8},{8,12},{12,16},{16,20},{20,24},{24,28},{1,5},{5,9},{9,... | collective-permute-start | bytes 1179656 | tf_op jit(solution)/shard_map/ppermute | solution.py:25
  100.7 0.0 collective-permute-done.11
  100.7 5.8 %collective-permute-start.10 = (f32[32,4,384]{2,1,0:T(4,128)}, f32[32,4,384]{2,1,0:T(4,128)}, u32[]{:S(2)}, u32[]{:S(2)}) collective-permute-start(f32[32,4,384]{2,1,0:T(4,128)} %get-tuple-element.21), channel_id=1, source_target_pairs={{0,1},{1,2},{2,3},{4,5},{5,6},{6,7},{8,9},{9,10},{10,11},{12,13},{... | collective-permute-start | bytes 589832 | tf_op jit(solution)/shard_map/ppermute | solution.py:25
  106.6 0.4 copy.21
  107.0 1.7 pad.27.refs_6_
  108.7 1.7 pad.26.refs_5_
  110.4 1.7 pad.31.refs_6_
  112.1 15.6 %collective-permute-done.10 = f32[32,4,384]{2,1,0:T(4,128)} collective-permute-done((f32[32,4,384]{2,1,0:T(4,128)}, f32[32,4,384]{2,1,0:T(4,128)}, u32[]{:S(2)}, u32[]{:S(2)}) %collective-permute-start.10) | collective-permute-done | bytes 196640 | tf_op jit(solution)/shard_map/ppermute | solution.py:25
  127.7 1.7 pad.30.refs_5_
  129.4 0.0 collective-permute-done.9.refs_4_
  129.4 0.7 copy-done.9
  130.2 28.8 %leap_wave2.1 = (f32[32,64,384]{2,1,0:T(8,128)}, f32[32,64,1]{2,1,0:T(8,128)}) custom-call(f32[32,64,384]{2,1,0:T(8,128)} %get-tuple-element.9.refs_0_.refs_1_.refs_2_, f32[32,64,384]{2,1,0:T(8,128)} %get-tuple-element.9.refs_0_.refs_1_.refs_2_, f32[32,64,384]{2,1,0:T(8,128)} %get-tuple-element.9.refs_0_.refs_1_.refs_2_, ...), custom_call_target="tpu_custom_call" | custom-call | flops 47185920 | bytes 31457280 | tf_op jit(solution)/shard_map/leap_wave2/pallas_call | solution.py:155
  159.0 2.4 sub.14.refs_10_
  161.4 0.7 copy-done.8
  162.1 15.5 %leap_adj1.1 = (f32[32,64,384]{2,1,0:T(8,128)}, f32[32,64,384]{2,1,0:T(8,128)}) custom-call(f32[32,64,384]{2,1,0:T(8,128)} %bitcast.30, f32[32,64,384]{2,1,0:T(8,128)} %bitcast.31, f32[32,64,384]{2,1,0:T(8,128)} %bitcast.32, f32[4,64,384]{2,1,0:T(8,128)} %collective-permute-done.refs_3_, f32[4,64,384]{2,1,0:T(8,128)} %copy-done.8, ...), custom_call_target="tpu_custom_call" | custom-call | flops 47185920 | bytes 31457280 | tf_op jit(solution)/shard_map/leap_adj1/pallas_call | solution.py:155
  177.6 2.0 fusion.1
  179.6 1.3 collective-permute-start.13
  180.9 4.0 %collective-permute-start.12 = (f32[4,64,384]{2,1,0:T(8,128)S(1)}, f32[4,64,384]{2,1,0:T(8,128)S(1)}, u32[]{:S(2)}, u32[]{:S(2)}) collective-permute-start(f32[4,64,384]{2,1,0:T(8,128)S(1)} %get-tuple-element.19), channel_id=1, source_target_pairs={{0,4},{4,8},{8,12},{12,16},{16,20},{20,24},{24,28},{1,5},{5,9},{9,... | collective-permute-start | bytes 1179656 | tf_op jit(solution)/shard_map/ppermute | solution.py:25
  184.9 1.9 fusion
  186.8 1.9 collective-permute-start.15
  188.7 6.5 %collective-permute-start.14 = (f32[32,4,384]{2,1,0:T(4,128)S(1)}, f32[32,4,384]{2,1,0:T(4,128)}, u32[]{:S(2)}, u32[]{:S(2)}) collective-permute-start(f32[32,4,384]{2,1,0:T(4,128)S(1)} %get-tuple-element.17), channel_id=1, source_target_pairs={{0,1},{1,2},{2,3},{4,5},{5,6},{6,7},{8,9},{9,10},{10,11},{12,13},{... | collective-permute-start | bytes 589832 | tf_op jit(solution)/shard_map/ppermute | solution.py:25
  195.1 0.4 copy.23
  195.6 1.1 sub.15.refs_10_
  196.7 1.8 collective-permute-done.15
  198.5 1.7 pad.33.refs_6_
  200.2 1.7 pad.32.refs_5_
  201.9 0.0 copy-start.5
  201.9 0.7 copy-done.4
  202.7 0.1 copy-done.5
  202.8 15.7 %leap_adj2.1.img_ref = f32[32,64,384]{2,1,0:T(8,128)} custom-call(f32[32,64,384]{2,1,0:T(8,128)} %get-tuple-element.12.refs_0_.refs_1_.refs_2_, f32[32,64,384]{2,1,0:T(8,128)} %get-tuple-element.12.refs_0_.refs_1_.refs_2_, f32[32,64,384]{2,1,0:T(8,128)} %get-tuple-element.12.refs_0_.refs_1_.refs_2_, f32[4,64,384]{2,1,0:T(8,128)} %copy-done.5, ...), custom_call_target="tpu_custom_call" | custom-call | flops 47185920 | bytes 31457280 | tf_op jit(solution)/shard_map/leap_adj2/pallas_call | solution.py:155
  218.5 33.7 %kick_reduce_scatter.1 = (f32[8,64,384]{2,1,0:T(8,128)S(1)}, f32[8,64,384]{2,1,0:T(8,128)S(1)}) custom-call(f32[32,64,384]{2,1,0:T(8,128)} %leap_adj2.1.img_ref, f32[8,64,384]{2,1,0:T(8,128)S(1)} %copy-done, f32[8,64,384]{2,1,0:T(8,128)S(1)} %copy-done.1, f32[8,64,384]{2,1,0:T(8,128)S(1)} %copy-done.2), custom_call_target="tpu_custom_call" | custom-call | tf_op jit(solution)/shard_map/kick_reduce_scatter/pallas_call | solution.py:226
  252.2 0.9 copy.27
  253.1 0.9 copy.28
  (33 shorter events, 0.1 us)
Async XLA Ops:
  7.2 19.8 %copy-start.12 = (s32[1,32,64]{2,1,0:T(8,128)S(1)}, s32[1,32,64]{2,1,0:T(8,128)}, u32[]{:S(2)}) copy-start(s32[1,32,64]{2,1,0:T(8,128)} %param.19) | copy-start | bytes 24580
  7.2 21.2 %copy-start.13 = (s32[1,3]{1,0:T(1,128)S(1)}, s32[1,3]{1,0:T(1,128)}, u32[]{:S(2)}) copy-start(s32[1,3]{1,0:T(1,128)} %param.20) | copy-start | bytes 40
  7.2 24.4 %copy-start.14 = (f32[1,2]{1,0:T(1,128)S(1)}, f32[1,2]{1,0:T(1,128)}, u32[]{:S(2)}) copy-start(f32[1,2]{1,0:T(1,128)} %param.21) | copy-start | bytes 28
  7.2 45.5 %all-gather.2.cloned.1.call-start = ((), (), s32[]{:S(2)}) async-start(), calls=%async_computation | async-start | bytes 3932160 | tf_op jit(solution)/shard_map/all_gather | solution.py:255
  9.1 23.0 %collective-permute-start.7 = (f32[32,4,384]{2,1,0:T(4,128)S(1)}, f32[32,4,384]{2,1,0:T(4,128)S(1)}, u32[]{:S(2)}, u32[]{:S(2)}) collective-permute-start(f32[32,4,384]{2,1,0:T(4,128)S(1)} %get-tuple-element.24), channel_id=1, source_target_pairs={{1,0},{2,1},{3,2},{5,4},{6,5},{7,6},{9,8},{10,9},{11,10},{13,12},{... | collective-permute-start | bytes 589832 | tf_op jit(solution)/shard_map/ppermute | solution.py:26
  12.5 25.7 %collective-permute-start.6 = (f32[32,4,384]{2,1,0:T(4,128)S(1)}, f32[32,4,384]{2,1,0:T(4,128)S(1)}, u32[]{:S(2)}, u32[]{:S(2)}) collective-permute-start(f32[32,4,384]{2,1,0:T(4,128)S(1)} %get-tuple-element.25), channel_id=1, source_target_pairs={{0,1},{1,2},{2,3},{4,5},{5,6},{6,7},{8,9},{9,10},{10,11},{12,13},{... | collective-permute-start | bytes 589832 | tf_op jit(solution)/shard_map/ppermute | solution.py:25
  18.4 20.5 %collective-permute-start.5 = (f32[4,64,384]{2,1,0:T(8,128)S(1)}, f32[4,64,384]{2,1,0:T(8,128)S(1)}, u32[]{:S(2)}, u32[]{:S(2)}) collective-permute-start(f32[4,64,384]{2,1,0:T(8,128)S(1)} %get-tuple-element.26), channel_id=1, source_target_pairs={{4,0},{8,4},{12,8},{16,12},{20,16},{24,20},{28,24},{5,1},{9,5},{13... | collective-permute-start | bytes 1179656 | tf_op jit(solution)/shard_map/ppermute | solution.py:26
  19.7 19.2 %collective-permute-start.4 = (f32[4,64,384]{2,1,0:T(8,128)S(1)}, f32[4,64,384]{2,1,0:T(8,128)S(1)}, u32[]{:S(2)}, u32[]{:S(2)}) collective-permute-start(f32[4,64,384]{2,1,0:T(8,128)S(1)} %get-tuple-element.27), channel_id=1, source_target_pairs={{0,4},{4,8},{8,12},{12,16},{16,20},{20,24},{24,28},{1,5},{5,9},{9,... | collective-permute-start | bytes 1179656 | tf_op jit(solution)/shard_map/ppermute | solution.py:25
  25.0 69.6 %collective-permute-start.3 = (f32[32,4,384]{2,1,0:T(4,128)S(1)}, f32[32,4,384]{2,1,0:T(4,128)S(1)}, u32[]{:S(2)}, u32[]{:S(2)}) collective-permute-start(f32[32,4,384]{2,1,0:T(4,128)S(1)} %get-tuple-element.28), channel_id=1, source_target_pairs={{1,0},{2,1},{3,2},{5,4},{6,5},{7,6},{9,8},{10,9},{11,10},{13,12},{... | collective-permute-start | bytes 589832 | tf_op jit(solution)/shard_map/ppermute | solution.py:26
  32.1 63.8 %collective-permute-start.2 = (f32[32,4,384]{2,1,0:T(4,128)S(1)}, f32[32,4,384]{2,1,0:T(4,128)}, u32[]{:S(2)}, u32[]{:S(2)}) collective-permute-start(f32[32,4,384]{2,1,0:T(4,128)S(1)} %get-tuple-element.29), channel_id=1, source_target_pairs={{0,1},{1,2},{2,3},{4,5},{5,6},{6,7},{8,9},{9,10},{10,11},{12,13},{... | collective-permute-start | bytes 589832 | tf_op jit(solution)/shard_map/ppermute | solution.py:25
  38.9 13.8 %copy-start.6 = (f32[4,64,384]{2,1,0:T(8,128)}, f32[4,64,384]{2,1,0:T(8,128)S(1)}, u32[]{:S(2)}) copy-start(f32[4,64,384]{2,1,0:T(8,128)S(1)} %collective-permute-done.5.refs_4_) | copy-start | bytes 1179652
  38.9 13.8 %copy-start.7 = (f32[4,64,384]{2,1,0:T(8,128)}, f32[4,64,384]{2,1,0:T(8,128)S(1)}, u32[]{:S(2)}) copy-start(f32[4,64,384]{2,1,0:T(8,128)S(1)} %collective-permute-done.4.refs_3_) | copy-start | bytes 1179652
  81.8 24.8 %copy-start.11 = (f32[1,2,32,64]{3,2,1,0:T(8,128)S(1)}, f32[1,2,32,64]{3,2,1,0:T(8,128)}, u32[]{:S(2)}) copy-start(f32[1,2,32,64]{3,2,1,0:T(8,128)} %param.18) | copy-start | bytes 49156
  84.8 15.9 %collective-permute-start.11 = (f32[32,4,384]{2,1,0:T(4,128)S(1)}, f32[32,4,384]{2,1,0:T(4,128)}, u32[]{:S(2)}, u32[]{:S(2)}) collective-permute-start(f32[32,4,384]{2,1,0:T(4,128)S(1)} %get-tuple-element.20), channel_id=1, source_target_pairs={{1,0},{2,1},{3,2},{5,4},{6,5},{7,6},{9,8},{10,9},{11,10},{13,12},{... | collective-permute-start | bytes 589832 | tf_op jit(solution)/shard_map/ppermute | solution.py:26
  87.4 42.0 %collective-permute-start.9 = (f32[4,64,384]{2,1,0:T(8,128)S(1)}, f32[4,64,384]{2,1,0:T(8,128)S(1)}, u32[]{:S(2)}, u32[]{:S(2)}) collective-permute-start(f32[4,64,384]{2,1,0:T(8,128)S(1)} %get-tuple-element.22), channel_id=1, source_target_pairs={{4,0},{8,4},{12,8},{16,12},{20,16},{24,20},{28,24},{5,1},{9,5},{13... | collective-permute-start | bytes 1179656 | tf_op jit(solution)/shard_map/ppermute | solution.py:26
  88.7 40.7 %collective-permute-start.8 = (f32[4,64,384]{2,1,0:T(8,128)S(1)}, f32[4,64,384]{2,1,0:T(8,128)}, u32[]{:S(2)}, u32[]{:S(2)}) collective-permute-start(f32[4,64,384]{2,1,0:T(8,128)S(1)} %get-tuple-element.23), channel_id=1, source_target_pairs={{0,4},{4,8},{8,12},{12,16},{16,20},{20,24},{24,28},{1,5},{5,9},{9,... | collective-permute-start | bytes 1179656 | tf_op jit(solution)/shard_map/ppermute | solution.py:25
  94.6 11.9 %copy-start.10 = (f32[32,4,384]{2,1,0:T(4,128)}, f32[32,4,384]{2,1,0:T(4,128)S(1)}, u32[]{:S(2)}) copy-start(f32[32,4,384]{2,1,0:T(4,128)S(1)} %collective-permute-done.3) | copy-start | bytes 589828
  94.7 66.7 %collective-permute-start.1 = (f32[4,64,384]{2,1,0:T(8,128)S(1)}, f32[4,64,384]{2,1,0:T(8,128)S(1)}, u32[]{:S(2)}, u32[]{:S(2)}) collective-permute-start(f32[4,64,384]{2,1,0:T(8,128)S(1)} %get-tuple-element.30), channel_id=1, source_target_pairs={{4,0},{8,4},{12,8},{16,12},{20,16},{24,20},{28,24},{5,1},{9,5},{13... | collective-permute-start | bytes 1179656 | tf_op jit(solution)/shard_map/ppermute | solution.py:26
  96.0 65.4 %collective-permute-start = (f32[4,64,384]{2,1,0:T(8,128)S(1)}, f32[4,64,384]{2,1,0:T(8,128)}, u32[]{:S(2)}, u32[]{:S(2)}) collective-permute-start(f32[4,64,384]{2,1,0:T(8,128)S(1)} %get-tuple-element.31), channel_id=1, source_target_pairs={{0,4},{4,8},{8,12},{12,16},{16,20},{20,24},{24,28},{1,5},{5,9},{9,... | collective-permute-start | bytes 1179656 | tf_op jit(solution)/shard_map/ppermute | solution.py:25
  100.7 27.0 %collective-permute-start.10 = (f32[32,4,384]{2,1,0:T(4,128)}, f32[32,4,384]{2,1,0:T(4,128)}, u32[]{:S(2)}, u32[]{:S(2)}) collective-permute-start(f32[32,4,384]{2,1,0:T(4,128)} %get-tuple-element.21), channel_id=1, source_target_pairs={{0,1},{1,2},{2,3},{4,5},{5,6},{6,7},{8,9},{9,10},{10,11},{12,13},{... | collective-permute-start | bytes 589832 | tf_op jit(solution)/shard_map/ppermute | solution.py:25
  129.4 0.7 copy-start.9
  161.4 0.7 copy-start.8
  177.6 18.0 %copy-start.3 = (f32[32,64,1]{2,1,0:T(8,128)S(1)}, f32[32,64,1]{2,1,0:T(8,128)}, u32[]{:S(2)}) copy-start(f32[32,64,1]{2,1,0:T(8,128)} %get-tuple-element.13) | copy-start | bytes 24580
  179.6 22.3 %collective-permute-start.13 = (f32[4,64,384]{2,1,0:T(8,128)}, f32[4,64,384]{2,1,0:T(8,128)S(1)}, u32[]{:S(2)}, u32[]{:S(2)}) collective-permute-start(f32[4,64,384]{2,1,0:T(8,128)} %get-tuple-element.18), channel_id=1, source_target_pairs={{4,0},{8,4},{12,8},{16,12},{20,16},{24,20},{28,24},{5,1},{9,5},{13... | collective-permute-start | bytes 1179656 | tf_op jit(solution)/shard_map/ppermute | solution.py:26
  180.9 21.0 %collective-permute-start.12 = (f32[4,64,384]{2,1,0:T(8,128)S(1)}, f32[4,64,384]{2,1,0:T(8,128)S(1)}, u32[]{:S(2)}, u32[]{:S(2)}) collective-permute-start(f32[4,64,384]{2,1,0:T(8,128)S(1)} %get-tuple-element.19), channel_id=1, source_target_pairs={{0,4},{4,8},{8,12},{12,16},{16,20},{20,24},{24,28},{1,5},{5,9},{9,... | collective-permute-start | bytes 1179656 | tf_op jit(solution)/shard_map/ppermute | solution.py:25
  186.8 11.7 %collective-permute-start.15 = (f32[32,4,384]{2,1,0:T(4,128)}, f32[32,4,384]{2,1,0:T(4,128)}, u32[]{:S(2)}, u32[]{:S(2)}) collective-permute-start(f32[32,4,384]{2,1,0:T(4,128)} %get-tuple-element.16), channel_id=1, source_target_pairs={{1,0},{2,1},{3,2},{5,4},{6,5},{7,6},{9,8},{10,9},{11,10},{13,12},{... | collective-permute-start | bytes 589832 | tf_op jit(solution)/shard_map/ppermute | solution.py:26
  188.7 11.5 %collective-permute-start.14 = (f32[32,4,384]{2,1,0:T(4,128)S(1)}, f32[32,4,384]{2,1,0:T(4,128)}, u32[]{:S(2)}, u32[]{:S(2)}) collective-permute-start(f32[32,4,384]{2,1,0:T(4,128)S(1)} %get-tuple-element.17), channel_id=1, source_target_pairs={{0,1},{1,2},{2,3},{4,5},{5,6},{6,7},{8,9},{9,10},{10,11},{12,13},{... | collective-permute-start | bytes 589832 | tf_op jit(solution)/shard_map/ppermute | solution.py:25
  201.9 0.7 copy-start.4
  201.9 0.9 copy-start.5
  202.8 15.7 %copy-start = (f32[8,64,384]{2,1,0:T(8,128)S(1)}, f32[8,64,384]{2,1,0:T(8,128)}, u32[]{:S(2)}) copy-start(f32[8,64,384]{2,1,0:T(8,128)} %vel_ref.1) | copy-start | bytes 2359300
  202.8 15.7 %copy-start.1 = (f32[8,64,384]{2,1,0:T(8,128)S(1)}, f32[8,64,384]{2,1,0:T(8,128)}, u32[]{:S(2)}) copy-start(f32[8,64,384]{2,1,0:T(8,128)} %mom_ref.1) | copy-start | bytes 2359300
  202.8 15.7 %copy-start.2 = (f32[8,64,384]{2,1,0:T(8,128)S(1)}, f32[8,64,384]{2,1,0:T(8,128)}, u32[]{:S(2)}) copy-start(f32[8,64,384]{2,1,0:T(8,128)} %mass_ref.1) | copy-start | bytes 2359300
Sparse Core Ops, SparseCore 0:
  9.7 42.9 all-gather.1

commit v3 on v2

--- a/solution.py
+++ b/solution.py
@@ -15,20 +15,107 @@
 Y_CHUNK = 8
 
 
-def halos(block):
-    out = []
-    for axis, dim in (("row", 0), ("col", 1)):
-        count = lax.axis_size(axis)
-        forward = [(i, i + 1) for i in range(count - 1)]
-        backward = [(target, source) for source, target in forward]
-        size = block.shape[dim]
-        low = lax.ppermute(lax.slice_in_dim(block, size - 4, None, axis=dim), axis, forward)
-        high = lax.ppermute(lax.slice_in_dim(block, 0, 4, axis=dim), axis, backward)
-        out += [low, high]
-    xlo, xhi, ylo, yhi = out
-    ylo = jnp.pad(ylo, ((0, 0), (4, 0), (0, 0)))
-    yhi = jnp.pad(yhi, ((0, 0), (0, 4), (0, 0)))
-    return xlo, xhi, ylo, yhi
+def exchange_kernel(nf, *refs):
+    fields = refs[:nf]
+    bufs = refs[nf : 5 * nf]
+    zero_x, zero_y, send_sem, recv_sem, zero_sem = refs[5 * nf :]
+    mesh = pl.DeviceIdType.MESH
+    row, nrow = lax.axis_index("row"), lax.axis_size("row")
+    col, ncol = lax.axis_index("col"), lax.axis_size("col")
+    rows, cols, depth = fields[0].shape
+    has = (row < nrow - 1, row > 0, col < ncol - 1, col > 0)
+    peer = ({"row": row + 1}, {"row": row - 1}, {"col": col + 1}, {"col": col - 1})
+    filler = (1, 0, 3, 2)
+
+    def source(f, d):
+        if d == 0:
+            return f.at[pl.ds(rows - 4, 4)]
+        if d == 1:
+            return f.at[pl.ds(0, 4)]
+        if d == 2:
+            return f.at[:, pl.ds(cols - 8, 8)]
+        return f.at[:, pl.ds(0, 8)]
+
+    def remote(j, d, b):
+        return pltpu.make_async_remote_copy(
+            src_ref=source(fields[j], d),
+            dst_ref=bufs[4 * j + b],
+            send_sem=send_sem.at[j, d],
+            recv_sem=recv_sem.at[j, b],
+            device_id=peer[d],
+            device_id_type=mesh,
+        )
+
+    barrier = pltpu.get_barrier_semaphore()
+    for d in range(4):
+        @pl.when(has[d])
+        def _():
+            pl.semaphore_signal(barrier, inc=1, device_id=peer[d], device_id_type=mesh)
+
+    count = (1 - row // (nrow - 1)) + (row + nrow - 1) // nrow + (1 - col // (ncol - 1)) + (col + ncol - 1) // ncol
+    pl.semaphore_wait(barrier, count)
+
+    for j in range(nf):
+        for d in range(4):
+            @pl.when(has[d])
+            def _():
+                remote(j, d, d).start()
+
+    @pl.when(jnp.logical_not(has[0] & has[1]))
+    def _():
+        zero_x[...] = jnp.zeros_like(zero_x)
+
+    @pl.when(jnp.logical_not(has[2] & has[3]))
+    def _():
+        zero_y[...] = jnp.zeros_like(zero_y)
+
+    for j in range(nf):
+        for b in range(4):
+            @pl.when(jnp.logical_not(has[filler[b]]))
+            def _():
+                copy = pltpu.make_async_copy(zero_x if b < 2 else zero_y, bufs[4 * j + b], zero_sem.at[j, b])
+                copy.start()
+                copy.wait()
+
+    for j in range(nf):
+        for d in range(4):
+            @pl.when(has[d])
+            def _():
+                remote(j, d, d).wait_send()
+        for b in range(4):
+            @pl.when(has[filler[b]])
+            def _():
+                remote(j, b, b).wait_recv()
+
+
+def exchange(fields, collective_id):
+    nf = len(fields)
+    rows, cols, depth = fields[0].shape
+    any_spec = pl.BlockSpec(memory_space=pl.ANY)
+    shapes = []
+    for _ in range(nf):
+        shapes += [
+            jax.ShapeDtypeStruct((4, cols, depth), jnp.float32),
+            jax.ShapeDtypeStruct((4, cols, depth), jnp.float32),
+            jax.ShapeDtypeStruct((rows, 8, depth), jnp.float32),
+            jax.ShapeDtypeStruct((rows, 8, depth), jnp.float32),
+        ]
+    outs = pl.pallas_call(
+        functools.partial(exchange_kernel, nf),
+        in_specs=[any_spec] * nf,
+        out_specs=[any_spec] * (4 * nf),
+        out_shape=shapes,
+        scratch_shapes=[
+            pltpu.VMEM((4, cols, depth), jnp.float32),
+            pltpu.VMEM((rows, 8, depth), jnp.float32),
+            pltpu.SemaphoreType.DMA((nf, 4)),
+            pltpu.SemaphoreType.DMA((nf, 4)),
+            pltpu.SemaphoreType.DMA((nf, 4)),
+        ],
+        compiler_params=pltpu.CompilerParams(collective_id=collective_id, has_side_effects=True),
+        name=f"halo_exchange_{collective_id}",
+    )(*fields)
+    return [outs[4 * j : 4 * j + 4] for j in range(nf)]
 
 
 def step_kernel(kind, *refs):
@@ -269,14 +356,13 @@
     ).astype(jnp.int32)
     amp = wavelet[0]
 
-    wave_h = halos(present)
-    adj_h = halos(adj_now)
+    wave_h, adj_h = exchange([present, adj_now], 1)
     advanced, dw1, pick_adv = leap("wave1", present, *wave_h, oldest, full_velocity, rec, src, amp[0:1])
-    dw2, pick_far = leap("wave2", advanced, *halos(advanced), present, full_velocity, rec, src, amp[1:2])
+    dw2, pick_far = leap("wave2", advanced, *exchange([advanced], 2)[0], present, full_velocity, rec, src, amp[1:2])
     misfit_late = pick_far - observed[0, 1][:, :, None]
     misfit_early = pick_adv - observed[0, 0][:, :, None]
     adj_two, part = leap("adj1", adj_now, *adj_h, adj_later, full_velocity, rec, misfit_late, dw2)
-    (imaging,) = leap("adj2", adj_two, *halos(adj_two), adj_now, full_velocity, rec, misfit_early, dw1, part)
+    (imaging,) = leap("adj2", adj_two, *exchange([adj_two], 3)[0], adj_now, full_velocity, rec, misfit_early, dw1, part)
     v_new, p_half = kick(imaging, velocity, momentum, mass_diag)
     return (v_new, p_half)
 

time: 262 us -> 249 us (0.950)
  Pallas kernels: 123 us -> 221 us
  starting transfers between devices: 54.7 us -> 0.04 us
  waiting for transfers between devices: 31.8 us -> 0.68 us
  local copies, waits for them, and re-layouts: 31.2 us -> 6.6 us
    pallas_call x0 -> x3, Pallas kernels: none -> 97.9 us  [exchange(): pl.pallas_call(functools.partial(exchange_kernel, nf), in_specs=[any_spec...]
    ppermute x16 -> x0, starting transfers between devices: 54.6 us -> none  [the longest x8 39.7 us: halos(): lax.ppermute(lax.slice_in_dim(block, size - 4, None, axis=dim), axis, for...]
    ppermute x16 -> x0, waiting for transfers between devices: 17.4 us -> none  [the longest x8 15.6 us: halos(): lax.ppermute(lax.slice_in_dim(block, size - 4, None, axis=dim), axis, for...]
    all_gather x1, waiting for transfers between devices: 13.8 us -> 0.01 us  [on_device(): full_velocity = lax.all_gather(velocity, 'shot', axis=0, tiled=True)]
    pad x8 -> x0, local copies, waits for them, and re-layouts: 11.9 us -> none  [the longest x4 5.96 us: halos(): ylo = jnp.pad(ylo, ((0, 0), (4, 0), (0, 0)))]
    slice x8 -> x0, local copies, waits for them, and re-layouts: 11.7 us -> none  [halos(): high = lax.ppermute(lax.slice_in_dim(block, 0, 4, axis=dim), axis, backward)]
  transfers between devices with their start and end apart: 17 -> 1, of which waited for: 3 -> 0; matrix products, arithmetic and copies ran while one was open for 11% -> 2% of each run, Pallas kernels for 22% -> 20%
where the time goes in v3:
time: 249 us; the launch traced here: 248 us
  Pallas kernels  221 us (89%)
  between operations  15.4 us (6%)
  local copies, waits for them, and re-layouts  6.6 us (3%)
  other arithmetic  4.72 us (2%)
    pallas_call x3, Pallas kernels, exchange(): pl.pallas_call(functools.partial(exchange_kernel, nf), in_specs=[any_spec...  97.9 us
    pallas_call x4, Pallas kernels, leap(): pl.pallas_call(functools.partial(step_kernel, kind), grid=grid, in_specs=...  89 us
    pallas_call x1, Pallas kernels, kick(): pl.pallas_call(kick_kernel, in_specs=[pl.BlockSpec(memory_space=pl.ANY),...  34 us
  transfers between devices with their start and end apart: 1, of which 0 were waited for; matrix products, arithmetic and copies ran while one was open for 2% of the time, Pallas kernels for 20%

profile of v3, /device:TPU:1, one launch (start us, length us, event | category | flops | bytes accessed | tf_op | source)
XLA Modules:
  0.0 248.4 jit_solution(14045555707316064283)
XLA Ops:
  7.2 0.0 copy-start.4
  7.2 0.0 all-gather.2.cloned.1.call-start
  7.2 0.7 all-gather.2.cloned.1.call-update
  7.9 0.7 slice_bitcast_fusion
  8.7 0.4 copy.23
  9.1 2.1 copy.22.refs_9_
  11.2 0.4 copy.21
  11.6 0.0 copy-done.4
  11.6 0.6 fusion.1
  13.4 0.0 copy-start.5
  13.4 48.5 %halo_exchange_1.1 = (f32[4,64,384]{2,1,0:T(8,128)}, f32[4,64,384]{2,1,0:T(8,128)}, f32[32,8,384]{2,1,0:T(8,128)}, f32[32,8,384]{2,1,0:T(8,128)}, f32[4,64,384]{...) custom-call(f32[32,64,384]{2,1,0:T(8,128)} %bitcast.16, f32[32,64,384]{2,1,0:T(8,128)} %bitcast.21), custom_call_target="tpu_custom_call" | custom-call | tf_op jit(solution)/shard_map/halo_exchange_1/pallas_call | solution.py:103
  61.9 1.2 pad_add_fusion.refs_10_
  63.1 0.0 copy-done.5
  63.1 0.6 fusion
  63.7 0.0 all-gather.2.cloned.1.call-done.refs_8_
  63.7 29.1 %leap_wave1.1 = (f32[32,64,384]{2,1,0:T(8,128)}, f32[32,64,384]{2,1,0:T(8,128)}, f32[32,64,1]{2,1,0:T(8,128)}) custom-call(f32[32,64,384]{2,1,0:T(8,128)} %bitcast.17, f32[32,64,384]{2,1,0:T(8,128)} %bitcast.18, f32[32,64,384]{2,1,0:T(8,128)} %bitcast.19, f32[4,64,384]{2,1,0:T(8,128)} %get-tuple-element.29.refs_3_, f32[4,64,384]{2,1,0:T(8,128)} %get-tuple-element.30.refs_4_, ...), custom_call_target="tpu_custom_call" | custom-call | flops 47185920 | bytes 34603008 | tf_op jit(solution)/shard_map/leap_wave1/pallas_call | solution.py:242
  92.8 24.7 %halo_exchange_2.1 = (f32[4,64,384]{2,1,0:T(8,128)}, f32[4,64,384]{2,1,0:T(8,128)}, f32[32,8,384]{2,1,0:T(8,128)}, f32[32,8,384]{2,1,0:T(8,128)}) custom-call(f32[32,64,384]{2,1,0:T(8,128)} %get-tuple-element.33.refs_0_.refs_1_.refs_2_), custom_call_target="tpu_custom_call" | custom-call | tf_op jit(solution)/shard_map/halo_exchange_2/pallas_call | solution.py:103
  117.6 28.9 %leap_wave2.1 = (f32[32,64,384]{2,1,0:T(8,128)}, f32[32,64,1]{2,1,0:T(8,128)}) custom-call(f32[32,64,384]{2,1,0:T(8,128)} %get-tuple-element.33.refs_0_.refs_1_.refs_2_, f32[32,64,384]{2,1,0:T(8,128)} %get-tuple-element.33.refs_0_.refs_1_.refs_2_, f32[32,64,384]{2,1,0:T(8,128)} %get-tuple-element.33.refs_0_.refs_1_.refs_2_, ...), custom_call_target="tpu_custom_call" | custom-call | flops 47185920 | bytes 31457280 | tf_op jit(solution)/shard_map/leap_wave2/pallas_call | solution.py:242
  146.4 2.4 sub.14.refs_10_
  148.8 15.4 %leap_adj1.1 = (f32[32,64,384]{2,1,0:T(8,128)}, f32[32,64,384]{2,1,0:T(8,128)}) custom-call(f32[32,64,384]{2,1,0:T(8,128)} %bitcast.22, f32[32,64,384]{2,1,0:T(8,128)} %bitcast.23, f32[32,64,384]{2,1,0:T(8,128)} %bitcast.24, f32[4,64,384]{2,1,0:T(8,128)} %get-tuple-element.25.refs_3_, f32[4,64,384]{2,1,0:T(8,128)} %get-tuple-element.26.refs_4_, ...), custom_call_target="tpu_custom_call" | custom-call | flops 47185920 | bytes 31457280 | tf_op jit(solution)/shard_map/leap_adj1/pallas_call | solution.py:242
  164.2 0.0 copy-start.3
  164.2 24.7 %halo_exchange_3.1 = (f32[4,64,384]{2,1,0:T(8,128)}, f32[4,64,384]{2,1,0:T(8,128)}, f32[32,8,384]{2,1,0:T(8,128)}, f32[32,8,384]{2,1,0:T(8,128)}) custom-call(f32[32,64,384]{2,1,0:T(8,128)} %get-tuple-element.40.refs_0_.refs_1_.refs_2_), custom_call_target="tpu_custom_call" | custom-call | tf_op jit(solution)/shard_map/halo_exchange_3/pallas_call | solution.py:103
  188.9 0.0 copy-done.3
  188.9 1.1 sub.15.refs_10_
  190.0 0.0 copy-start
  190.0 0.0 copy-start.1
  190.1 0.0 copy-start.2
  190.1 15.7 %leap_adj2.1.img_ref = f32[32,64,384]{2,1,0:T(8,128)} custom-call(f32[32,64,384]{2,1,0:T(8,128)} %get-tuple-element.40.refs_0_.refs_1_.refs_2_, f32[32,64,384]{2,1,0:T(8,128)} %get-tuple-element.40.refs_0_.refs_1_.refs_2_, f32[32,64,384]{2,1,0:T(8,128)} %get-tuple-element.40.refs_0_.refs_1_.refs_2_, f32[4,64,384]{2,1,0:T(8,128)} %get-tuple-element.41.refs_3_, ...), custom_call_target="tpu_custom_call" | custom-call | flops 47185920 | bytes 31457280 | tf_op jit(solution)/shard_map/leap_adj2/pallas_call | solution.py:242
  205.7 0.0 copy-done
  205.7 0.0 copy-done.1
  205.7 0.0 copy-done.2
  205.8 34.0 %kick_reduce_scatter.1 = (f32[8,64,384]{2,1,0:T(8,128)S(1)}, f32[8,64,384]{2,1,0:T(8,128)S(1)}) custom-call(f32[32,64,384]{2,1,0:T(8,128)} %leap_adj2.1.img_ref, f32[8,64,384]{2,1,0:T(8,128)S(1)} %copy-done, f32[8,64,384]{2,1,0:T(8,128)S(1)} %copy-done.1, f32[8,64,384]{2,1,0:T(8,128)S(1)} %copy-done.2), custom_call_target="tpu_custom_call" | custom-call | tf_op jit(solution)/shard_map/kick_reduce_scatter/pallas_call | solution.py:313
  239.8 0.9 copy.27
  240.7 0.9 copy.28
Async XLA Ops:
  7.2 4.4 %copy-start.4 = (s32[1,3]{1,0:T(1,128)S(1)}, s32[1,3]{1,0:T(1,128)}, u32[]{:S(2)}) copy-start(s32[1,3]{1,0:T(1,128)} %param.20) | copy-start | bytes 40
  7.2 56.5 %all-gather.2.cloned.1.call-start = ((), (), s32[]{:S(2)}) async-start(), calls=%async_computation | async-start | bytes 3932160 | tf_op jit(solution)/shard_map/all_gather | solution.py:342
  13.4 49.7 %copy-start.5 = (f32[1,2]{1,0:T(1,128)S(1)}, f32[1,2]{1,0:T(1,128)}, u32[]{:S(2)}) copy-start(f32[1,2]{1,0:T(1,128)} %param.21) | copy-start | bytes 28
  164.2 24.8 %copy-start.3 = (f32[32,64,1]{2,1,0:T(8,128)S(1)}, f32[32,64,1]{2,1,0:T(8,128)}, u32[]{:S(2)}) copy-start(f32[32,64,1]{2,1,0:T(8,128)} %get-tuple-element.45) | copy-start | bytes 24580
  190.0 15.7 %copy-start = (f32[8,64,384]{2,1,0:T(8,128)S(1)}, f32[8,64,384]{2,1,0:T(8,128)}, u32[]{:S(2)}) copy-start(f32[8,64,384]{2,1,0:T(8,128)} %vel_ref.1) | copy-start | bytes 2359300
  190.0 15.7 %copy-start.1 = (f32[8,64,384]{2,1,0:T(8,128)S(1)}, f32[8,64,384]{2,1,0:T(8,128)}, u32[]{:S(2)}) copy-start(f32[8,64,384]{2,1,0:T(8,128)} %mom_ref.1) | copy-start | bytes 2359300
  190.1 15.7 %copy-start.2 = (f32[8,64,384]{2,1,0:T(8,128)S(1)}, f32[8,64,384]{2,1,0:T(8,128)}, u32[]{:S(2)}) copy-start(f32[8,64,384]{2,1,0:T(8,128)} %mass_ref.1) | copy-start | bytes 2359300
Sparse Core Ops, SparseCore 0:
  9.7 42.9 all-gather.1

commit v4 on v3

--- a/solution.py
+++ b/solution.py
@@ -133,8 +133,12 @@
     elif kind == "adj2":
         dw_ref, part_ref = rest[:2]
         rest = rest[2:]
-    outs = rest[:-1]
-    pad = rest[-1]
+    if kind in ("wave1", "wave2"):
+        outs = rest[:-3]
+        picked_ref, pad, fold = rest[-3:]
+    else:
+        outs = rest[:-1]
+        pad = rest[-1]
 
     tb, cols, depth = f_ref.shape
     i = pl.program_id(0)
@@ -179,8 +183,12 @@
             if kind in ("wave1", "wave2"):
                 hit = (r == src_x) & (y_index + y0 == src_y) & (z_index == src_z)
                 out = out + jnp.where(hit, amp, 0.0)
-                picked = jnp.sum(jnp.where(at_rec, out, 0.0), axis=1, keepdims=True)
-                outs_now = [(out - 2.0 * c) + prev, picked]
+                sel = jnp.where(at_rec, out, 0.0)
+                folded = sel[:, 0:128]
+                for t in range(128, depth, 128):
+                    folded = folded + sel[:, t : t + 128]
+                fold[pl.ds(pl.multiple_of(r * cols + y0, Y_CHUNK), Y_CHUNK), :] = folded
+                outs_now = [(out - 2.0 * c) + prev]
                 if kind == "wave1":
                     outs_now = [out] + outs_now
             else:
@@ -195,6 +203,8 @@
         return carry
 
     lax.fori_loop(0, tb, row, 0)
+    if kind in ("wave1", "wave2"):
+        picked_ref[...] = jnp.sum(fold[...], axis=1, keepdims=True).reshape(picked_ref.shape)
 
 
 def leap(kind, f, xlo, xhi, ylo, yhi, prev, vel, rec, *extra):
@@ -245,7 +255,8 @@
         in_specs=in_specs,
         out_specs=out_specs,
         out_shape=out_shape,
-        scratch_shapes=[pltpu.VMEM((tb + 8, cols + 16, depth), jnp.float32)],
+        scratch_shapes=[pltpu.VMEM((tb + 8, cols + 16, depth), jnp.float32)]
+        + ([pltpu.VMEM((tb * cols, 128), jnp.float32)] if kind in ("wave1", "wave2") else []),
         compiler_params=pltpu.CompilerParams(vmem_limit_bytes=60 * 1024 * 1024),
         cost_estimate=cost,
         name=f"leap_{kind}",

time: 249 us -> 223 us (0.90)
  Pallas kernels: 221 us -> 195 us
    pallas_call x4, Pallas kernels: 89 us -> 63.2 us  [leap(): pl.pallas_call(functools.partial(step_kernel, kind), grid=grid, in_specs=...]
  transfers between devices with their start and end apart: 1 -> 1, of which waited for: 0 -> 0; matrix products, arithmetic and copies ran while one was open for 2% -> 3% of each run, Pallas kernels for 20% -> 22%
where the time goes in v4:
time: 223 us
  Pallas kernels  195 us (87%)
  between operations  15.4 us (7%)
  local copies, waits for them, and re-layouts  6.6 us (3%)
  other arithmetic  4.72 us (2%)
    pallas_call x3, Pallas kernels, exchange(): pl.pallas_call(functools.partial(exchange_kernel, nf), in_specs=[any_spec...  97.9 us
    pallas_call x4, Pallas kernels, leap(): pl.pallas_call(functools.partial(step_kernel, kind), grid=grid, in_specs=...  63.2 us
    pallas_call x1, Pallas kernels, kick(): pl.pallas_call(kick_kernel, in_specs=[pl.BlockSpec(memory_space=pl.ANY),...  34 us
  transfers between devices with their start and end apart: 1, of which 0 were waited for; matrix products, arithmetic and copies ran while one was open for 3% of the time, Pallas kernels for 22%

profile of v4, /device:TPU:1, one launch (start us, length us, event | category | flops | bytes accessed | tf_op | source)
XLA Modules:
  0.0 222.5 jit_solution(11141991399161101662)
XLA Ops:
  7.2 0.0 copy-start.4
  7.2 0.0 all-gather.2.cloned.1.call-start
  7.2 0.7 all-gather.2.cloned.1.call-update
  7.9 0.7 slice_bitcast_fusion
  8.7 0.4 copy.23
  9.1 2.1 copy.22.refs_9_
  11.2 0.4 copy.21
  11.6 0.0 copy-done.4
  11.6 0.6 fusion.1
  13.4 0.0 copy-start.5
  13.4 48.5 %halo_exchange_1.1 = (f32[4,64,384]{2,1,0:T(8,128)}, f32[4,64,384]{2,1,0:T(8,128)}, f32[32,8,384]{2,1,0:T(8,128)}, f32[32,8,384]{2,1,0:T(8,128)}, f32[4,64,384]{...) custom-call(f32[32,64,384]{2,1,0:T(8,128)} %bitcast.16, f32[32,64,384]{2,1,0:T(8,128)} %bitcast.21), custom_call_target="tpu_custom_call" | custom-call | tf_op jit(solution)/shard_map/halo_exchange_1/pallas_call | solution.py:103
  61.9 1.2 pad_add_fusion.refs_10_
  63.1 0.0 copy-done.5
  63.1 0.6 fusion
  63.7 0.0 all-gather.2.cloned.1.call-done.refs_8_
  63.7 16.2 %leap_wave1.1 = (f32[32,64,384]{2,1,0:T(8,128)}, f32[32,64,384]{2,1,0:T(8,128)}, f32[32,64,1]{2,1,0:T(8,128)}) custom-call(f32[32,64,384]{2,1,0:T(8,128)} %bitcast.17, f32[32,64,384]{2,1,0:T(8,128)} %bitcast.18, f32[32,64,384]{2,1,0:T(8,128)} %bitcast.19, f32[4,64,384]{2,1,0:T(8,128)} %get-tuple-element.29.refs_3_, f32[4,64,384]{2,1,0:T(8,128)} %get-tuple-element.30.refs_4_, ...), custom_call_target="tpu_custom_call" | custom-call | flops 47185920 | bytes 34603008 | tf_op jit(solution)/shard_map/leap_wave1/pallas_call | solution.py:252
  79.9 24.7 %halo_exchange_2.1 = (f32[4,64,384]{2,1,0:T(8,128)}, f32[4,64,384]{2,1,0:T(8,128)}, f32[32,8,384]{2,1,0:T(8,128)}, f32[32,8,384]{2,1,0:T(8,128)}) custom-call(f32[32,64,384]{2,1,0:T(8,128)} %get-tuple-element.33.refs_0_.refs_1_.refs_2_), custom_call_target="tpu_custom_call" | custom-call | tf_op jit(solution)/shard_map/halo_exchange_2/pallas_call | solution.py:103
  104.6 16.0 %leap_wave2.1 = (f32[32,64,384]{2,1,0:T(8,128)}, f32[32,64,1]{2,1,0:T(8,128)}) custom-call(f32[32,64,384]{2,1,0:T(8,128)} %get-tuple-element.33.refs_0_.refs_1_.refs_2_, f32[32,64,384]{2,1,0:T(8,128)} %get-tuple-element.33.refs_0_.refs_1_.refs_2_, f32[32,64,384]{2,1,0:T(8,128)} %get-tuple-element.33.refs_0_.refs_1_.refs_2_, ...), custom_call_target="tpu_custom_call" | custom-call | flops 47185920 | bytes 31457280 | tf_op jit(solution)/shard_map/leap_wave2/pallas_call | solution.py:252
  120.6 2.4 %sub.14.refs_10_ = f32[32,64,1]{2,1,0:T(8,128)} subtract(f32[32,64,1]{2,1,0:T(8,128)} %get-tuple-element.38, f32[32,64,1]{2,1,0:T(8,128)S(1)} %copy.21) | non-fusion elementwise | flops 2048 | bytes 24576 | tf_op jit(solution)/shard_map/sub | solution.py:373
  122.9 15.4 %leap_adj1.1 = (f32[32,64,384]{2,1,0:T(8,128)}, f32[32,64,384]{2,1,0:T(8,128)}) custom-call(f32[32,64,384]{2,1,0:T(8,128)} %bitcast.22, f32[32,64,384]{2,1,0:T(8,128)} %bitcast.23, f32[32,64,384]{2,1,0:T(8,128)} %bitcast.24, f32[4,64,384]{2,1,0:T(8,128)} %get-tuple-element.25.refs_3_, f32[4,64,384]{2,1,0:T(8,128)} %get-tuple-element.26.refs_4_, ...), custom_call_target="tpu_custom_call" | custom-call | flops 47185920 | bytes 31457280 | tf_op jit(solution)/shard_map/leap_adj1/pallas_call | solution.py:252
  138.3 0.0 copy-start.3
  138.3 24.7 %halo_exchange_3.1 = (f32[4,64,384]{2,1,0:T(8,128)}, f32[4,64,384]{2,1,0:T(8,128)}, f32[32,8,384]{2,1,0:T(8,128)}, f32[32,8,384]{2,1,0:T(8,128)}) custom-call(f32[32,64,384]{2,1,0:T(8,128)} %get-tuple-element.40.refs_0_.refs_1_.refs_2_), custom_call_target="tpu_custom_call" | custom-call | tf_op jit(solution)/shard_map/halo_exchange_3/pallas_call | solution.py:103
  163.0 0.0 copy-done.3
  163.1 1.1 sub.15.refs_10_
  164.2 0.0 copy-start
  164.2 0.0 copy-start.1
  164.2 0.0 copy-start.2
  164.2 15.7 %leap_adj2.1.img_ref = f32[32,64,384]{2,1,0:T(8,128)} custom-call(f32[32,64,384]{2,1,0:T(8,128)} %get-tuple-element.40.refs_0_.refs_1_.refs_2_, f32[32,64,384]{2,1,0:T(8,128)} %get-tuple-element.40.refs_0_.refs_1_.refs_2_, f32[32,64,384]{2,1,0:T(8,128)} %get-tuple-element.40.refs_0_.refs_1_.refs_2_, f32[4,64,384]{2,1,0:T(8,128)} %get-tuple-element.41.refs_3_, ...), custom_call_target="tpu_custom_call" | custom-call | flops 47185920 | bytes 31457280 | tf_op jit(solution)/shard_map/leap_adj2/pallas_call | solution.py:252
  179.9 0.0 copy-done
  179.9 0.0 copy-done.1
  179.9 0.0 copy-done.2
  179.9 34.0 %kick_reduce_scatter.1 = (f32[8,64,384]{2,1,0:T(8,128)S(1)}, f32[8,64,384]{2,1,0:T(8,128)S(1)}) custom-call(f32[32,64,384]{2,1,0:T(8,128)} %leap_adj2.1.img_ref, f32[8,64,384]{2,1,0:T(8,128)S(1)} %copy-done, f32[8,64,384]{2,1,0:T(8,128)S(1)} %copy-done.1, f32[8,64,384]{2,1,0:T(8,128)S(1)} %copy-done.2), custom_call_target="tpu_custom_call" | custom-call | tf_op jit(solution)/shard_map/kick_reduce_scatter/pallas_call | solution.py:324
  213.9 0.9 copy.27
  214.8 0.9 copy.28
Async XLA Ops:
  7.2 4.4 %copy-start.4 = (s32[1,3]{1,0:T(1,128)S(1)}, s32[1,3]{1,0:T(1,128)}, u32[]{:S(2)}) copy-start(s32[1,3]{1,0:T(1,128)} %param.20) | copy-start | bytes 40
  7.2 56.5 %all-gather.2.cloned.1.call-start = ((), (), s32[]{:S(2)}) async-start(), calls=%async_computation | async-start | bytes 3932160 | tf_op jit(solution)/shard_map/all_gather | solution.py:353
  13.4 49.7 %copy-start.5 = (f32[1,2]{1,0:T(1,128)S(1)}, f32[1,2]{1,0:T(1,128)}, u32[]{:S(2)}) copy-start(f32[1,2]{1,0:T(1,128)} %param.21) | copy-start | bytes 28
  138.3 24.8 %copy-start.3 = (f32[32,64,1]{2,1,0:T(8,128)S(1)}, f32[32,64,1]{2,1,0:T(8,128)}, u32[]{:S(2)}) copy-start(f32[32,64,1]{2,1,0:T(8,128)} %get-tuple-element.45) | copy-start | bytes 24580
  164.2 15.7 %copy-start = (f32[8,64,384]{2,1,0:T(8,128)S(1)}, f32[8,64,384]{2,1,0:T(8,128)}, u32[]{:S(2)}) copy-start(f32[8,64,384]{2,1,0:T(8,128)} %vel_ref.1) | copy-start | bytes 2359300
  164.2 15.7 %copy-start.1 = (f32[8,64,384]{2,1,0:T(8,128)S(1)}, f32[8,64,384]{2,1,0:T(8,128)}, u32[]{:S(2)}) copy-start(f32[8,64,384]{2,1,0:T(8,128)} %mom_ref.1) | copy-start | bytes 2359300
  164.2 15.7 %copy-start.2 = (f32[8,64,384]{2,1,0:T(8,128)S(1)}, f32[8,64,384]{2,1,0:T(8,128)}, u32[]{:S(2)}) copy-start(f32[8,64,384]{2,1,0:T(8,128)} %mass_ref.1) | copy-start | bytes 2359300
Sparse Core Ops, SparseCore 0:
  9.7 42.9 all-gather.1

commit v5 on v4

--- a/solution.py
+++ b/solution.py
@@ -33,13 +33,20 @@
         if d == 1:
             return f.at[pl.ds(0, 4)]
         if d == 2:
-            return f.at[:, pl.ds(cols - 8, 8)]
-        return f.at[:, pl.ds(0, 8)]
+            return f.at[:, pl.ds(cols - 4, 4)]
+        return f.at[:, pl.ds(0, 4)]
+
+    def target(j, b):
+        if b == 2:
+            return bufs[4 * j + b].at[:, pl.ds(4, 4)]
+        if b == 3:
+            return bufs[4 * j + b].at[:, pl.ds(0, 4)]
+        return bufs[4 * j + b]
 
     def remote(j, d, b):
         return pltpu.make_async_remote_copy(
             src_ref=source(fields[j], d),
-            dst_ref=bufs[4 * j + b],
+            dst_ref=target(j, b),
             send_sem=send_sem.at[j, d],
             recv_sem=recv_sem.at[j, b],
             device_id=peer[d],

time: 223 us -> 217 us (0.973)
  Pallas kernels: 195 us -> 189 us
    pallas_call x3, Pallas kernels: 97.9 us -> 89.5 us  [exchange(): pl.pallas_call(functools.partial(exchange_kernel, nf), in_specs=[any_spec...]
  transfers between devices with their start and end apart: 1 -> 1, of which waited for: 0 -> 0; matrix products, arithmetic and copies ran while one was open for 3% -> 3% of each run, Pallas kernels for 22% -> 20%
where the time goes in v5:
time: 217 us; the launch traced here: 216 us
  Pallas kernels  189 us (87%)
  between operations  15.4 us (7%)
  local copies, waits for them, and re-layouts  6.6 us (3%)
  other arithmetic  4.72 us (2%)
    pallas_call x3, Pallas kernels, exchange(): pl.pallas_call(functools.partial(exchange_kernel, nf), in_specs=[any_spec...  89.5 us
    pallas_call x4, Pallas kernels, leap(): pl.pallas_call(functools.partial(step_kernel, kind), grid=grid, in_specs=...  63.2 us
    pallas_call x1, Pallas kernels, kick(): pl.pallas_call(kick_kernel, in_specs=[pl.BlockSpec(memory_space=pl.ANY),...  36.1 us
  transfers between devices with their start and end apart: 1, of which 0 were waited for; matrix products, arithmetic and copies ran while one was open for 3% of the time, Pallas kernels for 20%

profile of v5, /device:TPU:1, one launch (start us, length us, event | category | flops | bytes accessed | tf_op | source)
XLA Modules:
  0.0 216.2 jit_solution(14620936770417628908)
XLA Ops:
  7.2 0.0 copy-start.4
  7.2 0.0 all-gather.2.cloned.1.call-start
  7.2 0.7 all-gather.2.cloned.1.call-update
  7.9 0.7 slice_bitcast_fusion
  8.7 0.4 copy.23
  9.1 2.1 copy.22.refs_9_
  11.2 0.4 copy.21
  11.6 0.0 copy-done.4
  11.6 0.6 fusion.1
  13.4 0.0 copy-start.5
  13.4 44.3 %halo_exchange_1.1 = (f32[4,64,384]{2,1,0:T(8,128)}, f32[4,64,384]{2,1,0:T(8,128)}, f32[32,8,384]{2,1,0:T(8,128)}, f32[32,8,384]{2,1,0:T(8,128)}, f32[4,64,384]{...) custom-call(f32[32,64,384]{2,1,0:T(8,128)} %bitcast.16, f32[32,64,384]{2,1,0:T(8,128)} %bitcast.21), custom_call_target="tpu_custom_call" | custom-call | tf_op jit(solution)/shard_map/halo_exchange_1/pallas_call | solution.py:110
  57.6 1.2 pad_add_fusion.refs_10_
  58.9 0.0 copy-done.5
  58.9 0.6 fusion
  59.5 0.0 all-gather.2.cloned.1.call-done.refs_8_
  59.5 16.2 %leap_wave1.1 = (f32[32,64,384]{2,1,0:T(8,128)}, f32[32,64,384]{2,1,0:T(8,128)}, f32[32,64,1]{2,1,0:T(8,128)}) custom-call(f32[32,64,384]{2,1,0:T(8,128)} %bitcast.17, f32[32,64,384]{2,1,0:T(8,128)} %bitcast.18, f32[32,64,384]{2,1,0:T(8,128)} %bitcast.19, f32[4,64,384]{2,1,0:T(8,128)} %get-tuple-element.29.refs_3_, f32[4,64,384]{2,1,0:T(8,128)} %get-tuple-element.30.refs_4_, ...), custom_call_target="tpu_custom_call" | custom-call | flops 47185920 | bytes 34603008 | tf_op jit(solution)/shard_map/leap_wave1/pallas_call | solution.py:259
  75.6 22.6 %halo_exchange_2.1 = (f32[4,64,384]{2,1,0:T(8,128)}, f32[4,64,384]{2,1,0:T(8,128)}, f32[32,8,384]{2,1,0:T(8,128)}, f32[32,8,384]{2,1,0:T(8,128)}) custom-call(f32[32,64,384]{2,1,0:T(8,128)} %get-tuple-element.33.refs_0_.refs_1_.refs_2_), custom_call_target="tpu_custom_call" | custom-call | tf_op jit(solution)/shard_map/halo_exchange_2/pallas_call | solution.py:110
  98.3 16.0 %leap_wave2.1 = (f32[32,64,384]{2,1,0:T(8,128)}, f32[32,64,1]{2,1,0:T(8,128)}) custom-call(f32[32,64,384]{2,1,0:T(8,128)} %get-tuple-element.33.refs_0_.refs_1_.refs_2_, f32[32,64,384]{2,1,0:T(8,128)} %get-tuple-element.33.refs_0_.refs_1_.refs_2_, f32[32,64,384]{2,1,0:T(8,128)} %get-tuple-element.33.refs_0_.refs_1_.refs_2_, ...), custom_call_target="tpu_custom_call" | custom-call | flops 47185920 | bytes 31457280 | tf_op jit(solution)/shard_map/leap_wave2/pallas_call | solution.py:259
  114.2 2.4 %sub.14.refs_10_ = f32[32,64,1]{2,1,0:T(8,128)} subtract(f32[32,64,1]{2,1,0:T(8,128)} %get-tuple-element.38, f32[32,64,1]{2,1,0:T(8,128)S(1)} %copy.21) | non-fusion elementwise | flops 2048 | bytes 24576 | tf_op jit(solution)/shard_map/sub | solution.py:380
  116.6 15.4 %leap_adj1.1 = (f32[32,64,384]{2,1,0:T(8,128)}, f32[32,64,384]{2,1,0:T(8,128)}) custom-call(f32[32,64,384]{2,1,0:T(8,128)} %bitcast.22, f32[32,64,384]{2,1,0:T(8,128)} %bitcast.23, f32[32,64,384]{2,1,0:T(8,128)} %bitcast.24, f32[4,64,384]{2,1,0:T(8,128)} %get-tuple-element.25.refs_3_, f32[4,64,384]{2,1,0:T(8,128)} %get-tuple-element.26.refs_4_, ...), custom_call_target="tpu_custom_call" | custom-call | flops 47185920 | bytes 31457280 | tf_op jit(solution)/shard_map/leap_adj1/pallas_call | solution.py:259
  132.0 0.0 copy-start.3
  132.0 22.6 %halo_exchange_3.1 = (f32[4,64,384]{2,1,0:T(8,128)}, f32[4,64,384]{2,1,0:T(8,128)}, f32[32,8,384]{2,1,0:T(8,128)}, f32[32,8,384]{2,1,0:T(8,128)}) custom-call(f32[32,64,384]{2,1,0:T(8,128)} %get-tuple-element.40.refs_0_.refs_1_.refs_2_), custom_call_target="tpu_custom_call" | custom-call | tf_op jit(solution)/shard_map/halo_exchange_3/pallas_call | solution.py:110
  154.6 0.0 copy-done.3
  154.6 1.1 sub.15.refs_10_
  155.7 0.0 copy-start
  155.8 0.0 copy-start.1
  155.8 0.0 copy-start.2
  155.8 15.7 %leap_adj2.1.img_ref = f32[32,64,384]{2,1,0:T(8,128)} custom-call(f32[32,64,384]{2,1,0:T(8,128)} %get-tuple-element.40.refs_0_.refs_1_.refs_2_, f32[32,64,384]{2,1,0:T(8,128)} %get-tuple-element.40.refs_0_.refs_1_.refs_2_, f32[32,64,384]{2,1,0:T(8,128)} %get-tuple-element.40.refs_0_.refs_1_.refs_2_, f32[4,64,384]{2,1,0:T(8,128)} %get-tuple-element.41.refs_3_, ...), custom_call_target="tpu_custom_call" | custom-call | flops 47185920 | bytes 31457280 | tf_op jit(solution)/shard_map/leap_adj2/pallas_call | solution.py:259
  171.4 0.0 copy-done
  171.4 0.0 copy-done.1
  171.5 0.0 copy-done.2
  171.5 36.1 %kick_reduce_scatter.1 = (f32[8,64,384]{2,1,0:T(8,128)S(1)}, f32[8,64,384]{2,1,0:T(8,128)S(1)}) custom-call(f32[32,64,384]{2,1,0:T(8,128)} %leap_adj2.1.img_ref, f32[8,64,384]{2,1,0:T(8,128)S(1)} %copy-done, f32[8,64,384]{2,1,0:T(8,128)S(1)} %copy-done.1, f32[8,64,384]{2,1,0:T(8,128)S(1)} %copy-done.2), custom_call_target="tpu_custom_call" | custom-call | tf_op jit(solution)/shard_map/kick_reduce_scatter/pallas_call | solution.py:331
  207.6 0.9 copy.27
  208.5 0.9 copy.28
Async XLA Ops:
  7.2 4.4 %copy-start.4 = (s32[1,3]{1,0:T(1,128)S(1)}, s32[1,3]{1,0:T(1,128)}, u32[]{:S(2)}) copy-start(s32[1,3]{1,0:T(1,128)} %param.20) | copy-start | bytes 40
  7.2 52.3 %all-gather.2.cloned.1.call-start = ((), (), s32[]{:S(2)}) async-start(), calls=%async_computation | async-start | bytes 3932160 | tf_op jit(solution)/shard_map/all_gather | solution.py:360
  13.4 45.5 %copy-start.5 = (f32[1,2]{1,0:T(1,128)S(1)}, f32[1,2]{1,0:T(1,128)}, u32[]{:S(2)}) copy-start(f32[1,2]{1,0:T(1,128)} %param.21) | copy-start | bytes 28
  132.0 22.7 %copy-start.3 = (f32[32,64,1]{2,1,0:T(8,128)S(1)}, f32[32,64,1]{2,1,0:T(8,128)}, u32[]{:S(2)}) copy-start(f32[32,64,1]{2,1,0:T(8,128)} %get-tuple-element.45) | copy-start | bytes 24580
  155.7 15.7 %copy-start = (f32[8,64,384]{2,1,0:T(8,128)S(1)}, f32[8,64,384]{2,1,0:T(8,128)}, u32[]{:S(2)}) copy-start(f32[8,64,384]{2,1,0:T(8,128)} %vel_ref.1) | copy-start | bytes 2359300
  155.8 15.7 %copy-start.1 = (f32[8,64,384]{2,1,0:T(8,128)S(1)}, f32[8,64,384]{2,1,0:T(8,128)}, u32[]{:S(2)}) copy-start(f32[8,64,384]{2,1,0:T(8,128)} %mom_ref.1) | copy-start | bytes 2359300
  155.8 15.7 %copy-start.2 = (f32[8,64,384]{2,1,0:T(8,128)S(1)}, f32[8,64,384]{2,1,0:T(8,128)}, u32[]{:S(2)}) copy-start(f32[8,64,384]{2,1,0:T(8,128)} %mass_ref.1) | copy-start | bytes 2359300
Sparse Core Ops, SparseCore 0:
  9.7 42.9 all-gather.1

commit v6 on v2

v6 whole, which is shorter than its diff:
```python
import functools

import jax
import jax.numpy as jnp
from jax import lax
from jax.experimental import pallas as pl
from jax.experimental.pallas import tpu as pltpu
from jax.sharding import PartitionSpec as P

STENCIL = (-205.0 / 72.0, 8.0 / 5.0, -1.0 / 5.0, 8.0 / 315.0, -1.0 / 560.0)
squared_courant = 0.012
leap_step = 0.2

ROWS_PER_STEP = 8
Y_CHUNK = 8


class Exchange:
    def __init__(self, fields, bufs, zero_x, zero_y, send_sem, recv_sem, zero_sem):
        self.fields, self.bufs = fields, bufs
        self.zero_x, self.zero_y = zero_x, zero_y
        self.send_sem, self.recv_sem, self.zero_sem = send_sem, recv_sem, zero_sem
        row, nrow = lax.axis_index("row"), lax.axis_size("row")
        col, ncol = lax.axis_index("col"), lax.axis_size("col")
        self.row, self.nrow, self.col, self.ncol = row, nrow, col, ncol
        self.has = (row < nrow - 1, row > 0, col < ncol - 1, col > 0)
        self.peer = ({"row": row + 1}, {"row": row - 1}, {"col": col + 1}, {"col": col - 1})
        self.filler = (1, 0, 3, 2)

    def source(self, f, d):
        rows, cols, _ = f.shape
        if d == 0:
            return f.at[pl.ds(rows - 4, 4)]
        if d == 1:
            return f.at[pl.ds(0, 4)]
        if d == 2:
            return f.at[:, pl.ds(cols - 4, 4)]
        return f.at[:, pl.ds(0, 4)]

    def target(self, j, b):
        if b == 2:
            return self.bufs[4 * j + b].at[:, pl.ds(4, 4)]
        if b == 3:
            return self.bufs[4 * j + b].at[:, pl.ds(0, 4)]
        return self.bufs[4 * j + b]

    def remote(self, j, d):
        return pltpu.make_async_remote_copy(
            src_ref=self.source(self.fields[j], d),
            dst_ref=self.target(j, d),
            send_sem=self.send_sem.at[j, d],
            recv_sem=self.recv_sem.at[j, d],
            device_id=self.peer[d],
            device_id_type=pl.DeviceIdType.MESH,
        )

    def start(self):
        has, row, nrow, col, ncol = self.has, self.row, self.nrow, self.col, self.ncol
        barrier = pltpu.get_barrier_semaphore()
        for d in range(4):
            @pl.when(has[d])
            def _():
                pl.semaphore_signal(barrier, inc=1, device_id=self.peer[d], device_id_type=pl.DeviceIdType.MESH)

        count = (1 - row // (nrow - 1)) + (row + nrow - 1) // nrow + (1 - col // (ncol - 1)) + (col + ncol - 1) // ncol
        pl.semaphore_wait(barrier, count)

        for j in range(len(self.fields)):
            for d in range(4):
                @pl.when(has[d])
                def _():
                    self.remote(j, d).start()

        @pl.when(jnp.logical_not(has[0] & has[1]))
        def _():
            self.zero_x[...] = jnp.zeros_like(self.zero_x)

        @pl.when(jnp.logical_not(has[2] & has[3]))
        def _():
            self.zero_y[...] = jnp.zeros_like(self.zero_y)

        for j in range(len(self.fields)):
            for b in range(4):
                @pl.when(jnp.logical_not(has[self.filler[b]]))
                def _():
                    zero = self.zero_x if b < 2 else self.zero_y
                    copy = pltpu.make_async_copy(zero, self.bufs[4 * j + b], self.zero_sem.at[j, b])
                    copy.start()
                    copy.wait()

    def finish(self):
        has = self.has
        for j in range(len(self.fields)):
            for d in range(4):
                @pl.when(has[d])
                def _():
                    self.remote(j, d).wait_send()
            for b in range(4):
                @pl.when(has[self.filler[b]])
                def _():
                    self.remote(j, b).wait_recv()


def exchange_io(nf, rows, cols, depth):
    shapes = []
    for _ in range(nf):
        shapes += [
            jax.ShapeDtypeStruct((4, cols, depth), jnp.float32),
            jax.ShapeDtypeStruct((4, cols, depth), jnp.float32),
            jax.ShapeDtypeStruct((rows, 8, depth), jnp.float32),
            jax.ShapeDtypeStruct((rows, 8, depth), jnp.float32),
        ]
    scratch = [
        pltpu.VMEM((4, cols, depth), jnp.float32),
        pltpu.VMEM((rows, 8, depth), jnp.float32),
        pltpu.SemaphoreType.DMA((nf, 4)),
        pltpu.SemaphoreType.DMA((nf, 4)),
        pltpu.SemaphoreType.DMA((nf, 4)),
    ]
    return shapes, scratch


def exchange_kernel(nf, *refs):
    ex = Exchange(refs[:nf], refs[nf : 5 * nf], *refs[5 * nf :])
    ex.start()
    ex.finish()


def exchange(fields, collective_id):
    nf = len(fields)
    rows, cols, depth = fields[0].shape
    any_spec = pl.BlockSpec(memory_space=pl.ANY)
    shapes, scratch = exchange_io(nf, rows, cols, depth)
    outs = pl.pallas_call(
        functools.partial(exchange_kernel, nf),
        in_specs=[any_spec] * nf,
        out_specs=[any_spec] * (4 * nf),
        out_shape=shapes,
        scratch_shapes=scratch,
        compiler_params=pltpu.CompilerParams(collective_id=collective_id, has_side_effects=True),
        name=f"halo_exchange_{collective_id}",
    )(*fields)
    return [outs[4 * j : 4 * j + 4] for j in range(nf)]


def step_kernel(kind, names, nf_ex, *refs):
    ref = dict(zip(names, refs))
    if nf_ex:
        ex = Exchange(
            [ref[f"ex_f{j}"] for j in range(nf_ex)],
            [ref[f"ex_b{k}"] for k in range(4 * nf_ex)],
            *[ref[k] for k in ("ex_zx", "ex_zy", "ex_ss", "ex_rs", "ex_zs")],
        )
    f_ref, pad = ref["f"], ref["pad"]
    tb, cols, depth = f_ref.shape
    i = pl.program_id(0)
    n = pl.num_programs(0)

    if nf_ex:
        @pl.when(i == 0)
        def _():
            ex.start()

    lo = jnp.where(i == 0, ref["xlo"][...], ref["flo"][...])
    hi = jnp.where(i == n - 1, ref["xhi"][...], ref["fhi"][...])
    pad[0:4, 8 : 8 + cols, :] = lo
    pad[4 : 4 + tb, 8 : 8 + cols, :] = f_ref[...]
    pad[4 + tb : 8 + tb, 8 : 8 + cols, :] = hi
    pad[4 : 4 + tb, 0:8, :] = ref["ylo"][...]
    pad[4 : 4 + tb, 8 + cols : 16 + cols, :] = ref["yhi"][...]

    z_index = lax.broadcasted_iota(jnp.int32, (Y_CHUNK, depth), 1)
    y_index = lax.broadcasted_iota(jnp.int32, (Y_CHUNK, depth), 0)
    wave = kind in ("wave1", "wave2")
    if wave:
        src_ref = ref["src"]
        src_x = src_ref[0] - i * tb
        src_y = src_ref[1]
        src_z = src_ref[2]
        amp = ref["amp"][0]

    def row(r, carry):
        for y0 in range(0, cols, Y_CHUNK):
            ys = pl.ds(y0, Y_CHUNK)
            pys = pl.ds(8 + y0, Y_CHUNK)
            c = pad[4 + r, pys, :]
            result = (3.0 * STENCIL[0]) * c
            for k in range(1, 5):
                along = pad[4 + r + k, pys, :] + pad[4 + r - k, pys, :]
                along = along + (
                    pad[4 + r, pl.ds(8 + y0 + k, Y_CHUNK), :]
                    + pad[4 + r, pl.ds(8 + y0 - k, Y_CHUNK), :]
                )
                zp = jnp.where(z_index < depth - k, pltpu.roll(c, depth - k, 1), 0.0)
                zm = jnp.where(z_index >= k, pltpu.roll(c, k, 1), 0.0)
                along = along + (zp + zm)
                result = result + STENCIL[k] * along
            v = ref["vel"][r, ys, :]
            stiff = squared_courant * v * v
            prev = ref["prev"][r, ys, :]
            out = 2.0 * c - prev + stiff * result
            if wave:
                at_rec = z_index == ref["rec"][r, ys, :]
                hit = (r == src_x) & (y_index + y0 == src_y) & (z_index == src_z)
                out = out + jnp.where(hit, amp, 0.0)
                sel = jnp.where(at_rec, out, 0.0)
                folded = sel[:, 0:128]
                for t in range(128, depth, 128):
                    folded = folded + sel[:, t : t + 128]
                ref["fold"][pl.ds(pl.multiple_of(r * cols + y0, Y_CHUNK), Y_CHUNK), :] = folded
                ref["o_dw"][r, ys, :] = (out - 2.0 * c) + prev
                if kind == "wave1":
                    ref["o_f"][r, ys, :] = out
            elif kind == "adjbulk":
                ref["o_f"][r, ys, :] = out
            else:
                at_rec = z_index == ref["rec"][r, ys, :]
                out = out + jnp.where(at_rec, ref["mis"][r, ys, :], 0.0)
                ref["o_img"][r, ys, :] = ref["part"][r, ys, :] + out * ref["dw"][r, ys, :]
        return carry

    lax.fori_loop(0, tb, row, 0)
    if wave:
        ref["o_pick"][...] = jnp.sum(ref["fold"][...], axis=1, keepdims=True).reshape(ref["o_pick"].shape)
    if kind == "wave2":
        def inject(r, carry):
            for y0 in range(0, cols, Y_CHUNK):
                ys = pl.ds(y0, Y_CHUNK)
                at_rec = z_index == ref["rec"][r, ys, :]
                misfit = ref["o_pick"][r, ys, :] - ref["obs"][r, ys, :]
                a2 = ref["a2raw"][r, ys, :] + jnp.where(at_rec, misfit, 0.0)
                ref["o_a2"][r, ys, :] = a2
                ref["o_part"][r, ys, :] = a2 * ref["o_dw"][r, ys, :]
            return carry

        lax.fori_loop(0, tb, inject, 0)

    if nf_ex:
        @pl.when(i == n - 1)
        def _():
            ex.finish()


def leap(kind, f, xlo, xhi, ylo, yhi, prev, vel, extra, exchanged=(), collective_id=None):
    rows, cols, depth = f.shape
    tb = ROWS_PER_STEP
    grid = (rows // tb,)
    nq = rows // 4
    block = pl.BlockSpec((tb, cols, depth), lambda i: (i, 0, 0))
    lo_spec = pl.BlockSpec((4, cols, depth), lambda i: (jnp.maximum(2 * i - 1, 0), 0, 0))
    hi_spec = pl.BlockSpec((4, cols, depth), lambda i: (jnp.minimum(2 * i + 2, nq - 1), 0, 0))
    whole4 = pl.BlockSpec((4, cols, depth), lambda i: (0, 0, 0))
    yspec = pl.BlockSpec((tb, 8, depth), lambda i: (i, 0, 0))
    col1 = pl.BlockSpec((tb, cols, 1), lambda i: (i, 0, 0))
    smem = pl.BlockSpec(memory_space=pltpu.SMEM)
    any_spec = pl.BlockSpec(memory_space=pl.ANY)
    field = jax.ShapeDtypeStruct((rows, cols, depth), jnp.float32)
    picked = jax.ShapeDtypeStruct((rows, cols, 1), jnp.float32)
    spec_of = {"src": smem, "amp": smem, "rec": col1, "mis": col1, "obs": col1}

    names = ["f", "flo", "fhi", "xlo", "xhi", "ylo", "yhi", "prev", "vel"]
    in_specs = [block, lo_spec, hi_spec, whole4, whole4, yspec, yspec, block, block]
    args = [f, f, f, xlo, xhi, ylo, yhi, prev, vel]
    for key, value in extra.items():
        names.append(key)
        in_specs.append(spec_of.get(key, block))
        args.append(value)
    nf_ex = len(exchanged)
    for j, g in enumerate(exchanged):
        names.append(f"ex_f{j}")
        in_specs.append(any_spec)
        args.append(g)

    outs = {
        "wave1": [("o_f", field, block), ("o_dw", field, block), ("o_pick", picked, col1)],
        "wave2": [("o_dw", field, block), ("o_pick", picked, col1), ("o_a2", field, block), ("o_part", field, block)],
        "adjbulk": [("o_f", field, block)],
        "adj2": [("o_img", field, block)],
    }[kind]
    names += [o[0] for o in outs]
    out_shape = [o[1] for o in outs]
    out_specs = [o[2] for o in outs]
    scratch = [pltpu.VMEM((tb + 8, cols + 16, depth), jnp.float32)]
    names.append("pad")
    if kind in ("wave1", "wave2"):
        scratch.append(pltpu.VMEM((tb * cols, 128), jnp.float32))
        names.append("fold")
    if nf_ex:
        ex_shapes, ex_scratch = exchange_io(nf_ex, rows, cols, depth)
        k = len(outs)
        names = names[: len(names) - len(scratch)]
        names += [f"ex_b{m}" for m in range(4 * nf_ex)]
        names += ["pad", "fold"][: len(scratch)]
        names += ["ex_zx", "ex_zy", "ex_ss", "ex_rs", "ex_zs"]
        out_shape += ex_shapes
        out_specs += [any_spec] * len(ex_shapes)
        scratch += ex_scratch
        params = pltpu.CompilerParams(
            collective_id=collective_id, has_side_effects=True, vmem_limit_bytes=60 * 1024 * 1024
        )
    else:
        params = pltpu.CompilerParams(vmem_limit_bytes=60 * 1024 * 1024)
    n_big = sum(1 for sp in in_specs if sp is block) + 1 + sum(1 for sp in out_specs if sp is block)
    cost = pl.CostEstimate(
        flops=60 * rows * cols * depth,
        transcendentals=0,
        bytes_accessed=4 * rows * cols * depth * n_big,
    )
    result = pl.pallas_call(
        functools.partial(step_kernel, kind, tuple(names), nf_ex),
        grid=grid,
        in_specs=in_specs,
        out_specs=out_specs,
        out_shape=out_shape,
        scratch_shapes=scratch,
        compiler_params=params,
        cost_estimate=cost,
        name=f"leap_{kind}",
    )(*args)
    if nf_ex:
        own = result[: len(outs)]
        ex = result[len(outs) :]
        return own, [ex[4 * j : 4 * j + 4] for j in range(nf_ex)]
    return result


def kick_kernel(img_ref, vel_ref, mom_ref, mass_ref, v_out, p_out, recv, send_sem, recv_sem, own_sem):
    me = lax.axis_index("shot")
    n = lax.axis_size("shot")
    rows = vel_ref.shape[0]
    mesh = pl.DeviceIdType.MESH

    barrier = pltpu.get_barrier_semaphore()
    for d in range(1, n):
        pl.semaphore_signal(barrier, inc=1, device_id={"shot": lax.rem(me + d, n)}, device_id_type=mesh)
    pl.semaphore_wait(barrier, n - 1)

    sends = []
    for d in (1, n - 1) + tuple(range(2, n - 1)):
        peer = lax.rem(me + d, n)
        copy = pltpu.make_async_remote_copy(
            src_ref=img_ref.at[pl.ds(pl.multiple_of(peer * rows, rows), rows)],
            dst_ref=recv.at[me],
            send_sem=send_sem.at[d],
            recv_sem=recv_sem.at[me],
            device_id={"shot": peer},
            device_id_type=mesh,
        )
        copy.start()
        sends.append(copy)
    own = pltpu.make_async_copy(img_ref.at[pl.ds(pl.multiple_of(me * rows, rows), rows)], recv.at[me], own_sem)
    own.start()
    for copy in sends:
        copy.wait_send()
    own.wait()
    for d in range(1, n):
        src = lax.rem(me + d, n)
        pltpu.make_async_remote_copy(
            src_ref=img_ref.at[pl.ds(0, rows)],
            dst_ref=recv.at[src],
            send_sem=send_sem.at[d],
            recv_sem=recv_sem.at[src],
            device_id={"shot": src},
            device_id_type=mesh,
        ).wait_recv()

    def row(r, carry):
        summed = recv[0, r]
        for s in range(1, n):
            summed = summed + recv[s, r]
        v = vel_ref[r]
        gradient = 2.0 / v * summed
        p_half = mom_ref[r] - 0.5 * leap_step * gradient
        p_out[r] = p_half
        v_out[r] = v + leap_step * p_half / mass_ref[r]
        return carry

    lax.fori_loop(0, rows, row, 0)


def kick(imaging, velocity, momentum, mass_diag):
    n = lax.axis_size("shot")
    vmem = pl.BlockSpec(memory_space=pltpu.VMEM)
    slab = jax.ShapeDtypeStruct(velocity.shape, jnp.float32)
    return pl.pallas_call(
        kick_kernel,
        in_specs=[pl.BlockSpec(memory_space=pl.ANY), vmem, vmem, vmem],
        out_specs=[vmem, vmem],
        out_shape=[slab, slab],
        scratch_shapes=[
            pltpu.VMEM((n,) + velocity.shape, jnp.float32),
            pltpu.SemaphoreType.DMA((n,)),
            pltpu.SemaphoreType.DMA((n,)),
            pltpu.SemaphoreType.DMA(()),
        ],
        compiler_params=pltpu.CompilerParams(collective_id=0, has_side_effects=True, vmem_limit_bytes=48 * 1024 * 1024),
        name="kick_reduce_scatter",
    )(imaging, velocity, momentum, mass_diag)


def on_device(
    velocity,
    momentum,
    mass_diag,
    u_prev,
    u_cur,
    adj_next,
    adj_cur,
    observed,
    rec_depth,
    src_cell,
    wavelet,
):
    full_velocity = lax.all_gather(velocity, "shot", axis=0, tiled=True)
    row_count, col_count, depth_cells = full_velocity.shape
    oldest = u_prev[0]
    present = u_cur[0]
    adj_later = adj_next[0]
    adj_now = adj_cur[0]
    rec = rec_depth[0][:, :, None]
    cell = src_cell[0]
    src = jnp.stack(
        [
            cell[0] - lax.axis_index("row") * row_count,
            cell[1] - lax.axis_index("col") * col_count,
            cell[2],
        ]
    ).astype(jnp.int32)
    amp = wavelet[0]

    wave_h, adj_h = exchange([present, adj_now], 1)
    advanced, dw1, pick_adv = leap(
        "wave1", present, *wave_h, oldest, full_velocity, {"rec": rec, "src": src, "amp": amp[0:1]}
    )
    (adj_bulk,), (adv_h,) = leap(
        "adjbulk", adj_now, *adj_h, adj_later, full_velocity, {}, exchanged=[advanced], collective_id=2
    )
    dw2, pick_far, adj_two, part = leap(
        "wave2",
        advanced,
        *adv_h,
        present,
        full_velocity,
        {"rec": rec, "src": src, "amp": amp[1:2], "a2raw": adj_bulk, "obs": observed[0, 1][:, :, None]},
    )
    misfit_early = pick_adv - observed[0, 0][:, :, None]
    (imaging,) = leap(
        "adj2",
        adj_two,
        *exchange([adj_two], 3)[0],
        adj_now,
        full_velocity,
        {"rec": rec, "mis": misfit_early, "dw": dw1, "part": part},
    )
    v_new, p_half = kick(imaging, velocity, momentum, mass_diag)
    return (v_new, p_half)


def solution(mesh):
    return jax.shard_map(
        on_device,
        mesh=mesh,
        in_specs=(
            P(("row", "shot"), "col", None),
            P(("row", "shot"), "col", None),
            P(("row", "shot"), "col", None),
            P("shot", "row", "col", None),
            P("shot", "row", "col", None),
            P("shot", "row", "col", None),
            P("shot", "row", "col", None),
            P("shot", None, "row", "col"),
            P("shot", "row", "col"),
            P("shot", None),
            P("shot", None),
        ),
        out_specs=(P(("row", "shot"), "col", None), P(("row", "shot"), "col", None)),
        check_vma=False,
    )
```

time: 262 us -> 208 us (0.79)
  Pallas kernels: 123 us -> 181 us
  starting transfers between devices: 54.7 us -> 0.04 us
  waiting for transfers between devices: 31.8 us -> 0.68 us
  local copies, waits for them, and re-layouts: 31.2 us -> 7.73 us
    pallas_call x4 -> x6, Pallas kernels: 89 us -> 145 us  [the longest x4 78.2 us: leap(): pl.pallas_call(functools.partial(step_kernel, kind, tuple(names), nf_ex),...]
    ppermute x16 -> x0, starting transfers between devices: 54.6 us -> none  [the longest x8 39.7 us: halos(): lax.ppermute(lax.slice_in_dim(block, size - 4, None, axis=dim), axis, for...]
    ppermute x16 -> x0, waiting for transfers between devices: 17.4 us -> none  [the longest x8 15.6 us: halos(): lax.ppermute(lax.slice_in_dim(block, size - 4, None, axis=dim), axis, for...]
    all_gather x1, waiting for transfers between devices: 13.8 us -> 0.01 us  [on_device(): full_velocity = lax.all_gather(velocity, 'shot', axis=0, tiled=True)]
    pad x8 -> x0, local copies, waits for them, and re-layouts: 11.9 us -> none  [the longest x4 5.96 us: halos(): ylo = jnp.pad(ylo, ((0, 0), (4, 0), (0, 0)))]
    slice x8 -> x0, local copies, waits for them, and re-layouts: 11.7 us -> none  [halos(): high = lax.ppermute(lax.slice_in_dim(block, 0, 4, axis=dim), axis, backward)]
  transfers between devices with their start and end apart: 17 -> 1, of which waited for: 3 -> 0; matrix products, arithmetic and copies ran while one was open for 11% -> 3% of each run, Pallas kernels for 22% -> 21%
where the time goes in v6:
time: 208 us
  Pallas kernels  181 us (87%)
  between operations  15.5 us (7%)
  local copies, waits for them, and re-layouts  7.73 us (4%)
  other arithmetic  2.35 us (1%)
    pallas_call x4, Pallas kernels, leap(): pl.pallas_call(functools.partial(step_kernel, kind, tuple(names), nf_ex),...  78.2 us
    pallas_call x2, Pallas kernels, exchange(): pl.pallas_call(functools.partial(exchange_kernel, nf), in_specs=[any_spec...  66.9 us
    pallas_call x1, Pallas kernels, kick(): pl.pallas_call(kick_kernel, in_specs=[pl.BlockSpec(memory_space=pl.ANY),...  36.1 us
  transfers between devices with their start and end apart: 1, of which 0 were waited for; matrix products, arithmetic and copies ran while one was open for 3% of the time, Pallas kernels for 21%

profile of v6, /device:TPU:1, one launch (start us, length us, event | category | flops | bytes accessed | tf_op | source)
XLA Modules:
  0.0 207.5 jit_solution(16923508592119488609)
XLA Ops:
  7.2 0.0 copy-start.4
  7.2 0.0 all-gather.2.cloned.1.call-start
  7.2 0.7 all-gather.2.cloned.1.call-update
  7.9 0.7 slice_bitcast_fusion
  8.7 0.4 copy.21
  9.1 2.1 %copy.18.refs_9_ = s32[32,64,1]{2,1,0:T(8,128)} copy(s32[32,64,1]{1,0,2:T(8,128)} %bitcast.28) | data formatting | bytes 16384 | tf_op jit(solution)/shard_map/broadcast_in_dim;squeeze | solution.py:420
  11.2 1.4 copy.20.refs_13_
  12.6 0.0 copy-done.4
  12.6 0.7 fusion.1
  14.6 0.0 copy-start.5
  14.6 44.3 %halo_exchange_1.1 = (f32[4,64,384]{2,1,0:T(8,128)}, f32[4,64,384]{2,1,0:T(8,128)}, f32[32,8,384]{2,1,0:T(8,128)}, f32[32,8,384]{2,1,0:T(8,128)}, f32[4,64,384]{...) custom-call(f32[32,64,384]{2,1,0:T(8,128)} %bitcast.21, f32[32,64,384]{2,1,0:T(8,128)} %bitcast.16), custom_call_target="tpu_custom_call" | custom-call | tf_op jit(solution)/shard_map/halo_exchange_1/pallas_call | solution.py:134
  58.9 1.2 pad_add_fusion.refs_10_
  60.1 0.0 copy-done.5
  60.1 0.6 fusion
  60.7 0.0 all-gather.2.cloned.1.call-done.refs_8_
  60.7 16.2 %leap_wave1.1 = (f32[32,64,384]{2,1,0:T(8,128)}, f32[32,64,384]{2,1,0:T(8,128)}, f32[32,64,1]{2,1,0:T(8,128)}) custom-call(f32[32,64,384]{2,1,0:T(8,128)} %bitcast.22, f32[32,64,384]{2,1,0:T(8,128)} %bitcast.23, f32[32,64,384]{2,1,0:T(8,128)} %bitcast.24, f32[4,64,384]{2,1,0:T(8,128)} %get-tuple-element.24.refs_3_, f32[4,64,384]{2,1,0:T(8,128)} %get-tuple-element.25.refs_4_, ...), custom_call_target="tpu_custom_call" | custom-call | flops 47185920 | bytes 18874368 | tf_op jit(solution)/shard_map/leap_wave1/pallas_call | solution.py:309
  76.9 26.3 %leap_adjbulk.1 = (f32[32,64,384]{2,1,0:T(8,128)}, f32[4,64,384]{2,1,0:T(8,128)}, f32[4,64,384]{2,1,0:T(8,128)}, f32[32,8,384]{2,1,0:T(8,128)}, f32[32,8,384]{2,1,0:T(8,128)}) custom-call(f32[32,64,384]{2,1,0:T(8,128)} %bitcast.17, f32[32,64,384]{2,1,0:T(8,128)} %bitcast.18, f32[32,64,384]{2,1,0:T(8,128)} %bitcast.19, ...), custom_call_target="tpu_custom_call" | custom-call | flops 47185920 | bytes 15728640 | tf_op jit(solution)/shard_map/leap_adjbulk/pallas_call | solution.py:309
  103.2 20.0 %leap_wave2.1 = (f32[32,64,384]{2,1,0:T(8,128)}, f32[32,64,1]{2,1,0:T(8,128)}, f32[32,64,384]{2,1,0:T(8,128)}, f32[32,64,384]{2,1,0:T(8,128)}) custom-call(f32[32,64,384]{2,1,0:T(8,128)} %get-tuple-element.28.refs_9_.refs_0_.refs_1_.refs_2_, f32[32,64,384]{2,1,0:T(8,128)} %get-tuple-element.28.refs_9_.refs_0_.refs_1_.refs_2_, ...), custom_call_target="tpu_custom_call" | custom-call | flops 47185920 | bytes 25165824 | tf_op jit(solution)/shard_map/leap_wave2/pallas_call | solution.py:309
  123.3 0.0 copy-start.3
  123.3 22.6 %halo_exchange_3.1 = (f32[4,64,384]{2,1,0:T(8,128)}, f32[4,64,384]{2,1,0:T(8,128)}, f32[32,8,384]{2,1,0:T(8,128)}, f32[32,8,384]{2,1,0:T(8,128)}) custom-call(f32[32,64,384]{2,1,0:T(8,128)} %get-tuple-element.38.refs_0_.refs_1_.refs_2_), custom_call_target="tpu_custom_call" | custom-call | tf_op jit(solution)/shard_map/halo_exchange_3/pallas_call | solution.py:134
  145.9 0.0 copy-done.3
  145.9 1.1 sub.11.refs_10_
  147.0 0.0 copy-start
  147.0 0.0 copy-start.1
  147.0 0.0 copy-start.2
  147.0 15.7 %leap_adj2.1.img_ref = f32[32,64,384]{2,1,0:T(8,128)} custom-call(f32[32,64,384]{2,1,0:T(8,128)} %get-tuple-element.38.refs_0_.refs_1_.refs_2_, f32[32,64,384]{2,1,0:T(8,128)} %get-tuple-element.38.refs_0_.refs_1_.refs_2_, f32[32,64,384]{2,1,0:T(8,128)} %get-tuple-element.38.refs_0_.refs_1_.refs_2_, f32[4,64,384]{2,1,0:T(8,128)} %get-tuple-element.39.refs_3_, ...), custom_call_target="tpu_custom_call" | custom-call | flops 47185920 | bytes 22020096 | tf_op jit(solution)/shard_map/leap_adj2/pallas_call | solution.py:309
  162.8 0.0 copy-done
  162.8 0.0 copy-done.1
  162.8 0.0 copy-done.2
  162.8 36.1 %kick_reduce_scatter.1 = (f32[8,64,384]{2,1,0:T(8,128)S(1)}, f32[8,64,384]{2,1,0:T(8,128)S(1)}) custom-call(f32[32,64,384]{2,1,0:T(8,128)} %leap_adj2.1.img_ref, f32[8,64,384]{2,1,0:T(8,128)S(1)} %copy-done, f32[8,64,384]{2,1,0:T(8,128)S(1)} %copy-done.1, f32[8,64,384]{2,1,0:T(8,128)S(1)} %copy-done.2), custom_call_target="tpu_custom_call" | custom-call | tf_op jit(solution)/shard_map/kick_reduce_scatter/pallas_call | solution.py:385
  198.9 0.9 copy.25
  199.8 0.9 copy.26
Async XLA Ops:
  7.2 5.5 %copy-start.4 = (s32[1,3]{1,0:T(1,128)S(1)}, s32[1,3]{1,0:T(1,128)}, u32[]{:S(2)}) copy-start(s32[1,3]{1,0:T(1,128)} %param.20) | copy-start | bytes 40
  7.2 53.5 %all-gather.2.cloned.1.call-start = ((), (), s32[]{:S(2)}) async-start(), calls=%async_computation | async-start | bytes 3932160 | tf_op jit(solution)/shard_map/all_gather | solution.py:414
  14.6 45.5 %copy-start.5 = (f32[1,2]{1,0:T(1,128)S(1)}, f32[1,2]{1,0:T(1,128)}, u32[]{:S(2)}) copy-start(f32[1,2]{1,0:T(1,128)} %param.21) | copy-start | bytes 28
  123.3 22.6 %copy-start.3 = (f32[32,64,1]{2,1,0:T(8,128)S(1)}, f32[32,64,1]{2,1,0:T(8,128)}, u32[]{:S(2)}) copy-start(f32[32,64,1]{2,1,0:T(8,128)} %get-tuple-element.43) | copy-start | bytes 24580
  147.0 15.7 %copy-start = (f32[8,64,384]{2,1,0:T(8,128)S(1)}, f32[8,64,384]{2,1,0:T(8,128)}, u32[]{:S(2)}) copy-start(f32[8,64,384]{2,1,0:T(8,128)} %vel_ref.1) | copy-start | bytes 2359300
  147.0 15.7 %copy-start.1 = (f32[8,64,384]{2,1,0:T(8,128)S(1)}, f32[8,64,384]{2,1,0:T(8,128)}, u32[]{:S(2)}) copy-start(f32[8,64,384]{2,1,0:T(8,128)} %mom_ref.1) | copy-start | bytes 2359300
  147.0 15.7 %copy-start.2 = (f32[8,64,384]{2,1,0:T(8,128)S(1)}, f32[8,64,384]{2,1,0:T(8,128)}, u32[]{:S(2)}) copy-start(f32[8,64,384]{2,1,0:T(8,128)} %mass_ref.1) | copy-start | bytes 2359300
Sparse Core Ops, SparseCore 0:
  9.7 42.9 all-gather.1

commit v7 on v6

--- a/solution.py
+++ b/solution.py
@@ -141,6 +141,125 @@
         name=f"halo_exchange_{collective_id}",
     )(*fields)
     return [outs[4 * j : 4 * j + 4] for j in range(nf)]
+
+
+class HaloSender:
+    def __init__(self, ref, nblk, tb):
+        self.ref, self.nblk, self.tb = ref, nblk, tb
+        row, nrow = lax.axis_index("row"), lax.axis_size("row")
+        col, ncol = lax.axis_index("col"), lax.axis_size("col")
+        self.row, self.nrow, self.col, self.ncol = row, nrow, col, ncol
+        self.has = (row < nrow - 1, row > 0, col < ncol - 1, col > 0)
+        self.peer = ({"row": row + 1}, {"row": row - 1}, {"col": col + 1}, {"col": col - 1})
+        self.filler = (1, 0, 3, 2)
+        self.bufs = [ref[f"h_b{b}"] for b in range(4)]
+
+    def copy(self, d, blk):
+        ref, tb = self.ref, self.tb
+        rows_here = pl.ds(pl.multiple_of(blk * tb, tb), tb)
+        if d == 0:
+            src, dst, sem = ref["stg_xlo"], self.bufs[0], ref["h_ss"].at[0, 0]
+        elif d == 1:
+            src, dst, sem = ref["stg_xhi"], self.bufs[1], ref["h_ss"].at[0, 1]
+        elif d == 2:
+            src, dst = ref["stg_ylo"].at[rows_here], self.bufs[2].at[rows_here, pl.ds(4, 4)]
+            sem = ref["h_ss"].at[blk, 2]
+        else:
+            src, dst = ref["stg_yhi"].at[rows_here], self.bufs[3].at[rows_here, pl.ds(0, 4)]
+            sem = ref["h_ss"].at[blk, 3]
+        return pltpu.make_async_remote_copy(
+            src_ref=src,
+            dst_ref=dst,
+            send_sem=sem,
+            recv_sem=ref["h_rs"].at[d],
+            device_id=self.peer[d],
+            device_id_type=pl.DeviceIdType.MESH,
+        )
+
+    def whole(self, b):
+        ref = self.ref
+        src = {0: ref["stg_xlo"], 1: ref["stg_xhi"], 2: ref["stg_ylo"], 3: ref["stg_yhi"]}[b]
+        dst = {0: self.bufs[0], 1: self.bufs[1], 2: self.bufs[2].at[:, pl.ds(4, 4)], 3: self.bufs[3].at[:, pl.ds(0, 4)]}[b]
+        return pltpu.make_async_remote_copy(
+            src_ref=src,
+            dst_ref=dst,
+            send_sem=ref["h_ss"].at[0, b],
+            recv_sem=ref["h_rs"].at[b],
+            device_id=self.peer[b],
+            device_id_type=pl.DeviceIdType.MESH,
+        )
+
+    def begin(self):
+        ref, has, row, nrow, col, ncol = self.ref, self.has, self.row, self.nrow, self.col, self.ncol
+        barrier = pltpu.get_barrier_semaphore()
+        for d in range(4):
+            @pl.when(has[d])
+            def _():
+                pl.semaphore_signal(barrier, inc=1, device_id=self.peer[d], device_id_type=pl.DeviceIdType.MESH)
+
+        count = (1 - row // (nrow - 1)) + (row + nrow - 1) // nrow + (1 - col // (ncol - 1)) + (col + ncol - 1) // ncol
+        pl.semaphore_wait(barrier, count)
+
+        @pl.when(jnp.logical_not(has[0] & has[1]))
+        def _():
+            ref["h_zx"][...] = jnp.zeros_like(ref["h_zx"])
+
+        @pl.when(jnp.logical_not(has[2] & has[3]))
+        def _():
+            ref["h_zy"][...] = jnp.zeros_like(ref["h_zy"])
+
+        for b in range(4):
+            @pl.when(jnp.logical_not(has[self.filler[b]]))
+            def _():
+                zero = ref["h_zx"] if b < 2 else ref["h_zy"]
+                copy = pltpu.make_async_copy(zero, self.bufs[b], ref["h_zs"].at[b])
+                copy.start()
+                copy.wait()
+
+    def send_block(self, blk):
+        ref, has, tb = self.ref, self.has, self.tb
+
+        @pl.when(blk == 0)
+        def _():
+            ref["stg_xhi"][...] = ref["o_a2"][0:4]
+
+        @pl.when(blk == self.nblk - 1)
+        def _():
+            ref["stg_xlo"][...] = ref["o_a2"][tb - 4 : tb]
+
+        for d in (2, 3):
+            @pl.when(has[d])
+            def _():
+                self.copy(d, blk).start()
+
+        @pl.when(has[1] & (blk == 0))
+        def _():
+            self.copy(1, blk).start()
+
+        @pl.when(has[0] & (blk == self.nblk - 1))
+        def _():
+            self.copy(0, blk).start()
+
+    def finish(self):
+        has = self.has
+        for blk in range(self.nblk):
+            for d in (2, 3):
+                @pl.when(has[d])
+                def _():
+                    self.copy(d, blk).wait_send()
+
+        @pl.when(has[1])
+        def _():
+            self.copy(1, 0).wait_send()
+
+        @pl.when(has[0])
+        def _():
+            self.copy(0, self.nblk - 1).wait_send()
+
+        for b in range(4):
+            @pl.when(has[self.filler[b]])
+            def _():
+                self.whole(b).wait_recv()
 
 
 def step_kernel(kind, names, nf_ex, *refs):
@@ -223,6 +342,12 @@
     if wave:
         ref["o_pick"][...] = jnp.sum(ref["fold"][...], axis=1, keepdims=True).reshape(ref["o_pick"].shape)
     if kind == "wave2":
+        sender = HaloSender(ref, n, tb)
+
+        @pl.when(i == 0)
+        def _():
+            sender.begin()
+
         def inject(r, carry):
             for y0 in range(0, cols, Y_CHUNK):
                 ys = pl.ds(y0, Y_CHUNK)
@@ -231,9 +356,18 @@
                 a2 = ref["a2raw"][r, ys, :] + jnp.where(at_rec, misfit, 0.0)
                 ref["o_a2"][r, ys, :] = a2
                 ref["o_part"][r, ys, :] = a2 * ref["o_dw"][r, ys, :]
+                if y0 == 0:
+                    ref["stg_yhi"][i * tb + r] = a2[0:4]
+                if y0 == cols - Y_CHUNK:
+                    ref["stg_ylo"][i * tb + r] = a2[Y_CHUNK - 4 : Y_CHUNK]
             return carry
 
         lax.fori_loop(0, tb, inject, 0)
+        sender.send_block(i)
+
+        @pl.when(i == n - 1)
+        def _():
+            sender.finish()
 
     if nf_ex:
         @pl.when(i == n - 1)
@@ -285,7 +419,29 @@
     if kind in ("wave1", "wave2"):
         scratch.append(pltpu.VMEM((tb * cols, 128), jnp.float32))
         names.append("fold")
-    if nf_ex:
+    if kind == "wave2":
+        h_shapes, _ = exchange_io(1, rows, cols, depth)
+        names = names[: len(names) - len(scratch)]
+        names += [f"h_b{m}" for m in range(4)]
+        names += ["pad", "fold"]
+        names += ["stg_xlo", "stg_xhi", "stg_ylo", "stg_yhi", "h_zx", "h_zy", "h_ss", "h_rs", "h_zs"]
+        out_shape += h_shapes
+        out_specs += [any_spec] * 4
+        scratch += [
+            pltpu.VMEM((4, cols, depth), jnp.float32),
+            pltpu.VMEM((4, cols, depth), jnp.float32),
+            pltpu.VMEM((rows, 4, depth), jnp.float32),
+            pltpu.VMEM((rows, 4, depth), jnp.float32),
+            pltpu.VMEM((4, cols, depth), jnp.float32),
+            pltpu.VMEM((rows, 8, depth), jnp.float32),
+            pltpu.SemaphoreType.DMA((rows // tb, 4)),
+            pltpu.SemaphoreType.DMA((4,)),
+            pltpu.SemaphoreType.DMA((4,)),
+        ]
+        params = pltpu.CompilerParams(
+            collective_id=collective_id, has_side_effects=True, vmem_limit_bytes=60 * 1024 * 1024
+        )
+    elif nf_ex:
         ex_shapes, ex_scratch = exchange_io(nf_ex, rows, cols, depth)
         k = len(outs)
         names = names[: len(names) - len(scratch)]
@@ -317,6 +473,8 @@
         cost_estimate=cost,
         name=f"leap_{kind}",
     )(*args)
+    if kind == "wave2":
+        return result[: len(outs)], result[len(outs) :]
     if nf_ex:
         own = result[: len(outs)]
         ex = result[len(outs) :]
@@ -435,19 +593,20 @@
     (adj_bulk,), (adv_h,) = leap(
         "adjbulk", adj_now, *adj_h, adj_later, full_velocity, {}, exchanged=[advanced], collective_id=2
     )
-    dw2, pick_far, adj_two, part = leap(
+    (dw2, pick_far, adj_two, part), adj_two_h = leap(
         "wave2",
         advanced,
         *adv_h,
         present,
         full_velocity,
         {"rec": rec, "src": src, "amp": amp[1:2], "a2raw": adj_bulk, "obs": observed[0, 1][:, :, None]},
+        collective_id=3,
     )
     misfit_early = pick_adv - observed[0, 0][:, :, None]
     (imaging,) = leap(
         "adj2",
         adj_two,
-        *exchange([adj_two], 3)[0],
+        *adj_two_h,
         adj_now,
         full_velocity,
         {"rec": rec, "mis": misfit_early, "dw": dw1, "part": part},

time: 208 us -> 203 us (0.976)
  Pallas kernels: 181 us -> 175 us
    pallas_call x2 -> x1, Pallas kernels: 66.9 us -> 44.3 us  [exchange(): pl.pallas_call(functools.partial(exchange_kernel, nf), in_specs=[any_spec...]
    pallas_call x4, Pallas kernels: 78.2 us -> 90.6 us  [leap(): pl.pallas_call(functools.partial(step_kernel, kind, tuple(names), nf_ex),...]
    pallas_call x1, Pallas kernels: 36.1 us -> 40.4 us  [kick(): pl.pallas_call(kick_kernel, in_specs=[pl.BlockSpec(memory_space=pl.ANY),...]
  transfers between devices with their start and end apart: 1 -> 1, of which waited for: 0 -> 0; matrix products, arithmetic and copies ran while one was open for 3% -> 4% of each run, Pallas kernels for 21% -> 22%
where the time goes in v7:
time: 203 us
  Pallas kernels  175 us (86%)
  between operations  15.3 us (8%)
  local copies, waits for them, and re-layouts  7.65 us (4%)
  other arithmetic  3.68 us (2%)
    pallas_call x4, Pallas kernels, leap(): pl.pallas_call(functools.partial(step_kernel, kind, tuple(names), nf_ex),...  90.6 us
    pallas_call x1, Pallas kernels, exchange(): pl.pallas_call(functools.partial(exchange_kernel, nf), in_specs=[any_spec...  44.3 us
    pallas_call x1, Pallas kernels, kick(): pl.pallas_call(kick_kernel, in_specs=[pl.BlockSpec(memory_space=pl.ANY),...  40.4 us
  transfers between devices with their start and end apart: 1, of which 0 were waited for; matrix products, arithmetic and copies ran while one was open for 4% of the time, Pallas kernels for 22%

profile of v7, /device:TPU:1, one launch (start us, length us, event | category | flops | bytes accessed | tf_op | source)
XLA Modules:
  0.0 202.6 jit_solution(1617967698646377222)
XLA Ops:
  7.2 0.0 copy-start.3
  7.2 0.0 all-gather.2.cloned.1.call-start
  7.2 0.7 all-gather.2.cloned.1.call-update
  7.9 0.7 slice_bitcast_fusion
  8.7 0.4 copy.21
  9.1 2.1 %copy.18.refs_9_ = s32[32,64,1]{2,1,0:T(8,128)} copy(s32[32,64,1]{1,0,2:T(8,128)} %bitcast.28) | data formatting | bytes 16384 | tf_op jit(solution)/shard_map/broadcast_in_dim;squeeze | solution.py:578
  11.2 1.4 copy.20.refs_13_
  12.6 0.0 copy-done.3
  12.6 0.6 fusion.1
  14.4 0.0 copy-start.4
  14.4 44.3 %halo_exchange_1.1 = (f32[4,64,384]{2,1,0:T(8,128)}, f32[4,64,384]{2,1,0:T(8,128)}, f32[32,8,384]{2,1,0:T(8,128)}, f32[32,8,384]{2,1,0:T(8,128)}, f32[4,64,384]{...) custom-call(f32[32,64,384]{2,1,0:T(8,128)} %bitcast.21, f32[32,64,384]{2,1,0:T(8,128)} %bitcast.16), custom_call_target="tpu_custom_call" | custom-call | tf_op jit(solution)/shard_map/halo_exchange_1/pallas_call | solution.py:134
  58.7 1.3 pad_add_fusion.refs_10_
  60.0 0.0 copy-done.4
  60.0 0.6 fusion
  60.6 0.0 all-gather.2.cloned.1.call-done.refs_8_
  60.6 16.2 %leap_wave1.1 = (f32[32,64,384]{2,1,0:T(8,128)}, f32[32,64,384]{2,1,0:T(8,128)}, f32[32,64,1]{2,1,0:T(8,128)}) custom-call(f32[32,64,384]{2,1,0:T(8,128)} %bitcast.22, f32[32,64,384]{2,1,0:T(8,128)} %bitcast.23, f32[32,64,384]{2,1,0:T(8,128)} %bitcast.24, f32[4,64,384]{2,1,0:T(8,128)} %get-tuple-element.24.refs_3_, f32[4,64,384]{2,1,0:T(8,128)} %get-tuple-element.25.refs_4_, ...), custom_call_target="tpu_custom_call" | custom-call | flops 47185920 | bytes 18874368 | tf_op jit(solution)/shard_map/leap_wave1/pallas_call | solution.py:465
  76.8 2.4 %sub.11.refs_10_ = f32[32,64,1]{2,1,0:T(8,128)} subtract(f32[32,64,1]{2,1,0:T(8,128)} %get-tuple-element.43, f32[32,64,1]{2,1,0:T(8,128)S(1)} %copy.21) | non-fusion elementwise | flops 2048 | bytes 24576 | tf_op jit(solution)/shard_map/sub | solution.py:605
  79.2 26.2 %leap_adjbulk.1 = (f32[32,64,384]{2,1,0:T(8,128)}, f32[4,64,384]{2,1,0:T(8,128)}, f32[4,64,384]{2,1,0:T(8,128)}, f32[32,8,384]{2,1,0:T(8,128)}, f32[32,8,384]{2,1,0:T(8,128)}) custom-call(f32[32,64,384]{2,1,0:T(8,128)} %bitcast.17, f32[32,64,384]{2,1,0:T(8,128)} %bitcast.18, f32[32,64,384]{2,1,0:T(8,128)} %bitcast.19, ...), custom_call_target="tpu_custom_call" | custom-call | flops 47185920 | bytes 15728640 | tf_op jit(solution)/shard_map/leap_adjbulk/pallas_call | solution.py:465
  105.3 32.5 %leap_wave2.1 = (f32[32,64,384]{2,1,0:T(8,128)}, f32[32,64,1]{2,1,0:T(8,128)}, f32[32,64,384]{2,1,0:T(8,128)}, f32[32,64,384]{2,1,0:T(8,128)}, f32[4,64,384]{2,1...) custom-call(f32[32,64,384]{2,1,0:T(8,128)} %get-tuple-element.28.refs_9_.refs_0_.refs_1_.refs_2_, ...), custom_call_target="tpu_custom_call" | custom-call | flops 47185920 | bytes 25165824 | tf_op jit(solution)/shard_map/leap_wave2/pallas_call | solution.py:465
  137.8 0.0 copy-start
  137.8 0.0 copy-start.1
  137.8 0.0 copy-start.2
  137.8 15.8 %leap_adj2.1.img_ref = f32[32,64,384]{2,1,0:T(8,128)} custom-call(f32[32,64,384]{2,1,0:T(8,128)} %get-tuple-element.38.refs_0_.refs_1_.refs_2_, f32[32,64,384]{2,1,0:T(8,128)} %get-tuple-element.38.refs_0_.refs_1_.refs_2_, f32[32,64,384]{2,1,0:T(8,128)} %get-tuple-element.38.refs_0_.refs_1_.refs_2_, f32[4,64,384]{2,1,0:T(8,128)} %get-tuple-element.39.refs_3_, ...), custom_call_target="tpu_custom_call" | custom-call | flops 47185920 | bytes 22020096 | tf_op jit(solution)/shard_map/leap_adj2/pallas_call | solution.py:465
  153.6 0.0 copy-done
  153.6 0.0 copy-done.1
  153.6 0.0 copy-done.2
  153.6 40.4 %kick_reduce_scatter.1 = (f32[8,64,384]{2,1,0:T(8,128)S(1)}, f32[8,64,384]{2,1,0:T(8,128)S(1)}) custom-call(f32[32,64,384]{2,1,0:T(8,128)} %leap_adj2.1.img_ref, f32[8,64,384]{2,1,0:T(8,128)S(1)} %copy-done, f32[8,64,384]{2,1,0:T(8,128)S(1)} %copy-done.1, f32[8,64,384]{2,1,0:T(8,128)S(1)} %copy-done.2), custom_call_target="tpu_custom_call" | custom-call | tf_op jit(solution)/shard_map/kick_reduce_scatter/pallas_call | solution.py:543
  194.0 0.9 copy.25
  194.9 0.9 copy.26
Async XLA Ops:
  7.2 5.5 %copy-start.3 = (s32[1,3]{1,0:T(1,128)S(1)}, s32[1,3]{1,0:T(1,128)}, u32[]{:S(2)}) copy-start(s32[1,3]{1,0:T(1,128)} %param.20) | copy-start | bytes 40
  7.2 53.4 %all-gather.2.cloned.1.call-start = ((), (), s32[]{:S(2)}) async-start(), calls=%async_computation | async-start | bytes 3932160 | tf_op jit(solution)/shard_map/all_gather | solution.py:572
  14.4 45.6 %copy-start.4 = (f32[1,2]{1,0:T(1,128)S(1)}, f32[1,2]{1,0:T(1,128)}, u32[]{:S(2)}) copy-start(f32[1,2]{1,0:T(1,128)} %param.21) | copy-start | bytes 28
  137.8 15.8 %copy-start = (f32[8,64,384]{2,1,0:T(8,128)S(1)}, f32[8,64,384]{2,1,0:T(8,128)}, u32[]{:S(2)}) copy-start(f32[8,64,384]{2,1,0:T(8,128)} %vel_ref.1) | copy-start | bytes 2359300
  137.8 15.8 %copy-start.1 = (f32[8,64,384]{2,1,0:T(8,128)S(1)}, f32[8,64,384]{2,1,0:T(8,128)}, u32[]{:S(2)}) copy-start(f32[8,64,384]{2,1,0:T(8,128)} %mom_ref.1) | copy-start | bytes 2359300
  137.8 15.8 %copy-start.2 = (f32[8,64,384]{2,1,0:T(8,128)S(1)}, f32[8,64,384]{2,1,0:T(8,128)}, u32[]{:S(2)}) copy-start(f32[8,64,384]{2,1,0:T(8,128)} %mass_ref.1) | copy-start | bytes 2359300
Sparse Core Ops, SparseCore 0:
  9.7 42.9 all-gather.1

commit v8 on v7

--- a/solution.py
+++ b/solution.py
@@ -11,11 +11,66 @@
 squared_courant = 0.012
 leap_step = 0.2
 
+class S:
+    a2raw = 0
+    amp = 1
+    dw = 2
+    ex_rs = 3
+    ex_ss = 4
+    ex_zs = 5
+    ex_zx = 6
+    ex_zy = 7
+    f = 8
+    fhi = 9
+    flo = 10
+    fold = 11
+    h_rs = 12
+    h_ss = 13
+    h_zs = 14
+    h_zx = 15
+    h_zy = 16
+    mass = 17
+    mis = 18
+    mom = 19
+    o_a2 = 20
+    o_dw = 21
+    o_f = 22
+    o_p = 23
+    o_part = 24
+    o_pick = 25
+    o_v = 26
+    obs = 27
+    pad = 28
+    part = 29
+    prev = 30
+    rec = 31
+    rs_own = 32
+    rs_rs = 33
+    rs_ss = 34
+    slot_in = 35
+    slot_out = 36
+    src = 37
+    stg_xhi = 38
+    stg_xlo = 39
+    stg_yhi = 40
+    stg_ylo = 41
+    vel = 42
+    vslab = 43
+    xhi = 44
+    xlo = 45
+    yhi = 46
+    ylo = 47
+    ex_f = 100
+    ex_b = 110
+    h_b = 130
+
+
 ROWS_PER_STEP = 8
 Y_CHUNK = 8
 
 
 class Exchange:
+
     def __init__(self, fields, bufs, zero_x, zero_y, send_sem, recv_sem, zero_sem):
         self.fields, self.bufs = fields, bufs
         self.zero_x, self.zero_y = zero_x, zero_y
@@ -144,6 +199,7 @@
 
 
 class HaloSender:
+
     def __init__(self, ref, nblk, tb):
         self.ref, self.nblk, self.tb = ref, nblk, tb
         row, nrow = lax.axis_index("row"), lax.axis_size("row")
@@ -152,39 +208,39 @@
         self.has = (row < nrow - 1, row > 0, col < ncol - 1, col > 0)
         self.peer = ({"row": row + 1}, {"row": row - 1}, {"col": col + 1}, {"col": col - 1})
         self.filler = (1, 0, 3, 2)
-        self.bufs = [ref[f"h_b{b}"] for b in range(4)]
+        self.bufs = [ref[S.h_b + b] for b in range(4)]
 
     def copy(self, d, blk):
         ref, tb = self.ref, self.tb
         rows_here = pl.ds(pl.multiple_of(blk * tb, tb), tb)
         if d == 0:
-            src, dst, sem = ref["stg_xlo"], self.bufs[0], ref["h_ss"].at[0, 0]
+            src, dst, sem = ref[S.stg_xlo], self.bufs[0], ref[S.h_ss].at[0, 0]
         elif d == 1:
-            src, dst, sem = ref["stg_xhi"], self.bufs[1], ref["h_ss"].at[0, 1]
+            src, dst, sem = ref[S.stg_xhi], self.bufs[1], ref[S.h_ss].at[0, 1]
         elif d == 2:
-            src, dst = ref["stg_ylo"].at[rows_here], self.bufs[2].at[rows_here, pl.ds(4, 4)]
-            sem = ref["h_ss"].at[blk, 2]
+            src, dst = ref[S.stg_ylo].at[rows_here], self.bufs[2].at[rows_here, pl.ds(4, 4)]
+            sem = ref[S.h_ss].at[blk, 2]
         else:
-            src, dst = ref["stg_yhi"].at[rows_here], self.bufs[3].at[rows_here, pl.ds(0, 4)]
-            sem = ref["h_ss"].at[blk, 3]
+            src, dst = ref[S.stg_yhi].at[rows_here], self.bufs[3].at[rows_here, pl.ds(0, 4)]
+            sem = ref[S.h_ss].at[blk, 3]
         return pltpu.make_async_remote_copy(
             src_ref=src,
             dst_ref=dst,
             send_sem=sem,
-            recv_sem=ref["h_rs"].at[d],
+            recv_sem=ref[S.h_rs].at[d],
             device_id=self.peer[d],
             device_id_type=pl.DeviceIdType.MESH,
         )
 
     def whole(self, b):
         ref = self.ref
-        src = {0: ref["stg_xlo"], 1: ref["stg_xhi"], 2: ref["stg_ylo"], 3: ref["stg_yhi"]}[b]
+        src = {0: ref[S.stg_xlo], 1: ref[S.stg_xhi], 2: ref[S.stg_ylo], 3: ref[S.stg_yhi]}[b]
         dst = {0: self.bufs[0], 1: self.bufs[1], 2: self.bufs[2].at[:, pl.ds(4, 4)], 3: self.bufs[3].at[:, pl.ds(0, 4)]}[b]
         return pltpu.make_async_remote_copy(
             src_ref=src,
             dst_ref=dst,
-            send_sem=ref["h_ss"].at[0, b],
-            recv_sem=ref["h_rs"].at[b],
+            send_sem=ref[S.h_ss].at[0, b],
+            recv_sem=ref[S.h_rs].at[b],
             device_id=self.peer[b],
             device_id_type=pl.DeviceIdType.MESH,
         )
@@ -202,17 +258,17 @@
 
         @pl.when(jnp.logical_not(has[0] & has[1]))
         def _():
-            ref["h_zx"][...] = jnp.zeros_like(ref["h_zx"])
+            ref[S.h_zx][...] = jnp.zeros_like(ref[S.h_zx])
 
         @pl.when(jnp.logical_not(has[2] & has[3]))
         def _():
-            ref["h_zy"][...] = jnp.zeros_like(ref["h_zy"])
+            ref[S.h_zy][...] = jnp.zeros_like(ref[S.h_zy])
 
         for b in range(4):
             @pl.when(jnp.logical_not(has[self.filler[b]]))
             def _():
-                zero = ref["h_zx"] if b < 2 else ref["h_zy"]
-                copy = pltpu.make_async_copy(zero, self.bufs[b], ref["h_zs"].at[b])
+                zero = ref[S.h_zx] if b < 2 else ref[S.h_zy]
+                copy = pltpu.make_async_copy(zero, self.bufs[b], ref[S.h_zs].at[b])
                 copy.start()
                 copy.wait()
 
@@ -221,11 +277,11 @@
 
         @pl.when(blk == 0)
         def _():
-            ref["stg_xhi"][...] = ref["o_a2"][0:4]
+            ref[S.stg_xhi][...] = ref[S.o_a2][0:4]
 
         @pl.when(blk == self.nblk - 1)
         def _():
-            ref["stg_xlo"][...] = ref["o_a2"][tb - 4 : tb]
+            ref[S.stg_xlo][...] = ref[S.o_a2][tb - 4 : tb]
 
         for d in (2, 3):
             @pl.when(has[d])
@@ -262,41 +318,116 @@
                 self.whole(b).wait_recv()
 
 
+class ReduceScatter:
+
+    def __init__(self, ref, me, n):
+        self.ref, self.me, self.n = ref, me, n
+
+    def copy(self, blk):
+        ref = self.ref
+        return pltpu.make_async_remote_copy(
+            src_ref=ref[S.slot_out].at[blk],
+            dst_ref=ref[S.slot_in].at[self.me],
+            send_sem=ref[S.rs_ss].at[blk],
+            recv_sem=ref[S.rs_rs].at[self.me],
+            device_id={"shot": blk},
+            device_id_type=pl.DeviceIdType.MESH,
+        )
+
+    def begin(self):
+        barrier = pltpu.get_barrier_semaphore()
+        for d in range(1, self.n):
+            pl.semaphore_signal(
+                barrier, inc=1, device_id={"shot": lax.rem(self.me + d, self.n)}, device_id_type=pl.DeviceIdType.MESH
+            )
+        pl.semaphore_wait(barrier, self.n - 1)
+
+    def send(self, blk):
+        self.copy(blk).start()
+
+    def finish(self):
+        ref, me, n = self.ref, self.me, self.n
+        own = pltpu.make_async_copy(ref[S.slot_out].at[me], ref[S.slot_in].at[me], ref[S.rs_own])
+        own.start()
+        for d in range(1, n):
+            self.copy(lax.rem(me + d, n)).wait_send()
+        own.wait()
+        for d in range(1, n):
+            src = lax.rem(me + d, n)
+            pltpu.make_async_remote_copy(
+                src_ref=ref[S.slot_out].at[src],
+                dst_ref=ref[S.slot_in].at[src],
+                send_sem=ref[S.rs_ss].at[src],
+                recv_sem=ref[S.rs_rs].at[src],
+                device_id={"shot": src},
+                device_id_type=pl.DeviceIdType.MESH,
+            ).wait_recv()
+
+        slot_in = ref[S.slot_in]
+
+        def row(r, carry):
+            summed = slot_in[0, r]
+            for s_ in range(1, n):
+                summed = summed + slot_in[s_, r]
+            v = ref[S.vslab][r]
+            gradient = 2.0 / v * summed
+            p_half = ref[S.mom][r] - 0.5 * leap_step * gradient
+            ref[S.o_p][r] = p_half
+            ref[S.o_v][r] = v + leap_step * p_half / ref[S.mass][r]
+            return carry
+
+        lax.fori_loop(0, slot_in.shape[1], row, 0)
+
+
 def step_kernel(kind, names, nf_ex, *refs):
     ref = dict(zip(names, refs))
     if nf_ex:
         ex = Exchange(
-            [ref[f"ex_f{j}"] for j in range(nf_ex)],
-            [ref[f"ex_b{k}"] for k in range(4 * nf_ex)],
-            *[ref[k] for k in ("ex_zx", "ex_zy", "ex_ss", "ex_rs", "ex_zs")],
+            [ref[S.ex_f + j] for j in range(nf_ex)],
+            [ref[S.ex_b + k] for k in range(4 * nf_ex)],
+            *[ref[k] for k in (S.ex_zx, S.ex_zy, S.ex_ss, S.ex_rs, S.ex_zs)],
         )
-    f_ref, pad = ref["f"], ref["pad"]
+    f_ref, pad = ref[S.f], ref[S.pad]
     tb, cols, depth = f_ref.shape
-    i = pl.program_id(0)
     n = pl.num_programs(0)
+    step = pl.program_id(0)
+    if kind == "adj2":
+        me = lax.axis_index("shot")
+        i = lax.rem(me + 1 + step, n)
+        rs = ReduceScatter(ref, me, n)
+
+        @pl.when(step == 0)
+        def _():
+            rs.begin()
+
+        @pl.when(step > 0)
+        def _():
+            rs.send(lax.rem(me + step, n))
+    else:
+        i = step
 
     if nf_ex:
         @pl.when(i == 0)
         def _():
             ex.start()
 
-    lo = jnp.where(i == 0, ref["xlo"][...], ref["flo"][...])
-    hi = jnp.where(i == n - 1, ref["xhi"][...], ref["fhi"][...])
+    lo = jnp.where(i == 0, ref[S.xlo][...], ref[S.flo][...])
+    hi = jnp.where(i == n - 1, ref[S.xhi][...], ref[S.fhi][...])
     pad[0:4, 8 : 8 + cols, :] = lo
     pad[4 : 4 + tb, 8 : 8 + cols, :] = f_ref[...]
     pad[4 + tb : 8 + tb, 8 : 8 + cols, :] = hi
-    pad[4 : 4 + tb, 0:8, :] = ref["ylo"][...]
-    pad[4 : 4 + tb, 8 + cols : 16 + cols, :] = ref["yhi"][...]
+    pad[4 : 4 + tb, 0:8, :] = ref[S.ylo][...]
+    pad[4 : 4 + tb, 8 + cols : 16 + cols, :] = ref[S.yhi][...]
 
     z_index = lax.broadcasted_iota(jnp.int32, (Y_CHUNK, depth), 1)
     y_index = lax.broadcasted_iota(jnp.int32, (Y_CHUNK, depth), 0)
     wave = kind in ("wave1", "wave2")
     if wave:
-        src_ref = ref["src"]
+        src_ref = ref[S.src]
         src_x = src_ref[0] - i * tb
         src_y = src_ref[1]
         src_z = src_ref[2]
-        amp = ref["amp"][0]
+        amp = ref[S.amp][0]
 
     def row(r, carry):
         for y0 in range(0, cols, Y_CHUNK):
@@ -314,33 +445,33 @@
                 zm = jnp.where(z_index >= k, pltpu.roll(c, k, 1), 0.0)
                 along = along + (zp + zm)
                 result = result + STENCIL[k] * along
-            v = ref["vel"][r, ys, :]
+            v = ref[S.vel][r, ys, :]
             stiff = squared_courant * v * v
-            prev = ref["prev"][r, ys, :]
+            prev = ref[S.prev][r, ys, :]
             out = 2.0 * c - prev + stiff * result
             if wave:
-                at_rec = z_index == ref["rec"][r, ys, :]
+                at_rec = z_index == ref[S.rec][r, ys, :]
                 hit = (r == src_x) & (y_index + y0 == src_y) & (z_index == src_z)
                 out = out + jnp.where(hit, amp, 0.0)
                 sel = jnp.where(at_rec, out, 0.0)
                 folded = sel[:, 0:128]
                 for t in range(128, depth, 128):
                     folded = folded + sel[:, t : t + 128]
-                ref["fold"][pl.ds(pl.multiple_of(r * cols + y0, Y_CHUNK), Y_CHUNK), :] = folded
-                ref["o_dw"][r, ys, :] = (out - 2.0 * c) + prev
+                ref[S.fold][pl.ds(pl.multiple_of(r * cols + y0, Y_CHUNK), Y_CHUNK), :] = folded
+                ref[S.o_dw][r, ys, :] = (out - 2.0 * c) + prev
                 if kind == "wave1":
-                    ref["o_f"][r, ys, :] = out
+                    ref[S.o_f][r, ys, :] = out
             elif kind == "adjbulk":
-                ref["o_f"][r, ys, :] = out
+                ref[S.o_f][r, ys, :] = out
             else:
-                at_rec = z_index == ref["rec"][r, ys, :]
-                out = out + jnp.where(at_rec, ref["mis"][r, ys, :], 0.0)
-                ref["o_img"][r, ys, :] = ref["part"][r, ys, :] + out * ref["dw"][r, ys, :]
+                at_rec = z_index == ref[S.rec][r, ys, :]
+                out = out + jnp.where(at_rec, ref[S.mis][r, ys, :], 0.0)
+                ref[S.slot_out][i, r, ys, :] = ref[S.part][r, ys, :] + out * ref[S.dw][r, ys, :]
         return carry
 
     lax.fori_loop(0, tb, row, 0)
     if wave:
-        ref["o_pick"][...] = jnp.sum(ref["fold"][...], axis=1, keepdims=True).reshape(ref["o_pick"].shape)
+        ref[S.o_pick][...] = jnp.sum(ref[S.fold][...], axis=1, keepdims=True).reshape(ref[S.o_pick].shape)
     if kind == "wave2":
         sender = HaloSender(ref, n, tb)
 
@@ -351,15 +482,15 @@
         def inject(r, carry):
             for y0 in range(0, cols, Y_CHUNK):
                 ys = pl.ds(y0, Y_CHUNK)
-                at_rec = z_index == ref["rec"][r, ys, :]
-                misfit = ref["o_pick"][r, ys, :] - ref["obs"][r, ys, :]
-                a2 = ref["a2raw"][r, ys, :] + jnp.where(at_rec, misfit, 0.0)
-                ref["o_a2"][r, ys, :] = a2
-                ref["o_part"][r, ys, :] = a2 * ref["o_dw"][r, ys, :]
+                at_rec = z_index == ref[S.rec][r, ys, :]
+                misfit = ref[S.o_pick][r, ys, :] - ref[S.obs][r, ys, :]
+                a2 = ref[S.a2raw][r, ys, :] + jnp.where(at_rec, misfit, 0.0)
+                ref[S.o_a2][r, ys, :] = a2
+                ref[S.o_part][r, ys, :] = a2 * ref[S.o_dw][r, ys, :]
                 if y0 == 0:
-                    ref["stg_yhi"][i * tb + r] = a2[0:4]
+                    ref[S.stg_yhi][i * tb + r] = a2[0:4]
                 if y0 == cols - Y_CHUNK:
-                    ref["stg_ylo"][i * tb + r] = a2[Y_CHUNK - 4 : Y_CHUNK]
+                    ref[S.stg_ylo][i * tb + r] = a2[Y_CHUNK - 4 : Y_CHUNK]
             return carry
 
         lax.fori_loop(0, tb, inject, 0)
@@ -373,26 +504,42 @@
         @pl.when(i == n - 1)
         def _():
             ex.finish()
+    if kind == "adj2":
+        @pl.when(step == n - 1)
+        def _():
+            rs.finish()
 
 
 def leap(kind, f, xlo, xhi, ylo, yhi, prev, vel, extra, exchanged=(), collective_id=None):
     rows, cols, depth = f.shape
     tb = ROWS_PER_STEP
-    grid = (rows // tb,)
+    nblk = rows // tb
+    grid = (nblk,)
     nq = rows // 4
-    block = pl.BlockSpec((tb, cols, depth), lambda i: (i, 0, 0))
-    lo_spec = pl.BlockSpec((4, cols, depth), lambda i: (jnp.maximum(2 * i - 1, 0), 0, 0))
-    hi_spec = pl.BlockSpec((4, cols, depth), lambda i: (jnp.minimum(2 * i + 2, nq - 1), 0, 0))
-    whole4 = pl.BlockSpec((4, cols, depth), lambda i: (0, 0, 0))
-    yspec = pl.BlockSpec((tb, 8, depth), lambda i: (i, 0, 0))
-    col1 = pl.BlockSpec((tb, cols, 1), lambda i: (i, 0, 0))
+    if kind == "adj2":
+        def at(fn):
+            return lambda i: fn(lax.rem(lax.axis_index("shot") + 1 + i, nblk))
+
+        fixed = at
+    else:
+        def at(fn):
+            return fn
+
+        fixed = at
+    block = pl.BlockSpec((tb, cols, depth), at(lambda i: (i, 0, 0)))
+    lo_spec = pl.BlockSpec((4, cols, depth), at(lambda i: (jnp.maximum(2 * i - 1, 0), 0, 0)))
+    hi_spec = pl.BlockSpec((4, cols, depth), at(lambda i: (jnp.minimum(2 * i + 2, nq - 1), 0, 0)))
+    whole4 = pl.BlockSpec((4, cols, depth), fixed(lambda i: (0, 0, 0)))
+    yspec = pl.BlockSpec((tb, 8, depth), at(lambda i: (i, 0, 0)))
+    col1 = pl.BlockSpec((tb, cols, 1), at(lambda i: (i, 0, 0)))
+    slab = pl.BlockSpec((tb, cols, depth), fixed(lambda i: (0, 0, 0)))
     smem = pl.BlockSpec(memory_space=pltpu.SMEM)
     any_spec = pl.BlockSpec(memory_space=pl.ANY)
     field = jax.ShapeDtypeStruct((rows, cols, depth), jnp.float32)
     picked = jax.ShapeDtypeStruct((rows, cols, 1), jnp.float32)
-    spec_of = {"src": smem, "amp": smem, "rec": col1, "mis": col1, "obs": col1}
-
-    names = ["f", "flo", "fhi", "xlo", "xhi", "ylo", "yhi", "prev", "vel"]
+    spec_of = {S.src: smem, S.amp: smem, S.rec: col1, S.mis: col1, S.obs: col1, S.vslab: slab, S.mom: slab, S.mass: slab}
+
+    names = [S.f, S.flo, S.fhi, S.xlo, S.xhi, S.ylo, S.yhi, S.prev, S.vel]
     in_specs = [block, lo_spec, hi_spec, whole4, whole4, yspec, yspec, block, block]
     args = [f, f, f, xlo, xhi, ylo, yhi, prev, vel]
     for key, value in extra.items():
@@ -401,30 +548,45 @@
         args.append(value)
     nf_ex = len(exchanged)
     for j, g in enumerate(exchanged):
-        names.append(f"ex_f{j}")
+        names.append(S.ex_f + j)
         in_specs.append(any_spec)
         args.append(g)
 
     outs = {
-        "wave1": [("o_f", field, block), ("o_dw", field, block), ("o_pick", picked, col1)],
-        "wave2": [("o_dw", field, block), ("o_pick", picked, col1), ("o_a2", field, block), ("o_part", field, block)],
-        "adjbulk": [("o_f", field, block)],
-        "adj2": [("o_img", field, block)],
+        "wave1": [(S.o_f, field, block), (S.o_dw, field, block), (S.o_pick, picked, col1)],
+        "wave2": [(S.o_dw, field, block), (S.o_pick, picked, col1), (S.o_a2, field, block), (S.o_part, field, block)],
+        "adjbulk": [(S.o_f, field, block)],
+        "adj2": [
+            (S.o_v, jax.ShapeDtypeStruct((tb, cols, depth), jnp.float32), slab),
+            (S.o_p, jax.ShapeDtypeStruct((tb, cols, depth), jnp.float32), slab),
+        ],
     }[kind]
     names += [o[0] for o in outs]
     out_shape = [o[1] for o in outs]
     out_specs = [o[2] for o in outs]
     scratch = [pltpu.VMEM((tb + 8, cols + 16, depth), jnp.float32)]
-    names.append("pad")
+    names.append(S.pad)
     if kind in ("wave1", "wave2"):
         scratch.append(pltpu.VMEM((tb * cols, 128), jnp.float32))
-        names.append("fold")
-    if kind == "wave2":
+        names.append(S.fold)
+    if kind == "adj2":
+        names += [S.slot_out, S.slot_in, S.rs_ss, S.rs_rs, S.rs_own]
+        scratch += [
+            pltpu.VMEM((nblk, tb, cols, depth), jnp.float32),
+            pltpu.VMEM((nblk, tb, cols, depth), jnp.float32),
+            pltpu.SemaphoreType.DMA((nblk,)),
+            pltpu.SemaphoreType.DMA((nblk,)),
+            pltpu.SemaphoreType.DMA(()),
+        ]
+        params = pltpu.CompilerParams(
+            collective_id=collective_id, has_side_effects=True, vmem_limit_bytes=60 * 1024 * 1024
+        )
+    elif kind == "wave2":
         h_shapes, _ = exchange_io(1, rows, cols, depth)
         names = names[: len(names) - len(scratch)]
-        names += [f"h_b{m}" for m in range(4)]
-        names += ["pad", "fold"]
-        names += ["stg_xlo", "stg_xhi", "stg_ylo", "stg_yhi", "h_zx", "h_zy", "h_ss", "h_rs", "h_zs"]
+        names += [S.h_b + m for m in range(4)]
+        names += [S.pad, S.fold]
+        names += [S.stg_xlo, S.stg_xhi, S.stg_ylo, S.stg_yhi, S.h_zx, S.h_zy, S.h_ss, S.h_rs, S.h_zs]
         out_shape += h_shapes
         out_specs += [any_spec] * 4
         scratch += [
@@ -445,9 +607,9 @@
         ex_shapes, ex_scratch = exchange_io(nf_ex, rows, cols, depth)
         k = len(outs)
         names = names[: len(names) - len(scratch)]
-        names += [f"ex_b{m}" for m in range(4 * nf_ex)]
-        names += ["pad", "fold"][: len(scratch)]
-        names += ["ex_zx", "ex_zy", "ex_ss", "ex_rs", "ex_zs"]
+        names += [S.ex_b + m for m in range(4 * nf_ex)]
+        names += [S.pad, S.fold][: len(scratch)]
+        names += [S.ex_zx, S.ex_zy, S.ex_ss, S.ex_rs, S.ex_zs]
         out_shape += ex_shapes
         out_specs += [any_spec] * len(ex_shapes)
         scratch += ex_scratch
@@ -482,80 +644,6 @@
     return result
 
 
-def kick_kernel(img_ref, vel_ref, mom_ref, mass_ref, v_out, p_out, recv, send_sem, recv_sem, own_sem):
-    me = lax.axis_index("shot")
-    n = lax.axis_size("shot")
-    rows = vel_ref.shape[0]
-    mesh = pl.DeviceIdType.MESH
-
-    barrier = pltpu.get_barrier_semaphore()
-    for d in range(1, n):
-        pl.semaphore_signal(barrier, inc=1, device_id={"shot": lax.rem(me + d, n)}, device_id_type=mesh)
-    pl.semaphore_wait(barrier, n - 1)
-
-    sends = []
-    for d in (1, n - 1) + tuple(range(2, n - 1)):
-        peer = lax.rem(me + d, n)
-        copy = pltpu.make_async_remote_copy(
-            src_ref=img_ref.at[pl.ds(pl.multiple_of(peer * rows, rows), rows)],
-            dst_ref=recv.at[me],
-            send_sem=send_sem.at[d],
-            recv_sem=recv_sem.at[me],
-            device_id={"shot": peer},
-            device_id_type=mesh,
-        )
-        copy.start()
-        sends.append(copy)
-    own = pltpu.make_async_copy(img_ref.at[pl.ds(pl.multiple_of(me * rows, rows), rows)], recv.at[me], own_sem)
-    own.start()
-    for copy in sends:
-        copy.wait_send()
-    own.wait()
-    for d in range(1, n):
-        src = lax.rem(me + d, n)
-        pltpu.make_async_remote_copy(
-            src_ref=img_ref.at[pl.ds(0, rows)],
-            dst_ref=recv.at[src],
-            send_sem=send_sem.at[d],
-            recv_sem=recv_sem.at[src],
-            device_id={"shot": src},
-            device_id_type=mesh,
-        ).wait_recv()
-
-    def row(r, carry):
-        summed = recv[0, r]
-        for s in range(1, n):
-            summed = summed + recv[s, r]
-        v = vel_ref[r]
-        gradient = 2.0 / v * summed
-        p_half = mom_ref[r] - 0.5 * leap_step * gradient
-        p_out[r] = p_half
-        v_out[r] = v + leap_step * p_half / mass_ref[r]
-        return carry
-
-    lax.fori_loop(0, rows, row, 0)
-
-
-def kick(imaging, velocity, momentum, mass_diag):
-    n = lax.axis_size("shot")
-    vmem = pl.BlockSpec(memory_space=pltpu.VMEM)
-    slab = jax.ShapeDtypeStruct(velocity.shape, jnp.float32)
-    return pl.pallas_call(
-        kick_kernel,
-        in_specs=[pl.BlockSpec(memory_space=pl.ANY), vmem, vmem, vmem],
-        out_specs=[vmem, vmem],
-        out_shape=[slab, slab],
-        scratch_shapes=[
-            pltpu.VMEM((n,) + velocity.shape, jnp.float32),
-            pltpu.SemaphoreType.DMA((n,)),
-            pltpu.SemaphoreType.DMA((n,)),
-            pltpu.SemaphoreType.DMA(()),
-        ],
-        compiler_params=pltpu.CompilerParams(collective_id=0, has_side_effects=True, vmem_limit_bytes=48 * 1024 * 1024),
-        name="kick_reduce_scatter",
-    )(imaging, velocity, momentum, mass_diag)
-
-
 def on_device(
     velocity,
     momentum,
@@ -588,7 +676,7 @@
 
     wave_h, adj_h = exchange([present, adj_now], 1)
     advanced, dw1, pick_adv = leap(
-        "wave1", present, *wave_h, oldest, full_velocity, {"rec": rec, "src": src, "amp": amp[0:1]}
+        "wave1", present, *wave_h, oldest, full_velocity, {S.rec: rec, S.src: src, S.amp: amp[0:1]}
     )
     (adj_bulk,), (adv_h,) = leap(
         "adjbulk", adj_now, *adj_h, adj_later, full_velocity, {}, exchanged=[advanced], collective_id=2
@@ -599,19 +687,27 @@
         *adv_h,
         present,
         full_velocity,
-        {"rec": rec, "src": src, "amp": amp[1:2], "a2raw": adj_bulk, "obs": observed[0, 1][:, :, None]},
+        {S.rec: rec, S.src: src, S.amp: amp[1:2], S.a2raw: adj_bulk, S.obs: observed[0, 1][:, :, None]},
         collective_id=3,
     )
     misfit_early = pick_adv - observed[0, 0][:, :, None]
-    (imaging,) = leap(
+    v_new, p_half = leap(
         "adj2",
         adj_two,
         *adj_two_h,
         adj_now,
         full_velocity,
-        {"rec": rec, "mis": misfit_early, "dw": dw1, "part": part},
+        {
+            S.rec: rec,
+            S.mis: misfit_early,
+            S.dw: dw1,
+            S.part: part,
+            S.vslab: velocity,
+            S.mom: momentum,
+            S.mass: mass_diag,
+        },
+        collective_id=0,
     )
-    v_new, p_half = kick(imaging, velocity, momentum, mass_diag)
     return (v_new, p_half)
 
 

time: 203 us -> 200 us (0.985)
  Pallas kernels: 175 us -> 170 us
  local copies, waits for them, and re-layouts: 7.65 us -> 9.99 us
    pallas_call x1 -> x0, Pallas kernels: 40.4 us -> none  [kick(): pl.pallas_call(kick_kernel, in_specs=[pl.BlockSpec(memory_space=pl.ANY),...]
    pallas_call x4, Pallas kernels: 90.6 us -> 125 us  [leap(): pl.pallas_call(functools.partial(step_kernel, kind, tuple(names), nf_ex),...]
    unnamed x12 -> x6, local copies, waits for them, and re-layouts: 1.79 us -> 4.15 us
where the time goes in v8:
time: 200 us; the launch traced here: 199 us
  Pallas kernels  170 us (85%)
  between operations  15.4 us (8%)
  local copies, waits for them, and re-layouts  9.99 us (5%)
  other arithmetic  3.68 us (2%)
    pallas_call x4, Pallas kernels, leap(): pl.pallas_call(functools.partial(step_kernel, kind, tuple(names), nf_ex),...  125 us
    pallas_call x1, Pallas kernels, exchange(): pl.pallas_call(functools.partial(exchange_kernel, nf), in_specs=[any_spec...  44.3 us
    unnamed x6, local copies, waits for them, and re-layouts  4.15 us
  transfers between devices with their start and end apart: 1, of which 0 were waited for; matrix products, arithmetic and copies ran while one was open for 4% of the time, Pallas kernels for 22%

profile of v8, /device:TPU:1, one launch (start us, length us, event | category | flops | bytes accessed | tf_op | source)
XLA Modules:
  0.0 199.3 jit_solution(173272674359113087)
XLA Ops:
  7.2 0.0 copy-start
  7.2 0.0 all-gather.2.cloned.1.call-start
  7.2 0.7 all-gather.2.cloned.1.call-update
  7.9 0.7 slice_bitcast_fusion
  8.7 0.4 copy.21
  9.1 2.1 %copy.18.refs_9_ = s32[32,64,1]{2,1,0:T(8,128)} copy(s32[32,64,1]{1,0,2:T(8,128)} %bitcast.28) | data formatting | bytes 16384 | tf_op jit(solution)/shard_map/broadcast_in_dim;squeeze | solution.py:666
  11.2 1.4 copy.20.refs_13_
  12.6 0.0 copy-done
  12.6 0.6 fusion.1
  14.5 0.0 copy-start.1
  14.5 44.3 %halo_exchange_1.1 = (f32[4,64,384]{2,1,0:T(8,128)}, f32[4,64,384]{2,1,0:T(8,128)}, f32[32,8,384]{2,1,0:T(8,128)}, f32[32,8,384]{2,1,0:T(8,128)}, f32[4,64,384]{...) custom-call(f32[32,64,384]{2,1,0:T(8,128)} %bitcast.16, f32[32,64,384]{2,1,0:T(8,128)} %bitcast.21), custom_call_target="tpu_custom_call" | custom-call | tf_op jit(solution)/shard_map/halo_exchange_1/pallas_call | solution.py:189
  58.7 1.3 pad_add_fusion.refs_10_
  60.0 0.0 copy-done.1
  60.0 0.6 fusion
  60.6 0.0 all-gather.2.cloned.1.call-done.refs_8_
  60.6 16.2 %leap_wave1.1 = (f32[32,64,384]{2,1,0:T(8,128)}, f32[32,64,384]{2,1,0:T(8,128)}, f32[32,64,1]{2,1,0:T(8,128)}) custom-call(f32[32,64,384]{2,1,0:T(8,128)} %bitcast.17, f32[32,64,384]{2,1,0:T(8,128)} %bitcast.18, f32[32,64,384]{2,1,0:T(8,128)} %bitcast.19, f32[4,64,384]{2,1,0:T(8,128)} %get-tuple-element.24.refs_3_, f32[4,64,384]{2,1,0:T(8,128)} %get-tuple-element.25.refs_4_, ...), custom_call_target="tpu_custom_call" | custom-call | flops 47185920 | bytes 18874368 | tf_op jit(solution)/shard_map/leap_wave1/pallas_call | solution.py:627
  76.8 2.4 %sub.11.refs_10_ = f32[32,64,1]{2,1,0:T(8,128)} subtract(f32[32,64,1]{2,1,0:T(8,128)} %get-tuple-element.43, f32[32,64,1]{2,1,0:T(8,128)S(1)} %copy.21) | non-fusion elementwise | flops 2048 | bytes 24576 | tf_op jit(solution)/shard_map/sub | solution.py:693
  79.2 26.2 %leap_adjbulk.1 = (f32[32,64,384]{2,1,0:T(8,128)}, f32[4,64,384]{2,1,0:T(8,128)}, f32[4,64,384]{2,1,0:T(8,128)}, f32[32,8,384]{2,1,0:T(8,128)}, f32[32,8,384]{2,1,0:T(8,128)}) custom-call(f32[32,64,384]{2,1,0:T(8,128)} %bitcast.22, f32[32,64,384]{2,1,0:T(8,128)} %bitcast.23, f32[32,64,384]{2,1,0:T(8,128)} %bitcast.24, ...), custom_call_target="tpu_custom_call" | custom-call | flops 47185920 | bytes 15728640 | tf_op jit(solution)/shard_map/leap_adjbulk/pallas_call | solution.py:627
  105.4 32.5 %leap_wave2.1 = (f32[32,64,384]{2,1,0:T(8,128)}, f32[32,64,1]{2,1,0:T(8,128)}, f32[32,64,384]{2,1,0:T(8,128)}, f32[32,64,384]{2,1,0:T(8,128)}, f32[4,64,384]{2,1...) custom-call(f32[32,64,384]{2,1,0:T(8,128)} %get-tuple-element.28.refs_9_.refs_0_.refs_1_.refs_2_, ...), custom_call_target="tpu_custom_call" | custom-call | flops 47185920 | bytes 25165824 | tf_op jit(solution)/shard_map/leap_wave2/pallas_call | solution.py:627
  137.8 50.5 %leap_adj2.1 = (f32[8,64,384]{2,1,0:T(8,128)}, f32[8,64,384]{2,1,0:T(8,128)}) custom-call(f32[32,64,384]{2,1,0:T(8,128)} %get-tuple-element.38.refs_0_.refs_1_.refs_2_, f32[32,64,384]{2,1,0:T(8,128)} %get-tuple-element.38.refs_0_.refs_1_.refs_2_, f32[32,64,384]{2,1,0:T(8,128)} %get-tuple-element.38.refs_0_.refs_1_.refs_2_, ...), custom_call_target="tpu_custom_call" | custom-call | flops 47185920 | bytes 18874368 | tf_op jit(solution)/shard_map/leap_adj2/pallas_call | solution.py:627
  188.3 2.1 %copy.25 = f32[8,64,384]{2,1,0:T(8,128)} copy(f32[8,64,384]{2,1,0:T(8,128)} %get-tuple-element.55) | data formatting | bytes 1572864
  190.4 2.1 %copy.26 = f32[8,64,384]{2,1,0:T(8,128)} copy(f32[8,64,384]{2,1,0:T(8,128)} %get-tuple-element.56) | data formatting | bytes 1572864
Async XLA Ops:
  7.2 5.4 %copy-start = (s32[1,3]{1,0:T(1,128)S(1)}, s32[1,3]{1,0:T(1,128)}, u32[]{:S(2)}) copy-start(s32[1,3]{1,0:T(1,128)} %param.20) | copy-start | bytes 40
  7.2 53.5 %all-gather.2.cloned.1.call-start = ((), (), s32[]{:S(2)}) async-start(), calls=%async_computation | async-start | bytes 3932160 | tf_op jit(solution)/shard_map/all_gather | solution.py:660
  14.5 45.6 %copy-start.1 = (f32[1,2]{1,0:T(1,128)S(1)}, f32[1,2]{1,0:T(1,128)}, u32[]{:S(2)}) copy-start(f32[1,2]{1,0:T(1,128)} %param.21) | copy-start | bytes 28
Sparse Core Ops, SparseCore 0:
  9.7 42.9 all-gather.1

commit v9 on v8

--- a/solution.py
+++ b/solution.py
@@ -403,6 +403,8 @@
         @pl.when(step > 0)
         def _():
             rs.send(lax.rem(me + step, n))
+    elif kind == "wave2":
+        i = lax.rem(step + n - 1, n)
     else:
         i = step
 
@@ -475,7 +477,7 @@
     if kind == "wave2":
         sender = HaloSender(ref, n, tb)
 
-        @pl.when(i == 0)
+        @pl.when(step == 0)
         def _():
             sender.begin()
 
@@ -496,7 +498,7 @@
         lax.fori_loop(0, tb, inject, 0)
         sender.send_block(i)
 
-        @pl.when(i == n - 1)
+        @pl.when(step == n - 1)
         def _():
             sender.finish()
 
@@ -521,6 +523,12 @@
             return lambda i: fn(lax.rem(lax.axis_index("shot") + 1 + i, nblk))
 
         fixed = at
+    elif kind == "wave2":
+        def at(fn):
+            return lambda i: fn(lax.rem(i + nblk - 1, nblk))
+
+        def fixed(fn):
+            return fn
     else:
         def at(fn):
             return fn

time: 200 us -> 198 us (0.990)
  Pallas kernels: 170 us -> 167 us
    pallas_call x4, Pallas kernels: 125 us -> 122 us  [leap(): pl.pallas_call(functools.partial(step_kernel, kind, tuple(names), nf_ex),...]
  transfers between devices with their start and end apart: 1 -> 1, of which waited for: 0 -> 0; matrix products, arithmetic and copies ran while one was open for 4% -> 4% of each run, Pallas kernels for 22% -> 23%
where the time goes in v9:
time: 198 us; the launch traced here: 196 us
  Pallas kernels  167 us (84%)
  between operations  15.4 us (8%)
  local copies, waits for them, and re-layouts  9.99 us (5%)
  other arithmetic  3.68 us (2%)
    pallas_call x4, Pallas kernels, leap(): pl.pallas_call(functools.partial(step_kernel, kind, tuple(names), nf_ex),...  122 us
    pallas_call x1, Pallas kernels, exchange(): pl.pallas_call(functools.partial(exchange_kernel, nf), in_specs=[any_spec...  44.3 us
    unnamed x6, local copies, waits for them, and re-layouts  4.15 us
  transfers between devices with their start and end apart: 1, of which 0 were waited for; matrix products, arithmetic and copies ran while one was open for 4% of the time, Pallas kernels for 23%

profile of v9, /device:TPU:1, one launch (start us, length us, event | category | flops | bytes accessed | tf_op | source)
XLA Modules:
  0.0 196.3 jit_solution(6888222561526538564)
XLA Ops:
  7.2 0.0 copy-start
  7.2 0.0 all-gather.2.cloned.1.call-start
  7.2 0.7 all-gather.2.cloned.1.call-update
  7.9 0.7 slice_bitcast_fusion
  8.7 0.4 copy.21
  9.1 2.1 %copy.18.refs_9_ = s32[32,64,1]{2,1,0:T(8,128)} copy(s32[32,64,1]{1,0,2:T(8,128)} %bitcast.28) | data formatting | bytes 16384 | tf_op jit(solution)/shard_map/broadcast_in_dim;squeeze | solution.py:674
  11.2 1.4 copy.20.refs_13_
  12.6 0.0 copy-done
  12.6 0.6 fusion.1
  14.5 0.0 copy-start.1
  14.5 44.3 %halo_exchange_1.1 = (f32[4,64,384]{2,1,0:T(8,128)}, f32[4,64,384]{2,1,0:T(8,128)}, f32[32,8,384]{2,1,0:T(8,128)}, f32[32,8,384]{2,1,0:T(8,128)}, f32[4,64,384]{...) custom-call(f32[32,64,384]{2,1,0:T(8,128)} %bitcast.16, f32[32,64,384]{2,1,0:T(8,128)} %bitcast.21), custom_call_target="tpu_custom_call" | custom-call | tf_op jit(solution)/shard_map/halo_exchange_1/pallas_call | solution.py:189
  58.7 1.3 pad_add_fusion.refs_10_
  60.0 0.0 copy-done.1
  60.0 0.6 fusion
  60.6 0.0 all-gather.2.cloned.1.call-done.refs_8_
  60.6 16.2 %leap_wave1.1 = (f32[32,64,384]{2,1,0:T(8,128)}, f32[32,64,384]{2,1,0:T(8,128)}, f32[32,64,1]{2,1,0:T(8,128)}) custom-call(f32[32,64,384]{2,1,0:T(8,128)} %bitcast.17, f32[32,64,384]{2,1,0:T(8,128)} %bitcast.18, f32[32,64,384]{2,1,0:T(8,128)} %bitcast.19, f32[4,64,384]{2,1,0:T(8,128)} %get-tuple-element.24.refs_3_, f32[4,64,384]{2,1,0:T(8,128)} %get-tuple-element.25.refs_4_, ...), custom_call_target="tpu_custom_call" | custom-call | flops 47185920 | bytes 18874368 | tf_op jit(solution)/shard_map/leap_wave1/pallas_call | solution.py:635
  76.8 2.4 %sub.11.refs_10_ = f32[32,64,1]{2,1,0:T(8,128)} subtract(f32[32,64,1]{2,1,0:T(8,128)} %get-tuple-element.43, f32[32,64,1]{2,1,0:T(8,128)S(1)} %copy.21) | non-fusion elementwise | flops 2048 | bytes 24576 | tf_op jit(solution)/shard_map/sub | solution.py:701
  79.2 26.2 %leap_adjbulk.1 = (f32[32,64,384]{2,1,0:T(8,128)}, f32[4,64,384]{2,1,0:T(8,128)}, f32[4,64,384]{2,1,0:T(8,128)}, f32[32,8,384]{2,1,0:T(8,128)}, f32[32,8,384]{2,1,0:T(8,128)}) custom-call(f32[32,64,384]{2,1,0:T(8,128)} %bitcast.22, f32[32,64,384]{2,1,0:T(8,128)} %bitcast.23, f32[32,64,384]{2,1,0:T(8,128)} %bitcast.24, ...), custom_call_target="tpu_custom_call" | custom-call | flops 47185920 | bytes 15728640 | tf_op jit(solution)/shard_map/leap_adjbulk/pallas_call | solution.py:635
  105.4 33.2 %leap_wave2.1 = (f32[32,64,384]{2,1,0:T(8,128)}, f32[32,64,1]{2,1,0:T(8,128)}, f32[32,64,384]{2,1,0:T(8,128)}, f32[32,64,384]{2,1,0:T(8,128)}, f32[4,64,384]{2,1...) custom-call(f32[32,64,384]{2,1,0:T(8,128)} %get-tuple-element.28.refs_9_.refs_0_.refs_1_.refs_2_, ...), custom_call_target="tpu_custom_call" | custom-call | flops 47185920 | bytes 25165824 | tf_op jit(solution)/shard_map/leap_wave2/pallas_call | solution.py:635
  138.5 46.8 %leap_adj2.1 = (f32[8,64,384]{2,1,0:T(8,128)}, f32[8,64,384]{2,1,0:T(8,128)}) custom-call(f32[32,64,384]{2,1,0:T(8,128)} %get-tuple-element.38.refs_0_.refs_1_.refs_2_, f32[32,64,384]{2,1,0:T(8,128)} %get-tuple-element.38.refs_0_.refs_1_.refs_2_, f32[32,64,384]{2,1,0:T(8,128)} %get-tuple-element.38.refs_0_.refs_1_.refs_2_, ...), custom_call_target="tpu_custom_call" | custom-call | flops 47185920 | bytes 18874368 | tf_op jit(solution)/shard_map/leap_adj2/pallas_call | solution.py:635
  185.3 2.1 %copy.25 = f32[8,64,384]{2,1,0:T(8,128)} copy(f32[8,64,384]{2,1,0:T(8,128)} %get-tuple-element.55) | data formatting | bytes 1572864
  187.4 2.1 %copy.26 = f32[8,64,384]{2,1,0:T(8,128)} copy(f32[8,64,384]{2,1,0:T(8,128)} %get-tuple-element.56) | data formatting | bytes 1572864
Async XLA Ops:
  7.2 5.4 %copy-start = (s32[1,3]{1,0:T(1,128)S(1)}, s32[1,3]{1,0:T(1,128)}, u32[]{:S(2)}) copy-start(s32[1,3]{1,0:T(1,128)} %param.20) | copy-start | bytes 40
  7.2 53.5 %all-gather.2.cloned.1.call-start = ((), (), s32[]{:S(2)}) async-start(), calls=%async_computation | async-start | bytes 3932160 | tf_op jit(solution)/shard_map/all_gather | solution.py:668
  14.5 45.6 %copy-start.1 = (f32[1,2]{1,0:T(1,128)S(1)}, f32[1,2]{1,0:T(1,128)}, u32[]{:S(2)}) copy-start(f32[1,2]{1,0:T(1,128)} %param.21) | copy-start | bytes 28
Sparse Core Ops, SparseCore 0:
  9.7 42.9 all-gather.1

commit v10 on v9

--- a/solution.py
+++ b/solution.py
@@ -60,6 +60,9 @@
     xlo = 45
     yhi = 46
     ylo = 47
+    rl_top = 90
+    rl_bot = 91
+    rl_rs = 92
     ex_f = 100
     ex_b = 110
     h_b = 130
@@ -322,46 +325,85 @@
 
     def __init__(self, ref, me, n):
         self.ref, self.me, self.n = ref, me, n
-
-    def copy(self, blk):
-        ref = self.ref
+        self.up, self.down, self.far = lax.rem(me + 1, n), lax.rem(me + n - 1, n), lax.rem(me + 2, n)
+        half = ref[S.slot_out].shape[1] // 2
+        self.top, self.bot = pl.ds(0, half), pl.ds(half, half)
+
+    def remote(self, src, dst, k, recv_sem, peer):
         return pltpu.make_async_remote_copy(
-            src_ref=ref[S.slot_out].at[blk],
-            dst_ref=ref[S.slot_in].at[self.me],
-            send_sem=ref[S.rs_ss].at[blk],
-            recv_sem=ref[S.rs_rs].at[self.me],
-            device_id={"shot": blk},
+            src_ref=src,
+            dst_ref=dst,
+            send_sem=self.ref[S.rs_ss].at[k],
+            recv_sem=recv_sem,
+            device_id={"shot": peer},
             device_id_type=pl.DeviceIdType.MESH,
         )
 
+    def direct(self, blk, k, peer):
+        ref = self.ref
+        return self.remote(ref[S.slot_out].at[blk], ref[S.slot_in].at[self.me], k, ref[S.rs_rs].at[self.me], peer)
+
+    def relay_top(self):
+        ref = self.ref
+        src = ref[S.slot_out].at[self.far, self.top]
+        return self.remote(src, ref[S.rl_top], 2, ref[S.rl_rs].at[0], self.up)
+
+    def relay_bot(self):
+        ref = self.ref
+        src = ref[S.slot_out].at[self.far, self.bot]
+        return self.remote(src, ref[S.rl_bot], 3, ref[S.rl_rs].at[1], self.down)
+
+    def fwd_top(self):
+        ref = self.ref
+        dst = ref[S.slot_in].at[self.down, self.top]
+        return self.remote(ref[S.rl_top], dst, 4, ref[S.rl_rs].at[2], self.up)
+
+    def fwd_bot(self):
+        ref = self.ref
+        dst = ref[S.slot_in].at[self.up, self.bot]
+        return self.remote(ref[S.rl_bot], dst, 5, ref[S.rl_rs].at[3], self.down)
+
     def begin(self):
         barrier = pltpu.get_barrier_semaphore()
-        for d in range(1, self.n):
-            pl.semaphore_signal(
-                barrier, inc=1, device_id={"shot": lax.rem(self.me + d, self.n)}, device_id_type=pl.DeviceIdType.MESH
-            )
-        pl.semaphore_wait(barrier, self.n - 1)
-
-    def send(self, blk):
-        self.copy(blk).start()
+        for peer in (self.up, self.down):
+            pl.semaphore_signal(barrier, inc=1, device_id={"shot": peer}, device_id_type=pl.DeviceIdType.MESH)
+        pl.semaphore_wait(barrier, 2)
+
+    def at_step(self, step):
+        @pl.when(step == 1)
+        def _():
+            self.direct(self.up, 0, self.up).start()
+
+        @pl.when(step == 2)
+        def _():
+            self.relay_top().start()
+            self.relay_bot().start()
+
+        @pl.when(step == 3)
+        def _():
+            self.direct(self.down, 1, self.down).start()
+            self.relay_top().wait_recv()
+            self.relay_bot().wait_recv()
+            self.fwd_top().start()
+            self.fwd_bot().start()
 
     def finish(self):
         ref, me, n = self.ref, self.me, self.n
         own = pltpu.make_async_copy(ref[S.slot_out].at[me], ref[S.slot_in].at[me], ref[S.rs_own])
         own.start()
-        for d in range(1, n):
-            self.copy(lax.rem(me + d, n)).wait_send()
+        self.direct(self.up, 0, self.up).wait_send()
+        self.direct(self.down, 1, self.down).wait_send()
+        self.relay_top().wait_send()
+        self.relay_bot().wait_send()
+        self.fwd_top().wait_send()
+        self.fwd_bot().wait_send()
         own.wait()
-        for d in range(1, n):
-            src = lax.rem(me + d, n)
-            pltpu.make_async_remote_copy(
-                src_ref=ref[S.slot_out].at[src],
-                dst_ref=ref[S.slot_in].at[src],
-                send_sem=ref[S.rs_ss].at[src],
-                recv_sem=ref[S.rs_rs].at[src],
-                device_id={"shot": src},
-                device_id_type=pl.DeviceIdType.MESH,
-            ).wait_recv()
+        for src in (self.down, self.up):
+            self.remote(ref[S.slot_out].at[src], ref[S.slot_in].at[src], 0, ref[S.rs_rs].at[src], src).wait_recv()
+        far_in = ref[S.slot_in].at[self.far, self.top]
+        self.remote(ref[S.rl_top], far_in, 4, ref[S.rl_rs].at[2], self.down).wait_recv()
+        far_in = ref[S.slot_in].at[self.far, self.bot]
+        self.remote(ref[S.rl_bot], far_in, 5, ref[S.rl_rs].at[3], self.up).wait_recv()
 
         slot_in = ref[S.slot_in]
 
@@ -400,9 +442,7 @@
         def _():
             rs.begin()
 
-        @pl.when(step > 0)
-        def _():
-            rs.send(lax.rem(me + step, n))
+        rs.at_step(step)
     elif kind == "wave2":
         i = lax.rem(step + n - 1, n)
     else:
@@ -578,13 +618,16 @@
         scratch.append(pltpu.VMEM((tb * cols, 128), jnp.float32))
         names.append(S.fold)
     if kind == "adj2":
-        names += [S.slot_out, S.slot_in, S.rs_ss, S.rs_rs, S.rs_own]
+        names += [S.slot_out, S.slot_in, S.rs_ss, S.rs_rs, S.rs_own, S.rl_top, S.rl_bot, S.rl_rs]
         scratch += [
             pltpu.VMEM((nblk, tb, cols, depth), jnp.float32),
             pltpu.VMEM((nblk, tb, cols, depth), jnp.float32),
-            pltpu.SemaphoreType.DMA((nblk,)),
+            pltpu.SemaphoreType.DMA((6,)),
             pltpu.SemaphoreType.DMA((nblk,)),
             pltpu.SemaphoreType.DMA(()),
+            pltpu.VMEM((tb // 2, cols, depth), jnp.float32),
+            pltpu.VMEM((tb // 2, cols, depth), jnp.float32),
+            pltpu.SemaphoreType.DMA((4,)),
         ]
         params = pltpu.CompilerParams(
             collective_id=collective_id, has_side_effects=True, vmem_limit_bytes=60 * 1024 * 1024

time: 198 us -> 196 us (0.990)
  no operation moved by 1% of the time
where the time goes in v10:
time: 196 us; the launch traced here: 195 us
  Pallas kernels  166 us (85%)
  between operations  15.4 us (8%)
  local copies, waits for them, and re-layouts  9.99 us (5%)
  other arithmetic  3.68 us (2%)
    pallas_call x4, Pallas kernels, leap(): pl.pallas_call(functools.partial(step_kernel, kind, tuple(names), nf_ex),...  121 us
    pallas_call x1, Pallas kernels, exchange(): pl.pallas_call(functools.partial(exchange_kernel, nf), in_specs=[any_spec...  44.3 us
    unnamed x6, local copies, waits for them, and re-layouts  4.15 us
  transfers between devices with their start and end apart: 1, of which 0 were waited for; matrix products, arithmetic and copies ran while one was open for 4% of the time, Pallas kernels for 23%

profile of v10, /device:TPU:1, one launch (start us, length us, event | category | flops | bytes accessed | tf_op | source)
XLA Modules:
  0.0 195.4 jit_solution(4094417647145844219)
XLA Ops:
  7.2 0.0 copy-start
  7.2 0.0 all-gather.2.cloned.1.call-start
  7.2 0.7 all-gather.2.cloned.1.call-update
  7.9 0.7 slice_bitcast_fusion
  8.7 0.4 copy.21
  9.1 2.1 %copy.18.refs_9_ = s32[32,64,1]{2,1,0:T(8,128)} copy(s32[32,64,1]{1,0,2:T(8,128)} %bitcast.28) | data formatting | bytes 16384 | tf_op jit(solution)/shard_map/broadcast_in_dim;squeeze | solution.py:717
  11.2 1.4 copy.20.refs_13_
  12.6 0.0 copy-done
  12.6 0.6 fusion.1
  14.5 0.0 copy-start.1
  14.5 44.3 %halo_exchange_1.1 = (f32[4,64,384]{2,1,0:T(8,128)}, f32[4,64,384]{2,1,0:T(8,128)}, f32[32,8,384]{2,1,0:T(8,128)}, f32[32,8,384]{2,1,0:T(8,128)}, f32[4,64,384]{...) custom-call(f32[32,64,384]{2,1,0:T(8,128)} %bitcast.16, f32[32,64,384]{2,1,0:T(8,128)} %bitcast.21), custom_call_target="tpu_custom_call" | custom-call | tf_op jit(solution)/shard_map/halo_exchange_1/pallas_call | solution.py:192
  58.7 1.3 pad_add_fusion.refs_10_
  60.0 0.0 copy-done.1
  60.0 0.6 fusion
  60.6 0.0 all-gather.2.cloned.1.call-done.refs_8_
  60.6 16.2 %leap_wave1.1 = (f32[32,64,384]{2,1,0:T(8,128)}, f32[32,64,384]{2,1,0:T(8,128)}, f32[32,64,1]{2,1,0:T(8,128)}) custom-call(f32[32,64,384]{2,1,0:T(8,128)} %bitcast.17, f32[32,64,384]{2,1,0:T(8,128)} %bitcast.18, f32[32,64,384]{2,1,0:T(8,128)} %bitcast.19, f32[4,64,384]{2,1,0:T(8,128)} %get-tuple-element.24.refs_3_, f32[4,64,384]{2,1,0:T(8,128)} %get-tuple-element.25.refs_4_, ...), custom_call_target="tpu_custom_call" | custom-call | flops 47185920 | bytes 18874368 | tf_op jit(solution)/shard_map/leap_wave1/pallas_call | solution.py:678
  76.8 2.4 %sub.11.refs_10_ = f32[32,64,1]{2,1,0:T(8,128)} subtract(f32[32,64,1]{2,1,0:T(8,128)} %get-tuple-element.43, f32[32,64,1]{2,1,0:T(8,128)S(1)} %copy.21) | non-fusion elementwise | flops 2048 | bytes 24576 | tf_op jit(solution)/shard_map/sub | solution.py:744
  79.2 26.2 %leap_adjbulk.1 = (f32[32,64,384]{2,1,0:T(8,128)}, f32[4,64,384]{2,1,0:T(8,128)}, f32[4,64,384]{2,1,0:T(8,128)}, f32[32,8,384]{2,1,0:T(8,128)}, f32[32,8,384]{2,1,0:T(8,128)}) custom-call(f32[32,64,384]{2,1,0:T(8,128)} %bitcast.22, f32[32,64,384]{2,1,0:T(8,128)} %bitcast.23, f32[32,64,384]{2,1,0:T(8,128)} %bitcast.24, ...), custom_call_target="tpu_custom_call" | custom-call | flops 47185920 | bytes 15728640 | tf_op jit(solution)/shard_map/leap_adjbulk/pallas_call | solution.py:678
  105.4 33.2 %leap_wave2.1 = (f32[32,64,384]{2,1,0:T(8,128)}, f32[32,64,1]{2,1,0:T(8,128)}, f32[32,64,384]{2,1,0:T(8,128)}, f32[32,64,384]{2,1,0:T(8,128)}, f32[4,64,384]{2,1...) custom-call(f32[32,64,384]{2,1,0:T(8,128)} %get-tuple-element.28.refs_9_.refs_0_.refs_1_.refs_2_, ...), custom_call_target="tpu_custom_call" | custom-call | flops 47185920 | bytes 25165824 | tf_op jit(solution)/shard_map/leap_wave2/pallas_call | solution.py:678
  138.5 45.8 %leap_adj2.1 = (f32[8,64,384]{2,1,0:T(8,128)}, f32[8,64,384]{2,1,0:T(8,128)}) custom-call(f32[32,64,384]{2,1,0:T(8,128)} %get-tuple-element.38.refs_0_.refs_1_.refs_2_, f32[32,64,384]{2,1,0:T(8,128)} %get-tuple-element.38.refs_0_.refs_1_.refs_2_, f32[32,64,384]{2,1,0:T(8,128)} %get-tuple-element.38.refs_0_.refs_1_.refs_2_, ...), custom_call_target="tpu_custom_call" | custom-call | flops 47185920 | bytes 18874368 | tf_op jit(solution)/shard_map/leap_adj2/pallas_call | solution.py:678
  184.4 2.1 %copy.25 = f32[8,64,384]{2,1,0:T(8,128)} copy(f32[8,64,384]{2,1,0:T(8,128)} %get-tuple-element.55) | data formatting | bytes 1572864
  186.5 2.1 %copy.26 = f32[8,64,384]{2,1,0:T(8,128)} copy(f32[8,64,384]{2,1,0:T(8,128)} %get-tuple-element.56) | data formatting | bytes 1572864
Async XLA Ops:
  7.2 5.4 %copy-start = (s32[1,3]{1,0:T(1,128)S(1)}, s32[1,3]{1,0:T(1,128)}, u32[]{:S(2)}) copy-start(s32[1,3]{1,0:T(1,128)} %param.20) | copy-start | bytes 40
  7.2 53.5 %all-gather.2.cloned.1.call-start = ((), (), s32[]{:S(2)}) async-start(), calls=%async_computation | async-start | bytes 3932160 | tf_op jit(solution)/shard_map/all_gather | solution.py:711
  14.5 45.6 %copy-start.1 = (f32[1,2]{1,0:T(1,128)S(1)}, f32[1,2]{1,0:T(1,128)}, u32[]{:S(2)}) copy-start(f32[1,2]{1,0:T(1,128)} %param.21) | copy-start | bytes 28
Sparse Core Ops, SparseCore 0:
  9.7 42.9 all-gather.1

commit v11 on v10

--- a/solution.py
+++ b/solution.py
@@ -66,6 +66,7 @@
     ex_f = 100
     ex_b = 110
     h_b = 130
+    pick = 140
 
 
 ROWS_PER_STEP = 8
@@ -507,7 +508,8 @@
                 ref[S.o_f][r, ys, :] = out
             else:
                 at_rec = z_index == ref[S.rec][r, ys, :]
-                out = out + jnp.where(at_rec, ref[S.mis][r, ys, :], 0.0)
+                misfit = ref[S.pick][r, ys, :] - ref[S.obs][r, ys, :]
+                out = out + jnp.where(at_rec, misfit, 0.0)
                 ref[S.slot_out][i, r, ys, :] = ref[S.part][r, ys, :] + out * ref[S.dw][r, ys, :]
         return carry
 
@@ -585,7 +587,7 @@
     any_spec = pl.BlockSpec(memory_space=pl.ANY)
     field = jax.ShapeDtypeStruct((rows, cols, depth), jnp.float32)
     picked = jax.ShapeDtypeStruct((rows, cols, 1), jnp.float32)
-    spec_of = {S.src: smem, S.amp: smem, S.rec: col1, S.mis: col1, S.obs: col1, S.vslab: slab, S.mom: slab, S.mass: slab}
+    spec_of = {S.src: smem, S.amp: smem, S.rec: col1, S.mis: col1, S.obs: col1, S.pick: col1, S.vslab: slab, S.mom: slab, S.mass: slab}
 
     names = [S.f, S.flo, S.fhi, S.xlo, S.xhi, S.ylo, S.yhi, S.prev, S.vel]
     in_specs = [block, lo_spec, hi_spec, whole4, whole4, yspec, yspec, block, block]
@@ -741,7 +743,6 @@
         {S.rec: rec, S.src: src, S.amp: amp[1:2], S.a2raw: adj_bulk, S.obs: observed[0, 1][:, :, None]},
         collective_id=3,
     )
-    misfit_early = pick_adv - observed[0, 0][:, :, None]
     v_new, p_half = leap(
         "adj2",
         adj_two,
@@ -750,7 +751,8 @@
         full_velocity,
         {
             S.rec: rec,
-            S.mis: misfit_early,
+            S.pick: pick_adv,
+            S.obs: observed[0, 0][:, :, None],
             S.dw: dw1,
             S.part: part,
             S.vslab: velocity,

time: 196 us -> 195 us (level)
  other arithmetic: 3.68 us -> 1.24 us
    sub x1 -> x0, other arithmetic: 2.37 us -> none  [on_device(): misfit_early = pick_adv - observed[0, 0][:, :, None]]
where the time goes in v11:
time: 195 us; the launch traced here: 194 us
  Pallas kernels  166 us (85%)
  between operations  15.4 us (8%)
  local copies, waits for them, and re-layouts  11 us (6%)
    pallas_call x4, Pallas kernels, leap(): pl.pallas_call(functools.partial(step_kernel, kind, tuple(names), nf_ex),...  121 us
    pallas_call x1, Pallas kernels, exchange(): pl.pallas_call(functools.partial(exchange_kernel, nf), in_specs=[any_spec...  44.1 us
    unnamed x6, local copies, waits for them, and re-layouts  4.14 us
  transfers between devices with their start and end apart: 1, of which 0 were waited for; matrix products, arithmetic and copies ran while one was open for 4% of the time, Pallas kernels for 23%

profile of v11, /device:TPU:1, one launch (start us, length us, event | category | flops | bytes accessed | tf_op | source)
XLA Modules:
  0.0 193.9 jit_solution(12070939810512555488)
XLA Ops:
  7.2 0.0 all-gather.2.cloned.1.call-start
  7.2 0.7 all-gather.2.cloned.1.call-update
  7.9 2.1 %copy.18.refs_9_ = s32[32,64,1]{2,1,0:T(8,128)} copy(s32[32,64,1]{1,0,2:T(8,128)} %bitcast.28) | data formatting | bytes 16384 | tf_op jit(solution)/shard_map/broadcast_in_dim;squeeze | solution.py:719
  10.0 0.7 slice_bitcast_fusion
  10.8 1.4 copy.20.refs_13_
  12.2 1.4 copy.22.refs_11_
  13.6 0.0 copy-start
  13.6 0.0 copy-start.1
  13.6 44.1 %halo_exchange_1.1 = (f32[4,64,384]{2,1,0:T(8,128)}, f32[4,64,384]{2,1,0:T(8,128)}, f32[32,8,384]{2,1,0:T(8,128)}, f32[32,8,384]{2,1,0:T(8,128)}, f32[4,64,384]{...) custom-call(f32[32,64,384]{2,1,0:T(8,128)} %bitcast.21, f32[32,64,384]{2,1,0:T(8,128)} %bitcast.16), custom_call_target="tpu_custom_call" | custom-call | tf_op jit(solution)/shard_map/halo_exchange_1/pallas_call | solution.py:193
  57.7 0.0 copy-done
  57.7 0.6 fusion.1
  59.6 1.2 pad_add_fusion.refs_10_
  60.9 0.0 copy-done.1
  60.9 0.6 fusion
  61.5 0.0 all-gather.2.cloned.1.call-done.refs_8_
  61.5 16.2 %leap_wave1.1 = (f32[32,64,384]{2,1,0:T(8,128)}, f32[32,64,384]{2,1,0:T(8,128)}, f32[32,64,1]{2,1,0:T(8,128)}) custom-call(f32[32,64,384]{2,1,0:T(8,128)} %bitcast.22, f32[32,64,384]{2,1,0:T(8,128)} %bitcast.23, f32[32,64,384]{2,1,0:T(8,128)} %bitcast.24, f32[4,64,384]{2,1,0:T(8,128)} %get-tuple-element.24.refs_3_, f32[4,64,384]{2,1,0:T(8,128)} %get-tuple-element.25.refs_4_, ...), custom_call_target="tpu_custom_call" | custom-call | flops 47185920 | bytes 18874368 | tf_op jit(solution)/shard_map/leap_wave1/pallas_call | solution.py:680
  77.7 26.3 %leap_adjbulk.1 = (f32[32,64,384]{2,1,0:T(8,128)}, f32[4,64,384]{2,1,0:T(8,128)}, f32[4,64,384]{2,1,0:T(8,128)}, f32[32,8,384]{2,1,0:T(8,128)}, f32[32,8,384]{2,1,0:T(8,128)}) custom-call(f32[32,64,384]{2,1,0:T(8,128)} %bitcast.17, f32[32,64,384]{2,1,0:T(8,128)} %bitcast.18, f32[32,64,384]{2,1,0:T(8,128)} %bitcast.19, ...), custom_call_target="tpu_custom_call" | custom-call | flops 47185920 | bytes 15728640 | tf_op jit(solution)/shard_map/leap_adjbulk/pallas_call | solution.py:680
  104.0 33.1 %leap_wave2.1 = (f32[32,64,384]{2,1,0:T(8,128)}, f32[32,64,1]{2,1,0:T(8,128)}, f32[32,64,384]{2,1,0:T(8,128)}, f32[32,64,384]{2,1,0:T(8,128)}, f32[4,64,384]{2,1...) custom-call(f32[32,64,384]{2,1,0:T(8,128)} %get-tuple-element.28.refs_9_.refs_0_.refs_1_.refs_2_, ...), custom_call_target="tpu_custom_call" | custom-call | flops 47185920 | bytes 25165824 | tf_op jit(solution)/shard_map/leap_wave2/pallas_call | solution.py:680
  137.1 45.8 %leap_adj2.1 = (f32[8,64,384]{2,1,0:T(8,128)}, f32[8,64,384]{2,1,0:T(8,128)}) custom-call(f32[32,64,384]{2,1,0:T(8,128)} %get-tuple-element.38.refs_0_.refs_1_.refs_2_, f32[32,64,384]{2,1,0:T(8,128)} %get-tuple-element.38.refs_0_.refs_1_.refs_2_, f32[32,64,384]{2,1,0:T(8,128)} %get-tuple-element.38.refs_0_.refs_1_.refs_2_, ...), custom_call_target="tpu_custom_call" | custom-call | flops 47185920 | bytes 18874368 | tf_op jit(solution)/shard_map/leap_adj2/pallas_call | solution.py:680
  182.9 2.1 %copy.25 = f32[8,64,384]{2,1,0:T(8,128)} copy(f32[8,64,384]{2,1,0:T(8,128)} %get-tuple-element.55) | data formatting | bytes 1572864
  185.0 2.1 %copy.26 = f32[8,64,384]{2,1,0:T(8,128)} copy(f32[8,64,384]{2,1,0:T(8,128)} %get-tuple-element.56) | data formatting | bytes 1572864
Async XLA Ops:
  7.2 54.3 %all-gather.2.cloned.1.call-start = ((), (), s32[]{:S(2)}) async-start(), calls=%async_computation | async-start | bytes 3932160 | tf_op jit(solution)/shard_map/all_gather | solution.py:713
  13.6 44.2 %copy-start = (s32[1,3]{1,0:T(1,128)S(1)}, s32[1,3]{1,0:T(1,128)}, u32[]{:S(2)}) copy-start(s32[1,3]{1,0:T(1,128)} %param.20) | copy-start | bytes 40
  13.6 47.3 %copy-start.1 = (f32[1,2]{1,0:T(1,128)S(1)}, f32[1,2]{1,0:T(1,128)}, u32[]{:S(2)}) copy-start(f32[1,2]{1,0:T(1,128)} %param.21) | copy-start | bytes 28
Sparse Core Ops, SparseCore 0:
  9.7 42.9 all-gather.1

commit v12 on v11

--- a/solution.py
+++ b/solution.py
@@ -412,11 +412,7 @@
             summed = slot_in[0, r]
             for s_ in range(1, n):
                 summed = summed + slot_in[s_, r]
-            v = ref[S.vslab][r]
-            gradient = 2.0 / v * summed
-            p_half = ref[S.mom][r] - 0.5 * leap_step * gradient
-            ref[S.o_p][r] = p_half
-            ref[S.o_v][r] = v + leap_step * p_half / ref[S.mass][r]
+            ref[S.o_v][r] = summed
             return carry
 
         lax.fori_loop(0, slot_in.shape[1], row, 0)
@@ -606,10 +602,7 @@
         "wave1": [(S.o_f, field, block), (S.o_dw, field, block), (S.o_pick, picked, col1)],
         "wave2": [(S.o_dw, field, block), (S.o_pick, picked, col1), (S.o_a2, field, block), (S.o_part, field, block)],
         "adjbulk": [(S.o_f, field, block)],
-        "adj2": [
-            (S.o_v, jax.ShapeDtypeStruct((tb, cols, depth), jnp.float32), slab),
-            (S.o_p, jax.ShapeDtypeStruct((tb, cols, depth), jnp.float32), slab),
-        ],
+        "adj2": [(S.o_v, jax.ShapeDtypeStruct((tb, cols, depth), jnp.float32), slab)],
     }[kind]
     names += [o[0] for o in outs]
     out_shape = [o[1] for o in outs]
@@ -743,7 +736,7 @@
         {S.rec: rec, S.src: src, S.amp: amp[1:2], S.a2raw: adj_bulk, S.obs: observed[0, 1][:, :, None]},
         collective_id=3,
     )
-    v_new, p_half = leap(
+    (summed,) = leap(
         "adj2",
         adj_two,
         *adj_two_h,
@@ -755,12 +748,12 @@
             S.obs: observed[0, 0][:, :, None],
             S.dw: dw1,
             S.part: part,
-            S.vslab: velocity,
-            S.mom: momentum,
-            S.mass: mass_diag,
         },
         collective_id=0,
     )
+    gradient = 2.0 / velocity * summed
+    p_half = momentum - 0.5 * leap_step * gradient
+    v_new = velocity + leap_step * p_half / mass_diag
     return (v_new, p_half)
 
 

time: 195 us -> 193 us (0.990)
  local copies, waits for them, and re-layouts: 11 us -> 6.97 us
  other arithmetic: 1.24 us -> 3.87 us
    unnamed x6 -> x10, local copies, waits for them, and re-layouts: 4.14 us -> 0.03 us
    add x0 -> x1, other arithmetic: none -> 2.55 us  [on_device(): v_new = velocity + leap_step * p_half / mass_diag]
where the time goes in v12:
time: 193 us; the launch traced here: 192 us
  Pallas kernels  165 us (85%)
  between operations  15.4 us (8%)
  local copies, waits for them, and re-layouts  6.97 us (4%)
  other arithmetic  3.87 us (2%)
    pallas_call x4, Pallas kernels, leap(): pl.pallas_call(functools.partial(step_kernel, kind, tuple(names), nf_ex),...  120 us
    pallas_call x1, Pallas kernels, exchange(): pl.pallas_call(functools.partial(exchange_kernel, nf), in_specs=[any_spec...  44.1 us
  transfers between devices with their start and end apart: 1, of which 0 were waited for; matrix products, arithmetic and copies ran while one was open for 4% of the time, Pallas kernels for 23%

profile of v12, /device:TPU:1, one launch (start us, length us, event | category | flops | bytes accessed | tf_op | source)
XLA Modules:
  0.0 191.5 jit_solution(5186939391435706687)
XLA Ops:
  7.2 0.0 all-gather.2.cloned.1.call-start
  7.2 0.7 all-gather.2.cloned.1.call-update
  7.9 2.1 %copy.18.refs_9_ = s32[32,64,1]{2,1,0:T(8,128)} copy(s32[32,64,1]{1,0,2:T(8,128)} %bitcast.28) | data formatting | bytes 16384 | tf_op jit(solution)/shard_map/broadcast_in_dim;squeeze | solution.py:712
  10.0 0.7 slice_bitcast_fusion
  10.8 1.4 copy.20.refs_13_
  12.2 1.4 copy.22.refs_11_
  13.6 0.0 copy-start.3
  13.6 0.0 copy-start.4
  13.6 44.1 %halo_exchange_1.1 = (f32[4,64,384]{2,1,0:T(8,128)}, f32[4,64,384]{2,1,0:T(8,128)}, f32[32,8,384]{2,1,0:T(8,128)}, f32[32,8,384]{2,1,0:T(8,128)}, f32[4,64,384]{...) custom-call(f32[32,64,384]{2,1,0:T(8,128)} %bitcast.16, f32[32,64,384]{2,1,0:T(8,128)} %bitcast.21), custom_call_target="tpu_custom_call" | custom-call | tf_op jit(solution)/shard_map/halo_exchange_1/pallas_call | solution.py:193
  57.8 0.0 copy-done.3
  57.8 0.6 fusion.1
  59.7 1.3 pad_add_fusion.refs_10_
  61.0 0.0 copy-done.4
  61.0 0.6 fusion
  61.6 0.0 all-gather.2.cloned.1.call-done.refs_8_
  61.6 16.2 %leap_wave1.1 = (f32[32,64,384]{2,1,0:T(8,128)}, f32[32,64,384]{2,1,0:T(8,128)}, f32[32,64,1]{2,1,0:T(8,128)}) custom-call(f32[32,64,384]{2,1,0:T(8,128)} %bitcast.17, f32[32,64,384]{2,1,0:T(8,128)} %bitcast.18, f32[32,64,384]{2,1,0:T(8,128)} %bitcast.19, f32[4,64,384]{2,1,0:T(8,128)} %get-tuple-element.24.refs_3_, f32[4,64,384]{2,1,0:T(8,128)} %get-tuple-element.25.refs_4_, ...), custom_call_target="tpu_custom_call" | custom-call | flops 47185920 | bytes 18874368 | tf_op jit(solution)/shard_map/leap_wave1/pallas_call | solution.py:673
  77.8 26.3 %leap_adjbulk.1 = (f32[32,64,384]{2,1,0:T(8,128)}, f32[4,64,384]{2,1,0:T(8,128)}, f32[4,64,384]{2,1,0:T(8,128)}, f32[32,8,384]{2,1,0:T(8,128)}, f32[32,8,384]{2,1,0:T(8,128)}) custom-call(f32[32,64,384]{2,1,0:T(8,128)} %bitcast.22, f32[32,64,384]{2,1,0:T(8,128)} %bitcast.23, f32[32,64,384]{2,1,0:T(8,128)} %bitcast.24, ...), custom_call_target="tpu_custom_call" | custom-call | flops 47185920 | bytes 15728640 | tf_op jit(solution)/shard_map/leap_adjbulk/pallas_call | solution.py:673
  104.1 33.2 %leap_wave2.1 = (f32[32,64,384]{2,1,0:T(8,128)}, f32[32,64,1]{2,1,0:T(8,128)}, f32[32,64,384]{2,1,0:T(8,128)}, f32[32,64,384]{2,1,0:T(8,128)}, f32[4,64,384]{2,1...) custom-call(f32[32,64,384]{2,1,0:T(8,128)} %get-tuple-element.28.refs_9_.refs_0_.refs_1_.refs_2_, ...), custom_call_target="tpu_custom_call" | custom-call | flops 47185920 | bytes 25165824 | tf_op jit(solution)/shard_map/leap_wave2/pallas_call | solution.py:673
  137.3 0.0 copy-start
  137.3 0.0 copy-start.1
  137.3 0.0 copy-start.2
  137.3 44.7 %leap_adj2.1 = f32[8,64,384]{2,1,0:T(8,128)} custom-call(f32[32,64,384]{2,1,0:T(8,128)} %get-tuple-element.38.refs_0_.refs_1_.refs_2_, f32[32,64,384]{2,1,0:T(8,128)} %get-tuple-element.38.refs_0_.refs_1_.refs_2_, f32[32,64,384]{2,1,0:T(8,128)} %get-tuple-element.38.refs_0_.refs_1_.refs_2_, f32[4,64,384]{2,1,0:T(8,128)} %get-tuple-element.39.refs_3_, ...), custom_call_target="tpu_custom_call" | custom-call | flops 47185920 | bytes 18874368 | tf_op jit(solution)/shard_map/leap_adj2/pallas_call | solution.py:673
  182.1 0.0 copy-done
  182.1 0.0 copy-done.1
  182.1 0.0 copy-done.2
  182.1 2.6 %divide_add_fusion = (f32[8,64,384]{2,1,0:T(8,128)}, f32[8,64,384]{2,1,0:T(8,128)}) fusion(f32[8,64,384]{2,1,0:T(8,128)S(1)} %copy-done, f32[8,64,384]{2,1,0:T(8,128)S(1)} %copy-done.1, f32[8,64,384]{2,1,0:T(8,128)S(1)} %copy-done.2, f32[8,64,384]{2,1,0:T(8,128)} %leap_adj2.1), kind=kLoop, calls=%fused_computation | loop fusion | flops 1376256 | bytes 4718592 | tf_op jit(solution)/shard_map/add | solution.py:756
Async XLA Ops:
  7.2 54.4 %all-gather.2.cloned.1.call-start = ((), (), s32[]{:S(2)}) async-start(), calls=%async_computation | async-start | bytes 3932160 | tf_op jit(solution)/shard_map/all_gather | solution.py:706
  13.6 44.2 %copy-start.3 = (s32[1,3]{1,0:T(1,128)S(1)}, s32[1,3]{1,0:T(1,128)}, u32[]{:S(2)}) copy-start(s32[1,3]{1,0:T(1,128)} %param.20) | copy-start | bytes 40
  13.6 47.4 %copy-start.4 = (f32[1,2]{1,0:T(1,128)S(1)}, f32[1,2]{1,0:T(1,128)}, u32[]{:S(2)}) copy-start(f32[1,2]{1,0:T(1,128)} %param.21) | copy-start | bytes 28
  137.3 44.8 %copy-start = (f32[8,64,384]{2,1,0:T(8,128)S(1)}, f32[8,64,384]{2,1,0:T(8,128)}, u32[]{:S(2)}) copy-start(f32[8,64,384]{2,1,0:T(8,128)} %param.11) | copy-start | bytes 2359300
  137.3 44.8 %copy-start.1 = (f32[8,64,384]{2,1,0:T(8,128)S(1)}, f32[8,64,384]{2,1,0:T(8,128)}, u32[]{:S(2)}) copy-start(f32[8,64,384]{2,1,0:T(8,128)} %param.13) | copy-start | bytes 2359300
  137.3 44.8 %copy-start.2 = (f32[8,64,384]{2,1,0:T(8,128)S(1)}, f32[8,64,384]{2,1,0:T(8,128)}, u32[]{:S(2)}) copy-start(f32[8,64,384]{2,1,0:T(8,128)} %param.12) | copy-start | bytes 2359300
Sparse Core Ops, SparseCore 0:
  9.7 42.9 all-gather.1

commit v13 on v12

--- a/solution.py
+++ b/solution.py
@@ -463,10 +463,10 @@
     wave = kind in ("wave1", "wave2")
     if wave:
         src_ref = ref[S.src]
-        src_x = src_ref[0] - i * tb
-        src_y = src_ref[1]
+        src_x = src_ref[0] - lax.axis_index("row") * (tb * n) - i * tb
+        src_y = src_ref[1] - lax.axis_index("col") * cols
         src_z = src_ref[2]
-        amp = ref[S.amp][0]
+        amp = ref[S.amp][0 if kind == "wave1" else 1]
 
     def row(r, carry):
         for y0 in range(0, cols, Y_CHUNK):
@@ -711,18 +711,12 @@
     adj_now = adj_cur[0]
     rec = rec_depth[0][:, :, None]
     cell = src_cell[0]
-    src = jnp.stack(
-        [
-            cell[0] - lax.axis_index("row") * row_count,
-            cell[1] - lax.axis_index("col") * col_count,
-            cell[2],
-        ]
-    ).astype(jnp.int32)
+    src = src_cell[0]
     amp = wavelet[0]
 
     wave_h, adj_h = exchange([present, adj_now], 1)
     advanced, dw1, pick_adv = leap(
-        "wave1", present, *wave_h, oldest, full_velocity, {S.rec: rec, S.src: src, S.amp: amp[0:1]}
+        "wave1", present, *wave_h, oldest, full_velocity, {S.rec: rec, S.src: src, S.amp: amp}
     )
     (adj_bulk,), (adv_h,) = leap(
         "adjbulk", adj_now, *adj_h, adj_later, full_velocity, {}, exchanged=[advanced], collective_id=2
@@ -733,7 +727,7 @@
         *adv_h,
         present,
         full_velocity,
-        {S.rec: rec, S.src: src, S.amp: amp[1:2], S.a2raw: adj_bulk, S.obs: observed[0, 1][:, :, None]},
+        {S.rec: rec, S.src: src, S.amp: amp, S.a2raw: adj_bulk, S.obs: observed[0, 1][:, :, None]},
         collective_id=3,
     )
     (summed,) = leap(

time: 193 us -> 187 us (0.969)
  Pallas kernels: 165 us -> 163 us
  transfers between devices with their start and end apart: 1 -> 1, of which waited for: 0 -> 0; matrix products, arithmetic and copies ran while one was open for 4% -> 3% of each run, Pallas kernels for 23% -> 24%
where the time goes in v13:
time: 187 us; the launch traced here: 186 us
  Pallas kernels  163 us (87%)
  between operations  14.1 us (8%)
  local copies, waits for them, and re-layouts  5.77 us (3%)
  other arithmetic  2.55 us (1%)
    pallas_call x4, Pallas kernels, leap(): pl.pallas_call(functools.partial(step_kernel, kind, tuple(names), nf_ex),...  119 us
    pallas_call x1, Pallas kernels, exchange(): pl.pallas_call(functools.partial(exchange_kernel, nf), in_specs=[any_spec...  44.1 us
  transfers between devices with their start and end apart: 1, of which 0 were waited for; matrix products, arithmetic and copies ran while one was open for 3% of the time, Pallas kernels for 24%

profile of v13, /device:TPU:1, one launch (start us, length us, event | category | flops | bytes accessed | tf_op | source)
XLA Modules:
  0.0 186.0 jit_solution(11317843381569269244)
XLA Ops:
  7.2 0.0 all-gather.2.cloned.1.call-start
  7.2 0.7 all-gather.2.cloned.1.call-update
  7.9 2.1 %copy.18.refs_9_ = s32[32,64,1]{2,1,0:T(8,128)} copy(s32[32,64,1]{1,0,2:T(8,128)} %bitcast.23) | data formatting | bytes 16384 | tf_op jit(solution)/shard_map/broadcast_in_dim;squeeze | solution.py:712
  10.0 0.7 slice_bitcast_fusion
  10.8 1.5 copy.20.refs_13_
  12.2 1.4 copy.22.refs_11_
  13.6 44.1 %halo_exchange_1.1 = (f32[4,64,384]{2,1,0:T(8,128)}, f32[4,64,384]{2,1,0:T(8,128)}, f32[32,8,384]{2,1,0:T(8,128)}, f32[32,8,384]{2,1,0:T(8,128)}, f32[4,64,384]{...) custom-call(f32[32,64,384]{2,1,0:T(8,128)} %bitcast.11, f32[32,64,384]{2,1,0:T(8,128)} %bitcast.16), custom_call_target="tpu_custom_call" | custom-call | tf_op jit(solution)/shard_map/halo_exchange_1/pallas_call | solution.py:193
  57.8 0.0 all-gather.2.cloned.1.call-done.refs_8_
  57.8 15.4 %leap_wave1.1 = (f32[32,64,384]{2,1,0:T(8,128)}, f32[32,64,384]{2,1,0:T(8,128)}, f32[32,64,1]{2,1,0:T(8,128)}) custom-call(f32[32,64,384]{2,1,0:T(8,128)} %bitcast.12, f32[32,64,384]{2,1,0:T(8,128)} %bitcast.13, f32[32,64,384]{2,1,0:T(8,128)} %bitcast.14, f32[4,64,384]{2,1,0:T(8,128)} %get-tuple-element.24.refs_3_, f32[4,64,384]{2,1,0:T(8,128)} %get-tuple-element.25.refs_4_, ...), custom_call_target="tpu_custom_call" | custom-call | flops 47185920 | bytes 18874368 | tf_op jit(solution)/shard_map/leap_wave1/pallas_call | solution.py:673
  73.2 26.3 %leap_adjbulk.1 = (f32[32,64,384]{2,1,0:T(8,128)}, f32[4,64,384]{2,1,0:T(8,128)}, f32[4,64,384]{2,1,0:T(8,128)}, f32[32,8,384]{2,1,0:T(8,128)}, f32[32,8,384]{2,1,0:T(8,128)}) custom-call(f32[32,64,384]{2,1,0:T(8,128)} %bitcast.17, f32[32,64,384]{2,1,0:T(8,128)} %bitcast.18, f32[32,64,384]{2,1,0:T(8,128)} %bitcast.19, ...), custom_call_target="tpu_custom_call" | custom-call | flops 47185920 | bytes 15728640 | tf_op jit(solution)/shard_map/leap_adjbulk/pallas_call | solution.py:673
  99.5 32.3 %leap_wave2.1 = (f32[32,64,384]{2,1,0:T(8,128)}, f32[32,64,1]{2,1,0:T(8,128)}, f32[32,64,384]{2,1,0:T(8,128)}, f32[32,64,384]{2,1,0:T(8,128)}, f32[4,64,384]{2,1...) custom-call(f32[32,64,384]{2,1,0:T(8,128)} %get-tuple-element.28.refs_9_.refs_0_.refs_1_.refs_2_, ...), custom_call_target="tpu_custom_call" | custom-call | flops 47185920 | bytes 25165824 | tf_op jit(solution)/shard_map/leap_wave2/pallas_call | solution.py:673
  131.8 0.0 copy-start
  131.8 0.0 copy-start.1
  131.8 0.0 copy-start.2
  131.8 44.7 %leap_adj2.1 = f32[8,64,384]{2,1,0:T(8,128)} custom-call(f32[32,64,384]{2,1,0:T(8,128)} %get-tuple-element.38.refs_0_.refs_1_.refs_2_, f32[32,64,384]{2,1,0:T(8,128)} %get-tuple-element.38.refs_0_.refs_1_.refs_2_, f32[32,64,384]{2,1,0:T(8,128)} %get-tuple-element.38.refs_0_.refs_1_.refs_2_, f32[4,64,384]{2,1,0:T(8,128)} %get-tuple-element.39.refs_3_, ...), custom_call_target="tpu_custom_call" | custom-call | flops 47185920 | bytes 18874368 | tf_op jit(solution)/shard_map/leap_adj2/pallas_call | solution.py:673
  176.6 0.0 copy-done
  176.6 0.0 copy-done.1
  176.6 0.0 copy-done.2
  176.6 2.6 %divide_add_fusion = (f32[8,64,384]{2,1,0:T(8,128)}, f32[8,64,384]{2,1,0:T(8,128)}) fusion(f32[8,64,384]{2,1,0:T(8,128)S(1)} %copy-done, f32[8,64,384]{2,1,0:T(8,128)S(1)} %copy-done.1, f32[8,64,384]{2,1,0:T(8,128)S(1)} %copy-done.2, f32[8,64,384]{2,1,0:T(8,128)} %leap_adj2.1), kind=kLoop, calls=%fused_computation | loop fusion | flops 1376256 | bytes 4718592 | tf_op jit(solution)/shard_map/add | solution.py:750
Async XLA Ops:
  7.2 50.7 %all-gather.2.cloned.1.call-start = ((), (), s32[]{:S(2)}) async-start(), calls=%async_computation | async-start | bytes 3932160 | tf_op jit(solution)/shard_map/all_gather | solution.py:706
  131.8 44.8 %copy-start = (f32[8,64,384]{2,1,0:T(8,128)S(1)}, f32[8,64,384]{2,1,0:T(8,128)}, u32[]{:S(2)}) copy-start(f32[8,64,384]{2,1,0:T(8,128)} %param.11) | copy-start | bytes 2359300
  131.8 44.8 %copy-start.1 = (f32[8,64,384]{2,1,0:T(8,128)S(1)}, f32[8,64,384]{2,1,0:T(8,128)}, u32[]{:S(2)}) copy-start(f32[8,64,384]{2,1,0:T(8,128)} %param.13) | copy-start | bytes 2359300
  131.8 44.8 %copy-start.2 = (f32[8,64,384]{2,1,0:T(8,128)S(1)}, f32[8,64,384]{2,1,0:T(8,128)}, u32[]{:S(2)}) copy-start(f32[8,64,384]{2,1,0:T(8,128)} %param.12) | copy-start | bytes 2359300
Sparse Core Ops, SparseCore 0:
  9.7 42.9 all-gather.1

commit v14 on v13

--- a/solution.py
+++ b/solution.py
@@ -113,7 +113,7 @@
             device_id_type=pl.DeviceIdType.MESH,
         )
 
-    def start(self):
+    def start(self, extra=0):
         has, row, nrow, col, ncol = self.has, self.row, self.nrow, self.col, self.ncol
         barrier = pltpu.get_barrier_semaphore()
         for d in range(4):
@@ -122,7 +122,7 @@
                 pl.semaphore_signal(barrier, inc=1, device_id=self.peer[d], device_id_type=pl.DeviceIdType.MESH)
 
         count = (1 - row // (nrow - 1)) + (row + nrow - 1) // nrow + (1 - col // (ncol - 1)) + (col + ncol - 1) // ncol
-        pl.semaphore_wait(barrier, count)
+        pl.semaphore_wait(barrier, count + extra)
 
         for j in range(len(self.fields)):
             for d in range(4):
@@ -179,27 +179,80 @@
     return shapes, scratch
 
 
-def exchange_kernel(nf, *refs):
-    ex = Exchange(refs[:nf], refs[nf : 5 * nf], *refs[5 * nf :])
-    ex.start()
+def exchange_kernel(nf, gather, *refs):
+    if not gather:
+        ex = Exchange(refs[:nf], refs[nf : 5 * nf], *refs[5 * nf :])
+        ex.start()
+        ex.finish()
+        return
+    vel = refs[nf]
+    bufs = refs[nf + 1 : 5 * nf + 1]
+    full = refs[5 * nf + 1]
+    ag_ss, ag_rs, ag_own = refs[-3:]
+    ex = Exchange(refs[:nf], bufs, *refs[5 * nf + 2 : -3])
+    me, n = lax.axis_index("shot"), lax.axis_size("shot")
+    rows = vel.shape[0]
+    barrier = pltpu.get_barrier_semaphore()
+    for d in range(1, n):
+        pl.semaphore_signal(barrier, inc=1, device_id={"shot": lax.rem(me + d, n)}, device_id_type=pl.DeviceIdType.MESH)
+
+    def send(d):
+        peer = lax.rem(me + d, n)
+        return pltpu.make_async_remote_copy(
+            src_ref=vel,
+            dst_ref=full.at[pl.ds(pl.multiple_of(me * rows, rows), rows)],
+            send_sem=ag_ss.at[d],
+            recv_sem=ag_rs.at[me],
+            device_id={"shot": peer},
+            device_id_type=pl.DeviceIdType.MESH,
+        )
+
+    ex.start(extra=n - 1)
+    for d in range(1, n):
+        send(d).start()
+    own = pltpu.make_async_copy(vel, full.at[pl.ds(pl.multiple_of(me * rows, rows), rows)], ag_own)
+    own.start()
     ex.finish()
-
-
-def exchange(fields, collective_id):
+    for d in range(1, n):
+        send(d).wait_send()
+    own.wait()
+    for d in range(1, n):
+        src = lax.rem(me + d, n)
+        pltpu.make_async_remote_copy(
+            src_ref=vel,
+            dst_ref=full.at[pl.ds(pl.multiple_of(src * rows, rows), rows)],
+            send_sem=ag_ss.at[d],
+            recv_sem=ag_rs.at[src],
+            device_id={"shot": src},
+            device_id_type=pl.DeviceIdType.MESH,
+        ).wait_recv()
+
+
+def exchange(fields, collective_id, velocity=None):
     nf = len(fields)
     rows, cols, depth = fields[0].shape
     any_spec = pl.BlockSpec(memory_space=pl.ANY)
     shapes, scratch = exchange_io(nf, rows, cols, depth)
+    args = list(fields)
+    gather = velocity is not None
+    if gather:
+        n = lax.axis_size("shot")
+        args.append(velocity)
+        shapes = shapes + [jax.ShapeDtypeStruct((n * velocity.shape[0],) + velocity.shape[1:], jnp.float32)]
+        scratch = scratch + [pltpu.SemaphoreType.DMA((n,)), pltpu.SemaphoreType.DMA((n,)), pltpu.SemaphoreType.DMA(())]
     outs = pl.pallas_call(
-        functools.partial(exchange_kernel, nf),
-        in_specs=[any_spec] * nf,
-        out_specs=[any_spec] * (4 * nf),
+        functools.partial(exchange_kernel, nf, gather),
+        in_specs=[any_spec] * len(args),
+        out_specs=[any_spec] * len(shapes),
         out_shape=shapes,
         scratch_shapes=scratch,
         compiler_params=pltpu.CompilerParams(collective_id=collective_id, has_side_effects=True),
         name=f"halo_exchange_{collective_id}",
-    )(*fields)
-    return [outs[4 * j : 4 * j + 4] for j in range(nf)]
+    )(*args)
+    halos = [outs[4 * j : 4 * j + 4] for j in range(nf)]
+    if gather:
+        return halos, outs[-1]
+    return halos
 
 
 class HaloSender:
@@ -703,8 +756,6 @@
     src_cell,
     wavelet,
 ):
-    full_velocity = lax.all_gather(velocity, "shot", axis=0, tiled=True)
-    row_count, col_count, depth_cells = full_velocity.shape
     oldest = u_prev[0]
     present = u_cur[0]
     adj_later = adj_next[0]
@@ -714,7 +765,7 @@
     src = src_cell[0]
     amp = wavelet[0]
 
-    wave_h, adj_h = exchange([present, adj_now], 1)
+    (wave_h, adj_h), full_velocity = exchange([present, adj_now], 1, velocity)
     advanced, dw1, pick_adv = leap(
         "wave1", present, *wave_h, oldest, full_velocity, {S.rec: rec, S.src: src, S.amp: amp}
     )

time: 187 us -> 172 us (0.920)
  between operations: 14.1 us -> 0.73 us
    pallas_call x4, Pallas kernels: 119 us -> 116 us  [leap(): pl.pallas_call(functools.partial(step_kernel, kind, tuple(names), nf_ex),...]
    pallas_call x1, Pallas kernels: 44.1 us -> 47.1 us  [exchange(): pl.pallas_call(functools.partial(exchange_kernel, nf, gather), in_specs=[...]
  transfers between devices with their start and end apart: 1 -> 0, of which waited for: 0 -> 0; matrix products, arithmetic and copies ran while one was open for 3% -> 0% of each run, Pallas kernels for 24% -> 0%
where the time goes in v14:
time: 172 us; the launch traced here: 170 us
  Pallas kernels  163 us (95%)
  local copies, waits for them, and re-layouts  4.25 us (2%)
  other arithmetic  2.55 us (1%)
    pallas_call x4, Pallas kernels, leap(): pl.pallas_call(functools.partial(step_kernel, kind, tuple(names), nf_ex),...  116 us
    pallas_call x1, Pallas kernels, exchange(): pl.pallas_call(functools.partial(exchange_kernel, nf, gather), in_specs=[...  47.1 us

profile of v14, /device:TPU:1, one launch (start us, length us, event | category | flops | bytes accessed | tf_op | source)
XLA Modules:
  0.0 170.4 jit_solution(10958932091507848761)
XLA Ops:
  0.6 0.0 copy-start.4
  0.6 47.1 %halo_exchange_1.1 = (f32[4,64,384]{2,1,0:T(8,128)}, f32[4,64,384]{2,1,0:T(8,128)}, f32[32,8,384]{2,1,0:T(8,128)}, f32[32,8,384]{2,1,0:T(8,128)}, f32[4,64,384]{...) custom-call(f32[32,64,384]{2,1,0:T(8,128)} %bitcast.11, ...), custom_call_target="tpu_custom_call" | custom-call | tf_op jit(solution)/shard_map/halo_exchange_1/pallas_call | solution.py:243
  47.7 0.0 copy-done.4
  47.7 1.4 copy.13.refs_9_
  49.1 15.3 %leap_wave1.1 = (f32[32,64,384]{2,1,0:T(8,128)}, f32[32,64,384]{2,1,0:T(8,128)}, f32[32,64,1]{2,1,0:T(8,128)}) custom-call(f32[32,64,384]{2,1,0:T(8,128)} %bitcast.12, f32[32,64,384]{2,1,0:T(8,128)} %bitcast.13, f32[32,64,384]{2,1,0:T(8,128)} %bitcast.14, f32[4,64,384]{2,1,0:T(8,128)} %get-tuple-element.25.refs_3_, f32[4,64,384]{2,1,0:T(8,128)} %get-tuple-element.26.refs_4_, ...), custom_call_target="tpu_custom_call" | custom-call | flops 47185920 | bytes 18874368 | tf_op jit(solution)/shard_map/leap_wave1/pallas_call | solution.py:726
  64.4 0.0 copy-start.3
  64.4 24.9 %leap_adjbulk.1 = (f32[32,64,384]{2,1,0:T(8,128)}, f32[4,64,384]{2,1,0:T(8,128)}, f32[4,64,384]{2,1,0:T(8,128)}, f32[32,8,384]{2,1,0:T(8,128)}, f32[32,8,384]{2,1,0:T(8,128)}) custom-call(f32[32,64,384]{2,1,0:T(8,128)} %bitcast.17, f32[32,64,384]{2,1,0:T(8,128)} %bitcast.18, f32[32,64,384]{2,1,0:T(8,128)} %bitcast.19, ...), custom_call_target="tpu_custom_call" | custom-call | flops 47185920 | bytes 15728640 | tf_op jit(solution)/shard_map/leap_adjbulk/pallas_call | solution.py:726
  89.3 0.0 copy-done.3
  89.3 1.4 copy.15.refs_13_
  90.7 33.0 %leap_wave2.1 = (f32[32,64,384]{2,1,0:T(8,128)}, f32[32,64,1]{2,1,0:T(8,128)}, f32[32,64,384]{2,1,0:T(8,128)}, f32[32,64,384]{2,1,0:T(8,128)}, f32[4,64,384]{2,1...) custom-call(f32[32,64,384]{2,1,0:T(8,128)} %get-tuple-element.30.refs_9_.refs_0_.refs_1_.refs_2_, ...), custom_call_target="tpu_custom_call" | custom-call | flops 47185920 | bytes 25165824 | tf_op jit(solution)/shard_map/leap_wave2/pallas_call | solution.py:726
  123.7 1.4 copy.17.refs_11_
  125.1 0.0 copy-start
  125.1 0.0 copy-start.1
  125.1 0.0 copy-start.2
  125.1 42.6 %leap_adj2.1 = f32[8,64,384]{2,1,0:T(8,128)} custom-call(f32[32,64,384]{2,1,0:T(8,128)} %get-tuple-element.40.refs_0_.refs_1_.refs_2_, f32[32,64,384]{2,1,0:T(8,128)} %get-tuple-element.40.refs_0_.refs_1_.refs_2_, f32[32,64,384]{2,1,0:T(8,128)} %get-tuple-element.40.refs_0_.refs_1_.refs_2_, f32[4,64,384]{2,1,0:T(8,128)} %get-tuple-element.41.refs_3_, ...), custom_call_target="tpu_custom_call" | custom-call | flops 47185920 | bytes 18874368 | tf_op jit(solution)/shard_map/leap_adj2/pallas_call | solution.py:726
  167.8 0.0 copy-done
  167.8 0.0 copy-done.1
  167.8 0.0 copy-done.2
  167.8 2.6 %divide_add_fusion = (f32[8,64,384]{2,1,0:T(8,128)}, f32[8,64,384]{2,1,0:T(8,128)}) fusion(f32[8,64,384]{2,1,0:T(8,128)S(1)} %copy-done, f32[8,64,384]{2,1,0:T(8,128)S(1)} %copy-done.1, f32[8,64,384]{2,1,0:T(8,128)S(1)} %copy-done.2, f32[8,64,384]{2,1,0:T(8,128)} %leap_adj2.1), kind=kLoop, calls=%fused_computation | loop fusion | flops 1376256 | bytes 4718592 | tf_op jit(solution)/shard_map/add | solution.py:801
  (1 shorter events, 0.0 us)
Async XLA Ops:
  0.6 47.1 %copy-start.4 = (s32[1,32,64]{2,1,0:T(8,128)S(1)}, s32[1,32,64]{2,1,0:T(8,128)}, u32[]{:S(2)}) copy-start(s32[1,32,64]{2,1,0:T(8,128)} %param.19) | copy-start | bytes 24580
  64.4 24.9 %copy-start.3 = (f32[1,2,32,64]{3,2,1,0:T(8,128)S(1)}, f32[1,2,32,64]{3,2,1,0:T(8,128)}, u32[]{:S(2)}) copy-start(f32[1,2,32,64]{3,2,1,0:T(8,128)} %param.18) | copy-start | bytes 49156
  125.1 42.6 %copy-start = (f32[8,64,384]{2,1,0:T(8,128)S(1)}, f32[8,64,384]{2,1,0:T(8,128)}, u32[]{:S(2)}) copy-start(f32[8,64,384]{2,1,0:T(8,128)} %refs_2_.1) | copy-start | bytes 2359300
  125.1 42.7 %copy-start.1 = (f32[8,64,384]{2,1,0:T(8,128)S(1)}, f32[8,64,384]{2,1,0:T(8,128)}, u32[]{:S(2)}) copy-start(f32[8,64,384]{2,1,0:T(8,128)} %param.13) | copy-start | bytes 2359300
  125.1 42.7 %copy-start.2 = (f32[8,64,384]{2,1,0:T(8,128)S(1)}, f32[8,64,384]{2,1,0:T(8,128)}, u32[]{:S(2)}) copy-start(f32[8,64,384]{2,1,0:T(8,128)} %param.12) | copy-start | bytes 2359300

commit v15 on v14

--- a/solution.py
+++ b/solution.py
@@ -67,6 +67,7 @@
     ex_b = 110
     h_b = 130
     pick = 140
+    aux = 141
 
 
 ROWS_PER_STEP = 8
@@ -513,6 +514,7 @@
 
     z_index = lax.broadcasted_iota(jnp.int32, (Y_CHUNK, depth), 1)
     y_index = lax.broadcasted_iota(jnp.int32, (Y_CHUNK, depth), 0)
+    obs_at = 2 if kind == "wave2" else 1
     wave = kind in ("wave1", "wave2")
     if wave:
         src_ref = ref[S.src]
@@ -542,7 +544,7 @@
             prev = ref[S.prev][r, ys, :]
             out = 2.0 * c - prev + stiff * result
             if wave:
-                at_rec = z_index == ref[S.rec][r, ys, :]
+                at_rec = z_index == ref[S.aux][r, ys, 0:1].astype(jnp.int32)
                 hit = (r == src_x) & (y_index + y0 == src_y) & (z_index == src_z)
                 out = out + jnp.where(hit, amp, 0.0)
                 sel = jnp.where(at_rec, out, 0.0)
@@ -556,8 +558,8 @@
             elif kind == "adjbulk":
                 ref[S.o_f][r, ys, :] = out
             else:
-                at_rec = z_index == ref[S.rec][r, ys, :]
-                misfit = ref[S.pick][r, ys, :] - ref[S.obs][r, ys, :]
+                at_rec = z_index == ref[S.aux][r, ys, 0:1].astype(jnp.int32)
+                misfit = ref[S.pick][r, ys, :] - ref[S.aux][r, ys, obs_at : obs_at + 1]
                 out = out + jnp.where(at_rec, misfit, 0.0)
                 ref[S.slot_out][i, r, ys, :] = ref[S.part][r, ys, :] + out * ref[S.dw][r, ys, :]
         return carry
@@ -575,8 +577,8 @@
         def inject(r, carry):
             for y0 in range(0, cols, Y_CHUNK):
                 ys = pl.ds(y0, Y_CHUNK)
-                at_rec = z_index == ref[S.rec][r, ys, :]
-                misfit = ref[S.o_pick][r, ys, :] - ref[S.obs][r, ys, :]
+                at_rec = z_index == ref[S.aux][r, ys, 0:1].astype(jnp.int32)
+                misfit = ref[S.o_pick][r, ys, :] - ref[S.aux][r, ys, obs_at : obs_at + 1]
                 a2 = ref[S.a2raw][r, ys, :] + jnp.where(at_rec, misfit, 0.0)
                 ref[S.o_a2][r, ys, :] = a2
                 ref[S.o_part][r, ys, :] = a2 * ref[S.o_dw][r, ys, :]
@@ -631,12 +633,13 @@
     whole4 = pl.BlockSpec((4, cols, depth), fixed(lambda i: (0, 0, 0)))
     yspec = pl.BlockSpec((tb, 8, depth), at(lambda i: (i, 0, 0)))
     col1 = pl.BlockSpec((tb, cols, 1), at(lambda i: (i, 0, 0)))
+    col3 = pl.BlockSpec((tb, cols, 3), at(lambda i: (i, 0, 0)))
     slab = pl.BlockSpec((tb, cols, depth), fixed(lambda i: (0, 0, 0)))
     smem = pl.BlockSpec(memory_space=pltpu.SMEM)
     any_spec = pl.BlockSpec(memory_space=pl.ANY)
     field = jax.ShapeDtypeStruct((rows, cols, depth), jnp.float32)
     picked = jax.ShapeDtypeStruct((rows, cols, 1), jnp.float32)
-    spec_of = {S.src: smem, S.amp: smem, S.rec: col1, S.mis: col1, S.obs: col1, S.pick: col1, S.vslab: slab, S.mom: slab, S.mass: slab}
+    spec_of = {S.aux: col3, S.src: smem, S.amp: smem, S.rec: col1, S.mis: col1, S.obs: col1, S.pick: col1, S.vslab: slab, S.mom: slab, S.mass: slab}
 
     names = [S.f, S.flo, S.fhi, S.xlo, S.xhi, S.ylo, S.yhi, S.prev, S.vel]
     in_specs = [block, lo_spec, hi_spec, whole4, whole4, yspec, yspec, block, block]
@@ -760,14 +763,14 @@
     present = u_cur[0]
     adj_later = adj_next[0]
     adj_now = adj_cur[0]
-    rec = rec_depth[0][:, :, None]
+    aux = jnp.stack([rec_depth[0].astype(jnp.float32), observed[0, 0], observed[0, 1]], axis=-1)
     cell = src_cell[0]
     src = src_cell[0]
     amp = wavelet[0]
 
     (wave_h, adj_h), full_velocity = exchange([present, adj_now], 1, velocity)
     advanced, dw1, pick_adv = leap(
-        "wave1", present, *wave_h, oldest, full_velocity, {S.rec: rec, S.src: src, S.amp: amp}
+        "wave1", present, *wave_h, oldest, full_velocity, {S.aux: aux, S.src: src, S.amp: amp}
     )
     (adj_bulk,), (adv_h,) = leap(
         "adjbulk", adj_now, *adj_h, adj_later, full_velocity, {}, exchanged=[advanced], collective_id=2
@@ -778,7 +781,7 @@
         *adv_h,
         present,
         full_velocity,
-        {S.rec: rec, S.src: src, S.amp: amp, S.a2raw: adj_bulk, S.obs: observed[0, 1][:, :, None]},
+        {S.aux: aux, S.src: src, S.amp: amp, S.a2raw: adj_bulk},
         collective_id=3,
     )
     (summed,) = leap(
@@ -788,9 +791,8 @@
         adj_now,
         full_velocity,
         {
-            S.rec: rec,
+            S.aux: aux,
             S.pick: pick_adv,
-            S.obs: observed[0, 0][:, :, None],
             S.dw: dw1,
             S.part: part,
         },

time: 172 us -> 175 us (1.017)
  Pallas kernels: 163 us -> 167 us
  local copies, waits for them, and re-layouts: 4.25 us -> 2.17 us
    pallas_call x4, Pallas kernels: 116 us -> 120 us  [leap(): pl.pallas_call(functools.partial(step_kernel, kind, tuple(names), nf_ex),...]
    another operation x4 -> x2, local copies, waits for them, and re-layouts: 4.23 us -> 2.16 us  [on_device(): jnp.stack([rec_depth[0].astype(jnp.float32), observed[0, 0], observed[0,...]
where the time goes in v15:
time: 175 us; the launch traced here: 173 us
  Pallas kernels  167 us (95%)
  other arithmetic  3.28 us (2%)
  local copies, waits for them, and re-layouts  2.17 us (1%)
    pallas_call x4, Pallas kernels, leap(): pl.pallas_call(functools.partial(step_kernel, kind, tuple(names), nf_ex),...  120 us
    pallas_call x1, Pallas kernels, exchange(): pl.pallas_call(functools.partial(exchange_kernel, nf, gather), in_specs=[...  47 us

profile of v15, /device:TPU:1, one launch (start us, length us, event | category | flops | bytes accessed | tf_op | source)
XLA Modules:
  0.0 173.3 jit_solution(2043497102838048889)
XLA Ops:
  0.6 0.7 convert_bitcast_fusion
  1.4 0.7 slice_bitcast_fusion.1
  2.1 1.4 copy.16.refs_9_
  3.5 47.0 %halo_exchange_1.1 = (f32[4,64,384]{2,1,0:T(8,128)}, f32[4,64,384]{2,1,0:T(8,128)}, f32[32,8,384]{2,1,0:T(8,128)}, f32[32,8,384]{2,1,0:T(8,128)}, f32[4,64,384]{...) custom-call(f32[32,64,384]{2,1,0:T(8,128)} %bitcast.17, ...), custom_call_target="tpu_custom_call" | custom-call | tf_op jit(solution)/shard_map/halo_exchange_1/pallas_call | solution.py:244
  50.5 15.2 %leap_wave1.1 = (f32[32,64,384]{2,1,0:T(8,128)}, f32[32,64,384]{2,1,0:T(8,128)}, f32[32,64,1]{2,1,0:T(8,128)}) custom-call(f32[32,64,384]{2,1,0:T(8,128)} %bitcast.18, f32[32,64,384]{2,1,0:T(8,128)} %bitcast.19, f32[32,64,384]{2,1,0:T(8,128)} %bitcast.20, f32[4,64,384]{2,1,0:T(8,128)} %get-tuple-element.25.refs_3_, f32[4,64,384]{2,1,0:T(8,128)} %get-tuple-element.26.refs_4_, ...), custom_call_target="tpu_custom_call" | custom-call | flops 47185920 | bytes 18874368 | tf_op jit(solution)/shard_map/leap_wave1/pallas_call | solution.py:729
  65.7 24.9 %leap_adjbulk.1 = (f32[32,64,384]{2,1,0:T(8,128)}, f32[4,64,384]{2,1,0:T(8,128)}, f32[4,64,384]{2,1,0:T(8,128)}, f32[32,8,384]{2,1,0:T(8,128)}, f32[32,8,384]{2,1,0:T(8,128)}) custom-call(f32[32,64,384]{2,1,0:T(8,128)} %bitcast.13, f32[32,64,384]{2,1,0:T(8,128)} %bitcast.14, f32[32,64,384]{2,1,0:T(8,128)} %bitcast.15, ...), custom_call_target="tpu_custom_call" | custom-call | flops 47185920 | bytes 15728640 | tf_op jit(solution)/shard_map/leap_adjbulk/pallas_call | solution.py:729
  90.6 33.5 %leap_wave2.1 = (f32[32,64,384]{2,1,0:T(8,128)}, f32[32,64,1]{2,1,0:T(8,128)}, f32[32,64,384]{2,1,0:T(8,128)}, f32[32,64,384]{2,1,0:T(8,128)}, f32[4,64,384]{2,1...) custom-call(f32[32,64,384]{2,1,0:T(8,128)} %get-tuple-element.30.refs_9_.refs_0_.refs_1_.refs_2_, ...), custom_call_target="tpu_custom_call" | custom-call | flops 47185920 | bytes 25165824 | tf_op jit(solution)/shard_map/leap_wave2/pallas_call | solution.py:729
  124.1 0.0 copy-start
  124.1 0.0 copy-start.1
  124.1 0.0 copy-start.2
  124.2 46.5 %leap_adj2.1 = f32[8,64,384]{2,1,0:T(8,128)} custom-call(f32[32,64,384]{2,1,0:T(8,128)} %get-tuple-element.40.refs_0_.refs_1_.refs_2_, f32[32,64,384]{2,1,0:T(8,128)} %get-tuple-element.40.refs_0_.refs_1_.refs_2_, f32[32,64,384]{2,1,0:T(8,128)} %get-tuple-element.40.refs_0_.refs_1_.refs_2_, f32[4,64,384]{2,1,0:T(8,128)} %get-tuple-element.41.refs_3_, ...), custom_call_target="tpu_custom_call" | custom-call | flops 47185920 | bytes 18874368 | tf_op jit(solution)/shard_map/leap_adj2/pallas_call | solution.py:729
  170.7 0.0 copy-done
  170.7 0.0 copy-done.1
  170.7 0.0 copy-done.2
  170.7 2.6 %divide_add_fusion = (f32[8,64,384]{2,1,0:T(8,128)}, f32[8,64,384]{2,1,0:T(8,128)}) fusion(f32[8,64,384]{2,1,0:T(8,128)S(1)} %copy-done, f32[8,64,384]{2,1,0:T(8,128)S(1)} %copy-done.1, f32[8,64,384]{2,1,0:T(8,128)S(1)} %copy-done.2, f32[8,64,384]{2,1,0:T(8,128)} %leap_adj2.1), kind=kLoop, calls=%fused_computation | loop fusion | flops 1376256 | bytes 4718592 | tf_op jit(solution)/shard_map/add | solution.py:803
  (1 shorter events, 0.0 us)
Async XLA Ops:
  124.1 46.5 %copy-start = (f32[8,64,384]{2,1,0:T(8,128)S(1)}, f32[8,64,384]{2,1,0:T(8,128)}, u32[]{:S(2)}) copy-start(f32[8,64,384]{2,1,0:T(8,128)} %refs_2_.1) | copy-start | bytes 2359300
  124.1 46.5 %copy-start.1 = (f32[8,64,384]{2,1,0:T(8,128)S(1)}, f32[8,64,384]{2,1,0:T(8,128)}, u32[]{:S(2)}) copy-start(f32[8,64,384]{2,1,0:T(8,128)} %param.13) | copy-start | bytes 2359300
  124.1 46.5 %copy-start.2 = (f32[8,64,384]{2,1,0:T(8,128)S(1)}, f32[8,64,384]{2,1,0:T(8,128)}, u32[]{:S(2)}) copy-start(f32[8,64,384]{2,1,0:T(8,128)} %param.12) | copy-start | bytes 2359300

commit v16 on v14

--- a/solution.py
+++ b/solution.py
@@ -605,7 +605,7 @@
 
 def leap(kind, f, xlo, xhi, ylo, yhi, prev, vel, extra, exchanged=(), collective_id=None):
     rows, cols, depth = f.shape
-    tb = ROWS_PER_STEP
+    tb = 4 if kind in ("wave1", "adjbulk") else ROWS_PER_STEP
     nblk = rows // tb
     grid = (nblk,)
     nq = rows // 4
@@ -626,8 +626,9 @@
 
         fixed = at
     block = pl.BlockSpec((tb, cols, depth), at(lambda i: (i, 0, 0)))
-    lo_spec = pl.BlockSpec((4, cols, depth), at(lambda i: (jnp.maximum(2 * i - 1, 0), 0, 0)))
-    hi_spec = pl.BlockSpec((4, cols, depth), at(lambda i: (jnp.minimum(2 * i + 2, nq - 1), 0, 0)))
+    q = tb // 4
+    lo_spec = pl.BlockSpec((4, cols, depth), at(lambda i: (jnp.maximum(q * i - 1, 0), 0, 0)))
+    hi_spec = pl.BlockSpec((4, cols, depth), at(lambda i: (jnp.minimum(q * i + q, nq - 1), 0, 0)))
     whole4 = pl.BlockSpec((4, cols, depth), fixed(lambda i: (0, 0, 0)))
     yspec = pl.BlockSpec((tb, 8, depth), at(lambda i: (i, 0, 0)))
     col1 = pl.BlockSpec((tb, cols, 1), at(lambda i: (i, 0, 0)))

time: 172 us -> 172 us (level)
  no operation moved by 1% of the time
where the time goes in v16:
time: 172 us; the launch traced here: 170 us
  Pallas kernels  162 us (94%)
  local copies, waits for them, and re-layouts  4.25 us (2%)
  other arithmetic  2.55 us (1%)
    pallas_call x4, Pallas kernels, leap(): pl.pallas_call(functools.partial(step_kernel, kind, tuple(names), nf_ex),...  115 us
    pallas_call x1, Pallas kernels, exchange(): pl.pallas_call(functools.partial(exchange_kernel, nf, gather), in_specs=[...  47.1 us

profile of v16, /device:TPU:1, one launch (start us, length us, event | category | flops | bytes accessed | tf_op | source)
XLA Modules:
  0.0 169.9 jit_solution(8596115915108611333)
XLA Ops:
  0.6 0.0 copy-start.4
  0.6 47.1 %halo_exchange_1.1 = (f32[4,64,384]{2,1,0:T(8,128)}, f32[4,64,384]{2,1,0:T(8,128)}, f32[32,8,384]{2,1,0:T(8,128)}, f32[32,8,384]{2,1,0:T(8,128)}, f32[4,64,384]{...) custom-call(f32[32,64,384]{2,1,0:T(8,128)} %bitcast.11, ...), custom_call_target="tpu_custom_call" | custom-call | tf_op jit(solution)/shard_map/halo_exchange_1/pallas_call | solution.py:243
  47.7 0.0 copy-done.4
  47.7 1.4 copy.13.refs_9_
  49.1 15.7 %leap_wave1.1 = (f32[32,64,384]{2,1,0:T(8,128)}, f32[32,64,384]{2,1,0:T(8,128)}, f32[32,64,1]{2,1,0:T(8,128)}) custom-call(f32[32,64,384]{2,1,0:T(8,128)} %bitcast.12, f32[32,64,384]{2,1,0:T(8,128)} %bitcast.13, f32[32,64,384]{2,1,0:T(8,128)} %bitcast.14, f32[4,64,384]{2,1,0:T(8,128)} %get-tuple-element.25.refs_3_, f32[4,64,384]{2,1,0:T(8,128)} %get-tuple-element.26.refs_4_, ...), custom_call_target="tpu_custom_call" | custom-call | flops 47185920 | bytes 18874368 | tf_op jit(solution)/shard_map/leap_wave1/pallas_call | solution.py:727
  64.8 0.0 copy-start.3
  64.8 24.0 %leap_adjbulk.1 = (f32[32,64,384]{2,1,0:T(8,128)}, f32[4,64,384]{2,1,0:T(8,128)}, f32[4,64,384]{2,1,0:T(8,128)}, f32[32,8,384]{2,1,0:T(8,128)}, f32[32,8,384]{2,1,0:T(8,128)}) custom-call(f32[32,64,384]{2,1,0:T(8,128)} %bitcast.17, f32[32,64,384]{2,1,0:T(8,128)} %bitcast.18, f32[32,64,384]{2,1,0:T(8,128)} %bitcast.19, ...), custom_call_target="tpu_custom_call" | custom-call | flops 47185920 | bytes 15728640 | tf_op jit(solution)/shard_map/leap_adjbulk/pallas_call | solution.py:727
  88.8 0.0 copy-done.3
  88.8 1.4 copy.15.refs_13_
  90.3 33.0 %leap_wave2.1 = (f32[32,64,384]{2,1,0:T(8,128)}, f32[32,64,1]{2,1,0:T(8,128)}, f32[32,64,384]{2,1,0:T(8,128)}, f32[32,64,384]{2,1,0:T(8,128)}, f32[4,64,384]{2,1...) custom-call(f32[32,64,384]{2,1,0:T(8,128)} %get-tuple-element.30.refs_9_.refs_0_.refs_1_.refs_2_, ...), custom_call_target="tpu_custom_call" | custom-call | flops 47185920 | bytes 25165824 | tf_op jit(solution)/shard_map/leap_wave2/pallas_call | solution.py:727
  123.3 1.4 copy.17.refs_11_
  124.7 0.0 copy-start
  124.7 0.0 copy-start.1
  124.7 0.0 copy-start.2
  124.7 42.6 %leap_adj2.1 = f32[8,64,384]{2,1,0:T(8,128)} custom-call(f32[32,64,384]{2,1,0:T(8,128)} %get-tuple-element.40.refs_0_.refs_1_.refs_2_, f32[32,64,384]{2,1,0:T(8,128)} %get-tuple-element.40.refs_0_.refs_1_.refs_2_, f32[32,64,384]{2,1,0:T(8,128)} %get-tuple-element.40.refs_0_.refs_1_.refs_2_, f32[4,64,384]{2,1,0:T(8,128)} %get-tuple-element.41.refs_3_, ...), custom_call_target="tpu_custom_call" | custom-call | flops 47185920 | bytes 18874368 | tf_op jit(solution)/shard_map/leap_adj2/pallas_call | solution.py:727
  167.3 0.0 copy-done
  167.3 0.0 copy-done.1
  167.3 0.0 copy-done.2
  167.3 2.6 %divide_add_fusion = (f32[8,64,384]{2,1,0:T(8,128)}, f32[8,64,384]{2,1,0:T(8,128)}) fusion(f32[8,64,384]{2,1,0:T(8,128)S(1)} %copy-done, f32[8,64,384]{2,1,0:T(8,128)S(1)} %copy-done.1, f32[8,64,384]{2,1,0:T(8,128)S(1)} %copy-done.2, f32[8,64,384]{2,1,0:T(8,128)} %leap_adj2.1), kind=kLoop, calls=%fused_computation | loop fusion | flops 1376256 | bytes 4718592 | tf_op jit(solution)/shard_map/add | solution.py:802
  (1 shorter events, 0.0 us)
Async XLA Ops:
  0.6 47.1 %copy-start.4 = (s32[1,32,64]{2,1,0:T(8,128)S(1)}, s32[1,32,64]{2,1,0:T(8,128)}, u32[]{:S(2)}) copy-start(s32[1,32,64]{2,1,0:T(8,128)} %param.19) | copy-start | bytes 24580
  64.8 24.0 %copy-start.3 = (f32[1,2,32,64]{3,2,1,0:T(8,128)S(1)}, f32[1,2,32,64]{3,2,1,0:T(8,128)}, u32[]{:S(2)}) copy-start(f32[1,2,32,64]{3,2,1,0:T(8,128)} %param.18) | copy-start | bytes 49156
  124.7 42.6 %copy-start = (f32[8,64,384]{2,1,0:T(8,128)S(1)}, f32[8,64,384]{2,1,0:T(8,128)}, u32[]{:S(2)}) copy-start(f32[8,64,384]{2,1,0:T(8,128)} %refs_2_.1) | copy-start | bytes 2359300
  124.7 42.7 %copy-start.1 = (f32[8,64,384]{2,1,0:T(8,128)S(1)}, f32[8,64,384]{2,1,0:T(8,128)}, u32[]{:S(2)}) copy-start(f32[8,64,384]{2,1,0:T(8,128)} %param.13) | copy-start | bytes 2359300
  124.7 42.7 %copy-start.2 = (f32[8,64,384]{2,1,0:T(8,128)S(1)}, f32[8,64,384]{2,1,0:T(8,128)}, u32[]{:S(2)}) copy-start(f32[8,64,384]{2,1,0:T(8,128)} %param.12) | copy-start | bytes 2359300

commit v17 on v14

--- a/solution.py
+++ b/solution.py
@@ -188,44 +188,49 @@
     vel = refs[nf]
     bufs = refs[nf + 1 : 5 * nf + 1]
     full = refs[5 * nf + 1]
-    ag_ss, ag_rs, ag_own = refs[-3:]
-    ex = Exchange(refs[:nf], bufs, *refs[5 * nf + 2 : -3])
+    ag_ss, ag_rs, ag_own, rl_top, rl_bot, rl_rs = refs[-6:]
+    ex = Exchange(refs[:nf], bufs, *refs[5 * nf + 2 : -6])
     me, n = lax.axis_index("shot"), lax.axis_size("shot")
+    up, down, far = lax.rem(me + 1, n), lax.rem(me + n - 1, n), lax.rem(me + 2, n)
     rows = vel.shape[0]
+    half = rows // 2
+    mesh = pl.DeviceIdType.MESH
+
+    def at_rows(who):
+        return full.at[pl.ds(pl.multiple_of(who * rows, rows), rows)]
+
+    def remote(src, dst, k, recv_sem, peer):
+        return pltpu.make_async_remote_copy(
+            src_ref=src, dst_ref=dst, send_sem=ag_ss.at[k], recv_sem=recv_sem, device_id={"shot": peer}, device_id_type=mesh
+        )
+
+    to_up = remote(vel, at_rows(me), 0, ag_rs.at[me], up)
+    to_down = remote(vel, at_rows(me), 1, ag_rs.at[me], down)
+    relay_top = remote(vel.at[pl.ds(0, half)], rl_top, 2, rl_rs.at[0], up)
+    relay_bot = remote(vel.at[pl.ds(half, half)], rl_bot, 3, rl_rs.at[1], down)
+    fwd_top = remote(rl_top, at_rows(down).at[pl.ds(0, half)], 4, rl_rs.at[2], up)
+    fwd_bot = remote(rl_bot, at_rows(up).at[pl.ds(half, half)], 5, rl_rs.at[3], down)
+
     barrier = pltpu.get_barrier_semaphore()
-    for d in range(1, n):
-        pl.semaphore_signal(barrier, inc=1, device_id={"shot": lax.rem(me + d, n)}, device_id_type=pl.DeviceIdType.MESH)
-
-    def send(d):
-        peer = lax.rem(me + d, n)
-        return pltpu.make_async_remote_copy(
-            src_ref=vel,
-            dst_ref=full.at[pl.ds(pl.multiple_of(me * rows, rows), rows)],
-            send_sem=ag_ss.at[d],
-            recv_sem=ag_rs.at[me],
-            device_id={"shot": peer},
-            device_id_type=pl.DeviceIdType.MESH,
-        )
-
-    ex.start(extra=n - 1)
-    for d in range(1, n):
-        send(d).start()
-    own = pltpu.make_async_copy(vel, full.at[pl.ds(pl.multiple_of(me * rows, rows), rows)], ag_own)
+    for peer in (up, down):
+        pl.semaphore_signal(barrier, inc=1, device_id={"shot": peer}, device_id_type=mesh)
+    ex.start(extra=2)
+    for copy in (to_up, to_down, relay_top, relay_bot):
+        copy.start()
+    own = pltpu.make_async_copy(vel, at_rows(me), ag_own)
     own.start()
+    relay_top.wait_recv()
+    relay_bot.wait_recv()
+    fwd_top.start()
+    fwd_bot.start()
     ex.finish()
-    for d in range(1, n):
-        send(d).wait_send()
+    for copy in (to_up, to_down, relay_top, relay_bot, fwd_top, fwd_bot):
+        copy.wait_send()
     own.wait()
-    for d in range(1, n):
-        src = lax.rem(me + d, n)
-        pltpu.make_async_remote_copy(
-            src_ref=vel,
-            dst_ref=full.at[pl.ds(pl.multiple_of(src * rows, rows), rows)],
-            send_sem=ag_ss.at[d],
-            recv_sem=ag_rs.at[src],
-            device_id={"shot": src},
-            device_id_type=pl.DeviceIdType.MESH,
-        ).wait_recv()
+    for src in (up, down):
+        remote(vel, at_rows(src), 0, ag_rs.at[src], src).wait_recv()
+    remote(rl_top, at_rows(far).at[pl.ds(0, half)], 4, rl_rs.at[2], down).wait_recv()
+    remote(rl_bot, at_rows(far).at[pl.ds(half, half)], 5, rl_rs.at[3], up).wait_recv()
 
 
 def exchange(fields, collective_id, velocity=None):
@@ -239,7 +244,15 @@
         n = lax.axis_size("shot")
         args.append(velocity)
         shapes = shapes + [jax.ShapeDtypeStruct((n * velocity.shape[0],) + velocity.shape[1:], jnp.float32)]
-        scratch = scratch + [pltpu.SemaphoreType.DMA((n,)), pltpu.SemaphoreType.DMA((n,)), pltpu.SemaphoreType.DMA(())]
+        half_slab = (velocity.shape[0] // 2,) + velocity.shape[1:]
+        scratch = scratch + [
+            pltpu.SemaphoreType.DMA((6,)),
+            pltpu.SemaphoreType.DMA((n,)),
+            pltpu.SemaphoreType.DMA(()),
+            pltpu.VMEM(half_slab, jnp.float32),
+            pltpu.VMEM(half_slab, jnp.float32),
+            pltpu.SemaphoreType.DMA((4,)),
+        ]
     outs = pl.pallas_call(
         functools.partial(exchange_kernel, nf, gather),
         in_specs=[any_spec] * len(args),

time: 172 us -> 173 us (level)
  Pallas kernels: 163 us -> 165 us
    pallas_call x4, Pallas kernels: 116 us -> 118 us  [leap(): pl.pallas_call(functools.partial(step_kernel, kind, tuple(names), nf_ex),...]
where the time goes in v17:
time: 173 us
  Pallas kernels  165 us (95%)
  local copies, waits for them, and re-layouts  4.25 us (2%)
  other arithmetic  2.55 us (1%)
    pallas_call x4, Pallas kernels, leap(): pl.pallas_call(functools.partial(step_kernel, kind, tuple(names), nf_ex),...  118 us
    pallas_call x1, Pallas kernels, exchange(): pl.pallas_call(functools.partial(exchange_kernel, nf, gather), in_specs=[...  47.1 us

profile of v17, /device:TPU:1, one launch (start us, length us, event | category | flops | bytes accessed | tf_op | source)
XLA Modules:
  0.0 172.6 jit_solution(12045603572547742685)
XLA Ops:
  0.6 0.0 copy-start.4
  0.6 47.1 %halo_exchange_1.1 = (f32[4,64,384]{2,1,0:T(8,128)}, f32[4,64,384]{2,1,0:T(8,128)}, f32[32,8,384]{2,1,0:T(8,128)}, f32[32,8,384]{2,1,0:T(8,128)}, f32[4,64,384]{...) custom-call(f32[32,64,384]{2,1,0:T(8,128)} %bitcast.11, ...), custom_call_target="tpu_custom_call" | custom-call | tf_op jit(solution)/shard_map/halo_exchange_1/pallas_call | solution.py:256
  47.8 0.0 copy-done.4
  47.8 1.4 copy.13.refs_9_
  49.2 15.3 %leap_wave1.1 = (f32[32,64,384]{2,1,0:T(8,128)}, f32[32,64,384]{2,1,0:T(8,128)}, f32[32,64,1]{2,1,0:T(8,128)}) custom-call(f32[32,64,384]{2,1,0:T(8,128)} %bitcast.12, f32[32,64,384]{2,1,0:T(8,128)} %bitcast.13, f32[32,64,384]{2,1,0:T(8,128)} %bitcast.14, f32[4,64,384]{2,1,0:T(8,128)} %get-tuple-element.25.refs_3_, f32[4,64,384]{2,1,0:T(8,128)} %get-tuple-element.26.refs_4_, ...), custom_call_target="tpu_custom_call" | custom-call | flops 47185920 | bytes 18874368 | tf_op jit(solution)/shard_map/leap_wave1/pallas_call | solution.py:739
  64.5 0.0 copy-start.3
  64.5 27.1 %leap_adjbulk.1 = (f32[32,64,384]{2,1,0:T(8,128)}, f32[4,64,384]{2,1,0:T(8,128)}, f32[4,64,384]{2,1,0:T(8,128)}, f32[32,8,384]{2,1,0:T(8,128)}, f32[32,8,384]{2,1,0:T(8,128)}) custom-call(f32[32,64,384]{2,1,0:T(8,128)} %bitcast.17, f32[32,64,384]{2,1,0:T(8,128)} %bitcast.18, f32[32,64,384]{2,1,0:T(8,128)} %bitcast.19, ...), custom_call_target="tpu_custom_call" | custom-call | flops 47185920 | bytes 15728640 | tf_op jit(solution)/shard_map/leap_adjbulk/pallas_call | solution.py:739
  91.6 0.0 copy-done.3
  91.7 1.4 copy.15.refs_13_
  93.1 31.3 %leap_wave2.1 = (f32[32,64,384]{2,1,0:T(8,128)}, f32[32,64,1]{2,1,0:T(8,128)}, f32[32,64,384]{2,1,0:T(8,128)}, f32[32,64,384]{2,1,0:T(8,128)}, f32[4,64,384]{2,1...) custom-call(f32[32,64,384]{2,1,0:T(8,128)} %get-tuple-element.30.refs_9_.refs_0_.refs_1_.refs_2_, ...), custom_call_target="tpu_custom_call" | custom-call | flops 47185920 | bytes 25165824 | tf_op jit(solution)/shard_map/leap_wave2/pallas_call | solution.py:739
  124.4 1.4 copy.17.refs_11_
  125.8 0.0 copy-start
  125.8 0.0 copy-start.1
  125.8 0.0 copy-start.2
  125.8 44.2 %leap_adj2.1 = f32[8,64,384]{2,1,0:T(8,128)} custom-call(f32[32,64,384]{2,1,0:T(8,128)} %get-tuple-element.40.refs_0_.refs_1_.refs_2_, f32[32,64,384]{2,1,0:T(8,128)} %get-tuple-element.40.refs_0_.refs_1_.refs_2_, f32[32,64,384]{2,1,0:T(8,128)} %get-tuple-element.40.refs_0_.refs_1_.refs_2_, f32[4,64,384]{2,1,0:T(8,128)} %get-tuple-element.41.refs_3_, ...), custom_call_target="tpu_custom_call" | custom-call | flops 47185920 | bytes 18874368 | tf_op jit(solution)/shard_map/leap_adj2/pallas_call | solution.py:739
  170.0 0.0 copy-done
  170.0 0.0 copy-done.1
  170.0 0.0 copy-done.2
  170.0 2.6 %divide_add_fusion = (f32[8,64,384]{2,1,0:T(8,128)}, f32[8,64,384]{2,1,0:T(8,128)}) fusion(f32[8,64,384]{2,1,0:T(8,128)S(1)} %copy-done, f32[8,64,384]{2,1,0:T(8,128)S(1)} %copy-done.1, f32[8,64,384]{2,1,0:T(8,128)S(1)} %copy-done.2, f32[8,64,384]{2,1,0:T(8,128)} %leap_adj2.1), kind=kLoop, calls=%fused_computation | loop fusion | flops 1376256 | bytes 4718592 | tf_op jit(solution)/shard_map/add | solution.py:814
  (1 shorter events, 0.0 us)
Async XLA Ops:
  0.6 47.2 %copy-start.4 = (s32[1,32,64]{2,1,0:T(8,128)S(1)}, s32[1,32,64]{2,1,0:T(8,128)}, u32[]{:S(2)}) copy-start(s32[1,32,64]{2,1,0:T(8,128)} %param.19) | copy-start | bytes 24580
  64.5 27.2 %copy-start.3 = (f32[1,2,32,64]{3,2,1,0:T(8,128)S(1)}, f32[1,2,32,64]{3,2,1,0:T(8,128)}, u32[]{:S(2)}) copy-start(f32[1,2,32,64]{3,2,1,0:T(8,128)} %param.18) | copy-start | bytes 49156
  125.8 44.2 %copy-start = (f32[8,64,384]{2,1,0:T(8,128)S(1)}, f32[8,64,384]{2,1,0:T(8,128)}, u32[]{:S(2)}) copy-start(f32[8,64,384]{2,1,0:T(8,128)} %refs_2_.1) | copy-start | bytes 2359300
  125.8 44.2 %copy-start.1 = (f32[8,64,384]{2,1,0:T(8,128)S(1)}, f32[8,64,384]{2,1,0:T(8,128)}, u32[]{:S(2)}) copy-start(f32[8,64,384]{2,1,0:T(8,128)} %param.13) | copy-start | bytes 2359300
  125.8 44.2 %copy-start.2 = (f32[8,64,384]{2,1,0:T(8,128)S(1)}, f32[8,64,384]{2,1,0:T(8,128)}, u32[]{:S(2)}) copy-start(f32[8,64,384]{2,1,0:T(8,128)} %param.12) | copy-start | bytes 2359300

commit v18 on v14

--- a/solution.py
+++ b/solution.py
@@ -70,7 +70,7 @@
 
 
 ROWS_PER_STEP = 8
-Y_CHUNK = 8
+Y_CHUNK = 16
 
 
 class Exchange:

time: 172 us -> 172 us (level)
  no operation moved by 1% of the time
where the time goes in v18:
time: 172 us; the launch traced here: 170 us
  Pallas kernels  163 us (95%)
  local copies, waits for them, and re-layouts  4.25 us (2%)
  other arithmetic  2.55 us (1%)
    pallas_call x4, Pallas kernels, leap(): pl.pallas_call(functools.partial(step_kernel, kind, tuple(names), nf_ex),...  116 us
    pallas_call x1, Pallas kernels, exchange(): pl.pallas_call(functools.partial(exchange_kernel, nf, gather), in_specs=[...  47.1 us

profile of v18, /device:TPU:1, one launch (start us, length us, event | category | flops | bytes accessed | tf_op | source)
XLA Modules:
  0.0 170.5 jit_solution(7284836412707317564)
XLA Ops:
  0.6 0.0 copy-start.4
  0.6 47.1 %halo_exchange_1.1 = (f32[4,64,384]{2,1,0:T(8,128)}, f32[4,64,384]{2,1,0:T(8,128)}, f32[32,8,384]{2,1,0:T(8,128)}, f32[32,8,384]{2,1,0:T(8,128)}, f32[4,64,384]{...) custom-call(f32[32,64,384]{2,1,0:T(8,128)} %bitcast.11, ...), custom_call_target="tpu_custom_call" | custom-call | tf_op jit(solution)/shard_map/halo_exchange_1/pallas_call | solution.py:243
  47.7 0.0 copy-done.4
  47.7 1.4 copy.13.refs_9_
  49.1 15.4 %leap_wave1.1 = (f32[32,64,384]{2,1,0:T(8,128)}, f32[32,64,384]{2,1,0:T(8,128)}, f32[32,64,1]{2,1,0:T(8,128)}) custom-call(f32[32,64,384]{2,1,0:T(8,128)} %bitcast.12, f32[32,64,384]{2,1,0:T(8,128)} %bitcast.13, f32[32,64,384]{2,1,0:T(8,128)} %bitcast.14, f32[4,64,384]{2,1,0:T(8,128)} %get-tuple-element.25.refs_3_, f32[4,64,384]{2,1,0:T(8,128)} %get-tuple-element.26.refs_4_, ...), custom_call_target="tpu_custom_call" | custom-call | flops 47185920 | bytes 18874368 | tf_op jit(solution)/shard_map/leap_wave1/pallas_call | solution.py:726
  64.6 0.0 copy-start.3
  64.6 24.9 %leap_adjbulk.1 = (f32[32,64,384]{2,1,0:T(8,128)}, f32[4,64,384]{2,1,0:T(8,128)}, f32[4,64,384]{2,1,0:T(8,128)}, f32[32,8,384]{2,1,0:T(8,128)}, f32[32,8,384]{2,1,0:T(8,128)}) custom-call(f32[32,64,384]{2,1,0:T(8,128)} %bitcast.17, f32[32,64,384]{2,1,0:T(8,128)} %bitcast.18, f32[32,64,384]{2,1,0:T(8,128)} %bitcast.19, ...), custom_call_target="tpu_custom_call" | custom-call | flops 47185920 | bytes 15728640 | tf_op jit(solution)/shard_map/leap_adjbulk/pallas_call | solution.py:726
  89.4 0.0 copy-done.3
  89.5 1.4 copy.15.refs_13_
  90.9 33.0 %leap_wave2.1 = (f32[32,64,384]{2,1,0:T(8,128)}, f32[32,64,1]{2,1,0:T(8,128)}, f32[32,64,384]{2,1,0:T(8,128)}, f32[32,64,384]{2,1,0:T(8,128)}, f32[4,64,384]{2,1...) custom-call(f32[32,64,384]{2,1,0:T(8,128)} %get-tuple-element.30.refs_9_.refs_0_.refs_1_.refs_2_, ...), custom_call_target="tpu_custom_call" | custom-call | flops 47185920 | bytes 25165824 | tf_op jit(solution)/shard_map/leap_wave2/pallas_call | solution.py:726
  123.9 1.4 copy.17.refs_11_
  125.3 0.0 copy-start
  125.3 0.0 copy-start.1
  125.3 0.0 copy-start.2
  125.3 42.6 %leap_adj2.1 = f32[8,64,384]{2,1,0:T(8,128)} custom-call(f32[32,64,384]{2,1,0:T(8,128)} %get-tuple-element.40.refs_0_.refs_1_.refs_2_, f32[32,64,384]{2,1,0:T(8,128)} %get-tuple-element.40.refs_0_.refs_1_.refs_2_, f32[32,64,384]{2,1,0:T(8,128)} %get-tuple-element.40.refs_0_.refs_1_.refs_2_, f32[4,64,384]{2,1,0:T(8,128)} %get-tuple-element.41.refs_3_, ...), custom_call_target="tpu_custom_call" | custom-call | flops 47185920 | bytes 18874368 | tf_op jit(solution)/shard_map/leap_adj2/pallas_call | solution.py:726
  167.9 0.0 copy-done
  167.9 0.0 copy-done.1
  167.9 0.0 copy-done.2
  167.9 2.6 %divide_add_fusion = (f32[8,64,384]{2,1,0:T(8,128)}, f32[8,64,384]{2,1,0:T(8,128)}) fusion(f32[8,64,384]{2,1,0:T(8,128)S(1)} %copy-done, f32[8,64,384]{2,1,0:T(8,128)S(1)} %copy-done.1, f32[8,64,384]{2,1,0:T(8,128)S(1)} %copy-done.2, f32[8,64,384]{2,1,0:T(8,128)} %leap_adj2.1), kind=kLoop, calls=%fused_computation | loop fusion | flops 1376256 | bytes 4718592 | tf_op jit(solution)/shard_map/add | solution.py:801
  (1 shorter events, 0.0 us)
Async XLA Ops:
  0.6 47.1 %copy-start.4 = (s32[1,32,64]{2,1,0:T(8,128)S(1)}, s32[1,32,64]{2,1,0:T(8,128)}, u32[]{:S(2)}) copy-start(s32[1,32,64]{2,1,0:T(8,128)} %param.19) | copy-start | bytes 24580
  64.6 24.9 %copy-start.3 = (f32[1,2,32,64]{3,2,1,0:T(8,128)S(1)}, f32[1,2,32,64]{3,2,1,0:T(8,128)}, u32[]{:S(2)}) copy-start(f32[1,2,32,64]{3,2,1,0:T(8,128)} %param.18) | copy-start | bytes 49156
  125.3 42.6 %copy-start = (f32[8,64,384]{2,1,0:T(8,128)S(1)}, f32[8,64,384]{2,1,0:T(8,128)}, u32[]{:S(2)}) copy-start(f32[8,64,384]{2,1,0:T(8,128)} %refs_2_.1) | copy-start | bytes 2359300
  125.3 42.6 %copy-start.1 = (f32[8,64,384]{2,1,0:T(8,128)S(1)}, f32[8,64,384]{2,1,0:T(8,128)}, u32[]{:S(2)}) copy-start(f32[8,64,384]{2,1,0:T(8,128)} %param.13) | copy-start | bytes 2359300
  125.3 42.7 %copy-start.2 = (f32[8,64,384]{2,1,0:T(8,128)S(1)}, f32[8,64,384]{2,1,0:T(8,128)}, u32[]{:S(2)}) copy-start(f32[8,64,384]{2,1,0:T(8,128)} %param.12) | copy-start | bytes 2359300

commit v19 on v14

--- a/solution.py
+++ b/solution.py
@@ -113,7 +113,7 @@
             device_id_type=pl.DeviceIdType.MESH,
         )
 
-    def start(self, extra=0):
+    def start(self, extra=0, first=None):
         has, row, nrow, col, ncol = self.has, self.row, self.nrow, self.col, self.ncol
         barrier = pltpu.get_barrier_semaphore()
         for d in range(4):
@@ -123,6 +123,8 @@
 
         count = (1 - row // (nrow - 1)) + (row + nrow - 1) // nrow + (1 - col // (ncol - 1)) + (col + ncol - 1) // ncol
         pl.semaphore_wait(barrier, count + extra)
+        if first is not None:
+            first()
 
         for j in range(len(self.fields)):
             for d in range(4):
@@ -207,9 +209,11 @@
             device_id_type=pl.DeviceIdType.MESH,
         )
 
-    ex.start(extra=n - 1)
-    for d in range(1, n):
-        send(d).start()
+    def gather_first():
+        for d in range(1, n):
+            send(d).start()
+
+    ex.start(extra=n - 1, first=gather_first)
     own = pltpu.make_async_copy(vel, full.at[pl.ds(pl.multiple_of(me * rows, rows), rows)], ag_own)
     own.start()
     ex.finish()

time: 172 us -> 172 us (level)
  no operation moved by 1% of the time
where the time goes in v19:
time: 172 us; the launch traced here: 170 us
  Pallas kernels  163 us (95%)
  local copies, waits for them, and re-layouts  4.25 us (2%)
  other arithmetic  2.55 us (1%)
    pallas_call x4, Pallas kernels, leap(): pl.pallas_call(functools.partial(step_kernel, kind, tuple(names), nf_ex),...  116 us
    pallas_call x1, Pallas kernels, exchange(): pl.pallas_call(functools.partial(exchange_kernel, nf, gather), in_specs=[...  47.1 us

profile of v19, /device:TPU:1, one launch (start us, length us, event | category | flops | bytes accessed | tf_op | source)
XLA Modules:
  0.0 170.4 jit_solution(2855374165036877947)
XLA Ops:
  0.6 0.0 copy-start.4
  0.6 47.1 %halo_exchange_1.1 = (f32[4,64,384]{2,1,0:T(8,128)}, f32[4,64,384]{2,1,0:T(8,128)}, f32[32,8,384]{2,1,0:T(8,128)}, f32[32,8,384]{2,1,0:T(8,128)}, f32[4,64,384]{...) custom-call(f32[32,64,384]{2,1,0:T(8,128)} %bitcast.11, ...), custom_call_target="tpu_custom_call" | custom-call | tf_op jit(solution)/shard_map/halo_exchange_1/pallas_call | solution.py:247
  47.7 0.0 copy-done.4
  47.7 1.4 copy.13.refs_9_
  49.2 15.3 %leap_wave1.1 = (f32[32,64,384]{2,1,0:T(8,128)}, f32[32,64,384]{2,1,0:T(8,128)}, f32[32,64,1]{2,1,0:T(8,128)}) custom-call(f32[32,64,384]{2,1,0:T(8,128)} %bitcast.12, f32[32,64,384]{2,1,0:T(8,128)} %bitcast.13, f32[32,64,384]{2,1,0:T(8,128)} %bitcast.14, f32[4,64,384]{2,1,0:T(8,128)} %get-tuple-element.25.refs_3_, f32[4,64,384]{2,1,0:T(8,128)} %get-tuple-element.26.refs_4_, ...), custom_call_target="tpu_custom_call" | custom-call | flops 47185920 | bytes 18874368 | tf_op jit(solution)/shard_map/leap_wave1/pallas_call | solution.py:730
  64.4 0.0 copy-start.3
  64.4 24.9 %leap_adjbulk.1 = (f32[32,64,384]{2,1,0:T(8,128)}, f32[4,64,384]{2,1,0:T(8,128)}, f32[4,64,384]{2,1,0:T(8,128)}, f32[32,8,384]{2,1,0:T(8,128)}, f32[32,8,384]{2,1,0:T(8,128)}) custom-call(f32[32,64,384]{2,1,0:T(8,128)} %bitcast.17, f32[32,64,384]{2,1,0:T(8,128)} %bitcast.18, f32[32,64,384]{2,1,0:T(8,128)} %bitcast.19, ...), custom_call_target="tpu_custom_call" | custom-call | flops 47185920 | bytes 15728640 | tf_op jit(solution)/shard_map/leap_adjbulk/pallas_call | solution.py:730
  89.3 0.0 copy-done.3
  89.3 1.4 copy.15.refs_13_
  90.7 33.0 %leap_wave2.1 = (f32[32,64,384]{2,1,0:T(8,128)}, f32[32,64,1]{2,1,0:T(8,128)}, f32[32,64,384]{2,1,0:T(8,128)}, f32[32,64,384]{2,1,0:T(8,128)}, f32[4,64,384]{2,1...) custom-call(f32[32,64,384]{2,1,0:T(8,128)} %get-tuple-element.30.refs_9_.refs_0_.refs_1_.refs_2_, ...), custom_call_target="tpu_custom_call" | custom-call | flops 47185920 | bytes 25165824 | tf_op jit(solution)/shard_map/leap_wave2/pallas_call | solution.py:730
  123.7 1.4 copy.17.refs_11_
  125.1 0.0 copy-start
  125.1 0.0 copy-start.1
  125.1 0.0 copy-start.2
  125.1 42.6 %leap_adj2.1 = f32[8,64,384]{2,1,0:T(8,128)} custom-call(f32[32,64,384]{2,1,0:T(8,128)} %get-tuple-element.40.refs_0_.refs_1_.refs_2_, f32[32,64,384]{2,1,0:T(8,128)} %get-tuple-element.40.refs_0_.refs_1_.refs_2_, f32[32,64,384]{2,1,0:T(8,128)} %get-tuple-element.40.refs_0_.refs_1_.refs_2_, f32[4,64,384]{2,1,0:T(8,128)} %get-tuple-element.41.refs_3_, ...), custom_call_target="tpu_custom_call" | custom-call | flops 47185920 | bytes 18874368 | tf_op jit(solution)/shard_map/leap_adj2/pallas_call | solution.py:730
  167.8 0.0 copy-done
  167.8 0.0 copy-done.1
  167.8 0.0 copy-done.2
  167.8 2.6 %divide_add_fusion = (f32[8,64,384]{2,1,0:T(8,128)}, f32[8,64,384]{2,1,0:T(8,128)}) fusion(f32[8,64,384]{2,1,0:T(8,128)S(1)} %copy-done, f32[8,64,384]{2,1,0:T(8,128)S(1)} %copy-done.1, f32[8,64,384]{2,1,0:T(8,128)S(1)} %copy-done.2, f32[8,64,384]{2,1,0:T(8,128)} %leap_adj2.1), kind=kLoop, calls=%fused_computation | loop fusion | flops 1376256 | bytes 4718592 | tf_op jit(solution)/shard_map/add | solution.py:805
  (1 shorter events, 0.0 us)
Async XLA Ops:
  0.6 47.1 %copy-start.4 = (s32[1,32,64]{2,1,0:T(8,128)S(1)}, s32[1,32,64]{2,1,0:T(8,128)}, u32[]{:S(2)}) copy-start(s32[1,32,64]{2,1,0:T(8,128)} %param.19) | copy-start | bytes 24580
  64.4 24.9 %copy-start.3 = (f32[1,2,32,64]{3,2,1,0:T(8,128)S(1)}, f32[1,2,32,64]{3,2,1,0:T(8,128)}, u32[]{:S(2)}) copy-start(f32[1,2,32,64]{3,2,1,0:T(8,128)} %param.18) | copy-start | bytes 49156
  125.1 42.6 %copy-start = (f32[8,64,384]{2,1,0:T(8,128)S(1)}, f32[8,64,384]{2,1,0:T(8,128)}, u32[]{:S(2)}) copy-start(f32[8,64,384]{2,1,0:T(8,128)} %refs_2_.1) | copy-start | bytes 2359300
  125.1 42.7 %copy-start.1 = (f32[8,64,384]{2,1,0:T(8,128)S(1)}, f32[8,64,384]{2,1,0:T(8,128)}, u32[]{:S(2)}) copy-start(f32[8,64,384]{2,1,0:T(8,128)} %param.13) | copy-start | bytes 2359300
  125.1 42.7 %copy-start.2 = (f32[8,64,384]{2,1,0:T(8,128)S(1)}, f32[8,64,384]{2,1,0:T(8,128)}, u32[]{:S(2)}) copy-start(f32[8,64,384]{2,1,0:T(8,128)} %param.12) | copy-start | bytes 2359300
